TPU v7x, 32 devices: a whole 2x2x4 slice. The times are simulated.
32 devices in a mesh: ctx: 8 (over y, x, core), fsdp: 4 (over z).
Axes of the slice: x: 2, y: 2, z: 4, core: 2. Of those that a mesh axis runs over, the one named last changes fastest.
Arguments:
- block_input: bfloat16 [2, 4, 512, 1536], P(None, 'fsdp', 'ctx'), may hold values from -6 to 6
- positions: int32 [2, 4, 512], P(None, 'fsdp', 'ctx'), may hold values from 0 to 511, as said below
- segments: int32 [2, 4, 512], P(None, 'fsdp', 'ctx'), may hold values from 0 to 2, as said below
- out_cotangent: bfloat16 [2, 4, 512, 1536], P(None, 'fsdp', 'ctx'), may hold values from -6 to 6
- attn_gain: bfloat16 [1536], P(('ctx', 'fsdp')), may hold values from 0.5 to 1.5
- w_query: bfloat16 [1536, 1536], P(('ctx', 'fsdp')), may hold values from -0.15625 to 0.15625
- w_key: bfloat16 [1536, 768], P(('ctx', 'fsdp')), may hold values from -0.15625 to 0.15625
- w_value: bfloat16 [1536, 768], P(('ctx', 'fsdp')), may hold values from -0.15625 to 0.15625
- w_out: bfloat16 [1536, 1536], P(('ctx', 'fsdp')), may hold values from -0.625 to 0.625
- mlp_gain: bfloat16 [1536], P(('ctx', 'fsdp')), may hold values from 0.5 to 1.5
- w_gate: bfloat16 [1536, 4096], P(('ctx', 'fsdp')), may hold values from -0.15625 to 0.15625
- w_up: bfloat16 [1536, 4096], P(('ctx', 'fsdp')), may hold values from -0.15625 to 0.15625
- w_down: bfloat16 [4096, 1536], P(('ctx', 'fsdp')), may hold values from -0.09375 to 0.09375
Outputs:
- block_output: bfloat16 [2, 4, 512, 1536], P(None, 'fsdp', 'ctx')
- input_grad: bfloat16 [2, 4, 512, 1536], P(None, 'fsdp', 'ctx')
- grad_attn_gain: float32 [1536], P(('ctx', 'fsdp'))
- grad_query: float32 [1536, 1536], P(('ctx', 'fsdp'))
- grad_key: float32 [1536, 768], P(('ctx', 'fsdp'))
- grad_value: float32 [1536, 768], P(('ctx', 'fsdp'))
- grad_out: float32 [1536, 1536], P(('ctx', 'fsdp'))
- grad_mlp_gain: float32 [1536], P(('ctx', 'fsdp'))
- grad_gate: float32 [1536, 4096], P(('ctx', 'fsdp'))
- grad_up: float32 [1536, 4096], P(('ctx', 'fsdp'))
- grad_down: float32 [4096, 1536], P(('ctx', 'fsdp'))
Inputs may be any that keep to these rules, and one draw needn't show every extreme that they name: In each sequence every position appears once; the 64 tokens of one index of ctx are 32 consecutive positions starting at c * 32 followed by 32 starting at (15 - c) * 32, for some c below 8. `segments`: ordered by position, segment ids start at 0 and rise by one at each new document, except that the last document of each sequence has the id 512 // 200; every document has 200 to 2000 positions except that the last of a sequence may have fewer.
All inputs are finite; a program needn't handle non-finite values.
Results may differ from a plain program's by a relative error of at most 0.02.
Values may be sent and summed in bfloat16 or wider, within the bound.
No kernel may reach another device: no remote copies, remote signals or barrier semaphores. Data moves between devices by JAX's collectives and lax.ppermute only.
A program may use at most 192 MiB of HBM per device.

v0:
```python
import math

import jax
import jax.numpy as jnp
from jax import lax
from jax.sharding import PartitionSpec as P

HEADS = 16
KV_HEADS = 8
HEAD = 96


epsilon = 1e-05
theta_base = 100000.0


def rope_tables(position_ids, head_size):
    half_size = head_size // 2
    ladder = jnp.arange(half_size).astype(jnp.float32) * (2.0 / head_size)
    inverse = jnp.exp(-math.log(theta_base) * ladder)
    angles = position_ids.astype(jnp.float32)[:, None] * inverse[None, :]
    return (jnp.cos(angles)[:, None, :], jnp.sin(angles)[:, None, :])


def rotate(vectors, cosine_part, sine_part):
    half_size = vectors.shape[-1] // 2
    first_half = vectors[..., :half_size]
    second_half = vectors[..., half_size:]
    return jnp.concatenate(
        [
            first_half * cosine_part - second_half * sine_part,
            second_half * cosine_part + first_half * sine_part,
        ],
        axis=-1,
    )


def unrotate(grads_in, cosine_part, sine_part):
    half_size = grads_in.shape[-1] // 2
    first_half = grads_in[..., :half_size]
    second_half = grads_in[..., half_size:]
    return jnp.concatenate(
        [
            first_half * cosine_part + second_half * sine_part,
            second_half * cosine_part - first_half * sine_part,
        ],
        axis=-1,
    )


def rms_scale(values_in):
    return lax.rsqrt(jnp.mean(values_in * values_in, axis=-1, keepdims=True) + epsilon)


def norm_back(grad_normed, normed, scale_rows):
    return scale_rows * (
        grad_normed - normed * jnp.mean(grad_normed * normed, axis=-1, keepdims=True)
    )


def left_product(left_side, right_side):
    return jnp.einsum("td,te->de", left_side, right_side, preferred_element_type=jnp.float32)


def back_product(grad_rows, weight_rows):
    return jnp.einsum("te,de->td", grad_rows, weight_rows, preferred_element_type=jnp.float32)


def add_lists(first_list, second_list):
    if first_list is None:
        return list(second_list)
    return [total_old + part_new for total_old, part_new in zip(first_list, second_list)]


def on_device(
    block_input,
    positions,
    segments,
    out_cotangent,
    attn_gain,
    w_query,
    w_key,
    w_value,
    w_out,
    mlp_gain,
    w_gate,
    w_up,
    w_down,
):
    micro_count = block_input.shape[0]
    tok_rows = block_input.shape[2]
    model_width = block_input.shape[3]
    kv_width = KV_HEADS * HEAD
    factor = HEAD ** (-0.5)
    ctx_count = lax.axis_size("ctx")
    fsdp_count = lax.axis_size("fsdp")
    fsdp_place = lax.axis_index("fsdp")
    key_pos, key_seg = (
        lax.all_gather(positions, "ctx", axis=2, tiled=True),
        lax.all_gather(segments, "ctx", axis=2, tiled=True),
    )
    seq_len = key_pos.shape[2]

    def column_group(rows_mat):
        row_count = rows_mat.shape[0]
        per_owner = rows_mat.shape[1] // (ctx_count * fsdp_count)
        shaped = rows_mat.reshape(row_count, ctx_count, fsdp_count, per_owner)
        picked = lax.dynamic_slice_in_dim(shaped, fsdp_place, 1, 2)
        return picked.reshape(row_count, ctx_count * per_owner)

    def fetch_attention():
        return (
            lax.all_gather(attn_gain, ("ctx", "fsdp"), axis=0, tiled=True),
            lax.all_gather(w_query, ("ctx", "fsdp"), axis=0, tiled=True),
            lax.all_gather(w_key, ("ctx", "fsdp"), axis=0, tiled=True),
            lax.all_gather(w_value, ("ctx", "fsdp"), axis=0, tiled=True),
            lax.all_gather(w_out, ("ctx", "fsdp"), axis=0, tiled=True),
        )

    def fetch_mlp():
        return (
            lax.all_gather(mlp_gain, ("ctx", "fsdp"), axis=0, tiled=True),
            lax.all_gather(w_gate, ("ctx", "fsdp"), axis=0, tiled=True),
            lax.all_gather(w_up, ("ctx", "fsdp"), axis=0, tiled=True),
            lax.all_gather(w_down, ("ctx", "fsdp"), axis=0, tiled=True),
        )

    attn_totals = [
        jnp.zeros(shard.shape, jnp.float32) for shard in (w_query, w_key, w_value, w_out)
    ]
    mlp_totals = [jnp.zeros(shard.shape, jnp.float32) for shard in (w_gate, w_up, w_down)]
    gain_one_total = jnp.zeros((model_width,), jnp.float32)
    gain_two_total = jnp.zeros((model_width,), jnp.float32)
    attn_full = None
    mlp_full = None
    output_list = []
    grad_list = []
    group_ids = jnp.arange(KV_HEADS)
    for micro_step in range(micro_count):
        residual = block_input[micro_step, 0].astype(jnp.float32)
        pos_rows = positions[micro_step, 0]
        seg_rows = segments[micro_step, 0]
        allowed = (seg_rows[:, None] == key_seg[micro_step, 0][None, :]) & (
            key_pos[micro_step, 0][None, :] <= pos_rows[:, None]
        )
        cosine_part, sine_part = rope_tables(pos_rows, HEAD)
        gain_one, query_w, key_w, value_w, out_w = fetch_attention()
        scale_one = rms_scale(residual)
        normed_one = residual * scale_one
        hidden_one = (normed_one * gain_one.astype(jnp.float32)).astype(jnp.bfloat16)
        query_pre = jnp.dot(hidden_one, query_w, preferred_element_type=jnp.float32)
        key_pre = jnp.dot(hidden_one, key_w, preferred_element_type=jnp.float32)
        value_rows = jnp.dot(hidden_one, value_w, preferred_element_type=jnp.float32).astype(
            jnp.bfloat16
        )
        query_rot = (
            rotate(query_pre.reshape(tok_rows, HEADS, HEAD), cosine_part, sine_part)
            .astype(jnp.bfloat16)
            .reshape(tok_rows, model_width)
        )
        key_rot = (
            rotate(key_pre.reshape(tok_rows, KV_HEADS, HEAD), cosine_part, sine_part)
            .astype(jnp.bfloat16)
            .reshape(tok_rows, kv_width)
        )
        every_key_row, every_value_row = (
            lax.all_gather(key_rot, "ctx", axis=0, tiled=True),
            lax.all_gather(value_rows, "ctx", axis=0, tiled=True),
        )

        def group_parts(kv_group):
            query_g = lax.dynamic_slice_in_dim(query_rot, kv_group * 2 * HEAD, 2 * HEAD, 1).reshape(
                tok_rows, 2, HEAD
            )
            key_g = lax.dynamic_slice_in_dim(every_key_row, kv_group * HEAD, HEAD, 1)
            value_g = lax.dynamic_slice_in_dim(every_value_row, kv_group * HEAD, HEAD, 1)
            scores = (
                jnp.einsum("trh,sh->rts", query_g, key_g, preferred_element_type=jnp.float32)
                * factor
            )
            scores = jnp.where(allowed[None], scores, -1e30)
            return (query_g, key_g, value_g, scores)

        def forward_group(kv_group):
            query_g, key_g, value_g, scores = group_parts(kv_group)
            row_max = jnp.max(scores, axis=-1, keepdims=True)
            raised = jnp.exp(scores - row_max)
            row_sum = jnp.sum(raised, axis=-1, keepdims=True)
            softmax_rows = (raised / row_sum).astype(jnp.bfloat16)
            mixed_values = jnp.einsum(
                "rts,sh->trh", softmax_rows, value_g, preferred_element_type=jnp.float32
            ).astype(jnp.bfloat16)
            return (mixed_values.reshape(tok_rows, 2 * HEAD), row_max + jnp.log(row_sum))

        group_outs, log_sums = lax.map(forward_group, group_ids)
        attended = jnp.transpose(group_outs, (1, 0, 2)).reshape(tok_rows, model_width)
        middle = residual + jnp.dot(attended, out_w, preferred_element_type=jnp.float32)
        gain_two, gate_w, up_w, down_w = fetch_mlp()
        scale_two = rms_scale(middle)
        normed_two = middle * scale_two
        hidden_two = (normed_two * gain_two.astype(jnp.float32)).astype(jnp.bfloat16)
        gate_rows = jnp.dot(hidden_two, gate_w, preferred_element_type=jnp.float32)
        up_rows = jnp.dot(hidden_two, up_w, preferred_element_type=jnp.float32)
        sigma = jax.nn.sigmoid(gate_rows)
        activated = (gate_rows * sigma * up_rows).astype(jnp.bfloat16)
        result = middle + jnp.dot(activated, down_w, preferred_element_type=jnp.float32)
        output_list.append(result.astype(jnp.bfloat16))
        gain_two, gate_w, up_w, down_w = fetch_mlp()
        grad_result = out_cotangent[micro_step, 0].astype(jnp.float32)
        grad_low = grad_result.astype(jnp.bfloat16)
        grad_act = back_product(grad_low, down_w)
        gate_grad_rows = (grad_act * up_rows * sigma * (1.0 + gate_rows * (1.0 - sigma))).astype(
            jnp.bfloat16
        )
        up_grad_rows = (grad_act * gate_rows * sigma).astype(jnp.bfloat16)
        grad_hidden_two = back_product(gate_grad_rows, gate_w) + back_product(up_grad_rows, up_w)
        gain_two_total = gain_two_total + jnp.sum(grad_hidden_two * normed_two, axis=0)
        grad_middle = grad_result + norm_back(
            grad_hidden_two * gain_two.astype(jnp.float32), normed_two, scale_two
        )
        hidden_two_all, activated_all, grad_low_all, gate_grad_all, up_grad_all = (
            lax.all_gather(hidden_two, "fsdp", axis=0, tiled=True),
            lax.all_gather(activated, "fsdp", axis=0, tiled=True),
            lax.all_gather(grad_low, "fsdp", axis=0, tiled=True),
            lax.all_gather(gate_grad_rows, "fsdp", axis=0, tiled=True),
            lax.all_gather(up_grad_rows, "fsdp", axis=0, tiled=True),
        )
        hidden_two_cols = column_group(hidden_two_all)
        gate_grad = left_product(hidden_two_cols, gate_grad_all)
        up_grad = left_product(hidden_two_cols, up_grad_all)
        down_grad = left_product(column_group(activated_all), grad_low_all)
        mlp_full = add_lists(mlp_full, (gate_grad, up_grad, down_grad))
        gain_one, query_w, key_w, value_w, out_w = fetch_attention()
        grad_branch = grad_middle.astype(jnp.bfloat16)
        grad_attended = back_product(grad_branch, out_w).astype(jnp.bfloat16)

        def backward_group(kv_group):
            query_g, key_g, value_g, scores = group_parts(kv_group)
            grad_g = lax.dynamic_slice_in_dim(
                grad_attended, kv_group * 2 * HEAD, 2 * HEAD, 1
            ).reshape(tok_rows, 2, HEAD)
            soft_full = jnp.exp(scores - log_sums[kv_group])
            soft_low = soft_full.astype(jnp.bfloat16)
            grad_soft = jnp.einsum(
                "trh,sh->rts", grad_g, value_g, preferred_element_type=jnp.float32
            )
            value_grad_g = jnp.einsum(
                "rts,trh->sh", soft_low, grad_g, preferred_element_type=jnp.float32
            )
            inner_rows = jnp.sum(soft_full * grad_soft, axis=-1, keepdims=True)
            grad_scores = (soft_full * (grad_soft - inner_rows)).astype(jnp.bfloat16)
            query_grad_g = (
                jnp.einsum("rts,sh->trh", grad_scores, key_g, preferred_element_type=jnp.float32)
                * factor
            )
            key_grad_g = (
                jnp.einsum("rts,trh->sh", grad_scores, query_g, preferred_element_type=jnp.float32)
                * factor
            )
            return (query_grad_g.reshape(tok_rows, 2 * HEAD), key_grad_g, value_grad_g)

        query_grads, key_grads, value_grads = lax.map(backward_group, group_ids)
        grad_query_rot = jnp.transpose(query_grads, (1, 0, 2)).reshape(tok_rows, HEADS, HEAD)
        grad_keys_all = jnp.transpose(key_grads, (1, 0, 2)).reshape(seq_len, kv_width)
        grad_values_all = jnp.transpose(value_grads, (1, 0, 2)).reshape(seq_len, kv_width)
        mine_keys, mine_values = (
            lax.psum_scatter(
                grad_keys_all.astype(jnp.bfloat16), "ctx", scatter_dimension=0, tiled=True
            ).astype(jnp.float32),
            lax.psum_scatter(
                grad_values_all.astype(jnp.bfloat16), "ctx", scatter_dimension=0, tiled=True
            ).astype(jnp.float32),
        )
        query_low = (
            unrotate(grad_query_rot, cosine_part, sine_part)
            .reshape(tok_rows, model_width)
            .astype(jnp.bfloat16)
        )
        key_low = (
            unrotate(mine_keys.reshape(tok_rows, KV_HEADS, HEAD), cosine_part, sine_part)
            .reshape(tok_rows, kv_width)
            .astype(jnp.bfloat16)
        )
        value_low = mine_values.astype(jnp.bfloat16)
        grad_hidden_one = (
            back_product(query_low, query_w)
            + back_product(key_low, key_w)
            + back_product(value_low, value_w)
        )
        gain_one_total = gain_one_total + jnp.sum(grad_hidden_one * normed_one, axis=0)
        grad_input = grad_middle + norm_back(
            grad_hidden_one * gain_one.astype(jnp.float32), normed_one, scale_one
        )
        grad_list.append(grad_input.astype(jnp.bfloat16))
        hidden_one_all, attended_all, branch_all, query_all, key_all, value_all = (
            lax.all_gather(hidden_one, "fsdp", axis=0, tiled=True),
            lax.all_gather(attended, "fsdp", axis=0, tiled=True),
            lax.all_gather(grad_branch, "fsdp", axis=0, tiled=True),
            lax.all_gather(query_low, "fsdp", axis=0, tiled=True),
            lax.all_gather(key_low, "fsdp", axis=0, tiled=True),
            lax.all_gather(value_low, "fsdp", axis=0, tiled=True),
        )
        hidden_one_cols = column_group(hidden_one_all)
        query_grad = left_product(hidden_one_cols, query_all)
        key_grad = left_product(hidden_one_cols, key_all)
        value_grad = left_product(hidden_one_cols, value_all)
        out_grad = left_product(column_group(attended_all), branch_all)
        attn_full = add_lists(attn_full, (query_grad, key_grad, value_grad, out_grad))
    mlp_totals = list(
        (
            lax.psum_scatter(
                mlp_full[0].astype(jnp.bfloat16), "ctx", scatter_dimension=0, tiled=True
            ).astype(jnp.float32),
            lax.psum_scatter(
                mlp_full[1].astype(jnp.bfloat16), "ctx", scatter_dimension=0, tiled=True
            ).astype(jnp.float32),
            lax.psum_scatter(
                mlp_full[2].astype(jnp.bfloat16), "ctx", scatter_dimension=0, tiled=True
            ).astype(jnp.float32),
        )
    )
    attn_totals = list(
        (
            lax.psum_scatter(
                attn_full[0].astype(jnp.bfloat16), "ctx", scatter_dimension=0, tiled=True
            ).astype(jnp.float32),
            lax.psum_scatter(
                attn_full[1].astype(jnp.bfloat16), "ctx", scatter_dimension=0, tiled=True
            ).astype(jnp.float32),
            lax.psum_scatter(
                attn_full[2].astype(jnp.bfloat16), "ctx", scatter_dimension=0, tiled=True
            ).astype(jnp.float32),
            lax.psum_scatter(
                attn_full[3].astype(jnp.bfloat16), "ctx", scatter_dimension=0, tiled=True
            ).astype(jnp.float32),
        )
    )
    gain_one_grad, gain_two_grad = (
        lax.psum_scatter(gain_one_total, ("ctx", "fsdp"), scatter_dimension=0, tiled=True),
        lax.psum_scatter(gain_two_total, ("ctx", "fsdp"), scatter_dimension=0, tiled=True),
    )
    block_output = jnp.stack(output_list)[:, None]
    input_grad = jnp.stack(grad_list)[:, None]
    return (
        block_output,
        input_grad,
        gain_one_grad,
        attn_totals[0],
        attn_totals[1],
        attn_totals[2],
        attn_totals[3],
        gain_two_grad,
        mlp_totals[0],
        mlp_totals[1],
        mlp_totals[2],
    )


def solution(mesh):
    return jax.shard_map(
        on_device,
        mesh=mesh,
        in_specs=(
            P(None, "fsdp", "ctx", None),
            P(None, "fsdp", "ctx"),
            P(None, "fsdp", "ctx"),
            P(None, "fsdp", "ctx", None),
            P(("ctx", "fsdp")),
            P(("ctx", "fsdp"), None),
            P(("ctx", "fsdp"), None),
            P(("ctx", "fsdp"), None),
            P(("ctx", "fsdp"), None),
            P(("ctx", "fsdp")),
            P(("ctx", "fsdp"), None),
            P(("ctx", "fsdp"), None),
            P(("ctx", "fsdp"), None),
        ),
        out_specs=(
            P(None, "fsdp", "ctx", None),
            P(None, "fsdp", "ctx", None),
            P(("ctx", "fsdp")),
            P(("ctx", "fsdp"), None),
            P(("ctx", "fsdp"), None),
            P(("ctx", "fsdp"), None),
            P(("ctx", "fsdp"), None),
            P(("ctx", "fsdp")),
            P(("ctx", "fsdp"), None),
            P(("ctx", "fsdp"), None),
            P(("ctx", "fsdp"), None),
        ),
        check_vma=False,
    )
```

profile of v0, /device:TPU:0, one launch (start us, length us, event | category | flops | bytes accessed | tf_op | source)
XLA Modules:
  0.0 1601.5 jit_solution(5657085253578849542)
XLA Ops:
  17.6 42.2 %all-reduce.5 = (bf16[1536]{0:T(1024)(128)(2,1)S(1)}, bf16[1536]{0:T(1024)(128)(2,1)S(1)}) all-reduce(bf16[1536]{0:T(1024)(128)(2,1)S(1)} %dynamic-update-slice, bf16[1536]{0:T(1024)(128)(2,1)S(1)} %dynamic-update-slice.1), channel_id=1, replica_groups=mesh['ctx'=8,'fsdp'=4] {'ctx','fsdp'}, use_global_device_ids=true, to_apply=%add | all-reduce | flops 3072 | bytes 12288
  61.0 10.3 all_gather.141
  71.3 19.5 %slice_reduce_fusion.3 = (s32[512]{0:T(512)}, s32[512]{0:T(512)}) fusion(s32[2,1,512]{0,1,2:T(1,128)S(1)} %all_gather.141), kind=kLoop, calls=%fused_computation.213 | loop fusion | bytes 8192 | tf_op jit(solution)/shard_map/slice | solution.py:143
  90.8 8.5 all_gather.142
  99.4 19.7 %slice_reduce_fusion.2 = (s32[512]{0:T(512)}, s32[512]{0:T(512)}) fusion(s32[2,1,512]{0,1,2:T(1,128)S(1)} %all_gather.142), kind=kLoop, calls=%fused_computation.212 | loop fusion | bytes 8192 | tf_op jit(solution)/shard_map/slice | solution.py:144
  131.9 11.3 all_gather.151
  146.1 10.7 all_gather.152
  160.6 10.0 all_gather.140
  171.4 13.0 all_gather.144
  184.7 11.7 all-gather.20.cloned.1.call-done
  208.2 39.0 %while.65 = (s32[]{:T(128)}, bf16[8,64,192]{2,1,0:T(8,128)(2,1)S(1)}, f32[8,2,64,1]{2,1,3,0:T(2,128)S(1)}, s32[8]{0:T(128)S(1)}, bf16[512,768]{0,1:T(8,128)(2,1)...) while((s32[]{:T(128)}, ...), condition=%wide.region_10.11_spmd.clone, body=%wide.region_7.10_spmd.clone.sunk | while | flops 25800584 | bytes 1370401 | solution.py:195
  252.9 24.9 %while.64 = (s32[]{:T(128)}, bf16[8,64,192]{2,1,0:T(8,128)(2,1)S(1)}, f32[8,2,64,1]{2,1,3,0:T(2,128)S(1)}, s32[8]{0:T(128)S(1)}, bf16[512,768]{0,1:T(8,128)(2,1)...) while((s32[]{:T(128)}, ...), condition=%wide.region_4.5_spmd.clone, body=%wide.region_1.4_spmd.clone.sunk | while | flops 25800584 | bytes 1379617 | solution.py:195
  284.0 73.9 %all-gather.24.cloned.1.call-done = bf16[1536,4096]{1,0:T(8,128)(2,1)} async-done(((bf16[48,4096]{1,0:T(8,128)(2,1)}), bf16[1536,4096]{1,0:T(8,128)(2,1)}) %all-gather.24.cloned.1.call-update) | async-done | bytes 12582928 | tf_op jit(solution)/shard_map/all_gather | solution.py:123
  357.9 7.9 fusion.150
  365.7 88.7 %all-gather.26.cloned.1.call-done = bf16[1536,4096]{1,0:T(8,128)(2,1)} async-done(((bf16[48,4096]{1,0:T(8,128)(2,1)}), bf16[1536,4096]{1,0:T(8,128)(2,1)}) %all-gather.26.cloned.1.call-update) | async-done | bytes 12582928 | tf_op jit(solution)/shard_map/all_gather | solution.py:124
  462.3 88.9 %all-gather.28.cloned.1.call-done = bf16[4096,1536]{1,0:T(8,128)(2,1)} async-done(((bf16[128,1536]{1,0:T(8,128)(2,1)}), bf16[4096,1536]{1,0:T(8,128)(2,1)}) %all-gather.28.cloned.1.call-update) | async-done | bytes 12582928 | tf_op jit(solution)/shard_map/all_gather | solution.py:125
  551.2 9.8 multiply_convert_fusion.4
  560.9 8.9 fusion.154
  569.9 10.1 multiply_reduce_fusion.3
  580.6 8.1 fusion.152
  588.7 8.1 fusion.153
  603.6 9.5 fusion.156
  613.2 9.7 multiply_reduce_fusion.2
  628.0 88.3 %while.67 = (s32[]{:T(128)}, f32[8,64,192]{2,1,0:T(8,128)S(1)}, bf16[8,512,96]{1,2,0:T(8,128)(2,1)}, bf16[8,512,96]{1,2,0:T(8,128)(2,1)}, s32[8]{0:T(128)S(1)}, ...) while((s32[]{:T(128)}, f32[8,64,192]{2,1,0:T(8,128)S(1)}, ...), condition=%wide.region_22.23_spmd.clone, body=%wide.region_20.22_spmd.clone.sunk | while | flops 63664012 | bytes 3399023 | solution.py:262
  724.7 88.1 %while.66 = (s32[]{:T(128)}, f32[8,64,192]{2,1,0:T(8,128)S(1)}, bf16[8,512,96]{1,2,0:T(8,128)(2,1)}, bf16[8,512,96]{1,2,0:T(8,128)(2,1)}, s32[8]{0:T(128)S(1)}, ...) while((s32[]{:T(128)}, f32[8,64,192]{2,1,0:T(8,128)S(1)}, ...), condition=%wide.region_15.16_spmd.clone, body=%wide.region_13.15_spmd.clone.sunk | while | flops 63664012 | bytes 3399023 | solution.py:262
  823.2 18.7 %all_gather.153 = bf16[256,1536]{1,0:T(8,128)(2,1)} all-gather(bf16[64,1536]{1,0:T(8,128)(2,1)S(1)} %copy-done.41), channel_id=1, replica_groups=mesh['ctx'=8,'fsdp'=4] {'fsdp'}, dimensions={0}, use_global_device_ids=true | all-gather | bytes 983040 | tf_op jit(solution)/shard_map/all_gather | solution.py:296
  844.1 18.8 %all_gather.155 = bf16[256,1536]{1,0:T(8,128)(2,1)} all-gather(bf16[64,1536]{1,0:T(8,128)(2,1)S(1)} %copy-done.40), channel_id=1, replica_groups=mesh['ctx'=8,'fsdp'=4] {'fsdp'}, dimensions={0}, use_global_device_ids=true | all-gather | bytes 983040 | tf_op jit(solution)/shard_map/all_gather | solution.py:296
  867.2 18.2 %all_gather.161 = bf16[256,1536]{1,0:T(8,128)(2,1)} all-gather(bf16[64,1536]{1,0:T(8,128)(2,1)S(1)} %copy-done.31), channel_id=1, replica_groups=mesh['ctx'=8,'fsdp'=4] {'fsdp'}, dimensions={0}, use_global_device_ids=true | all-gather | bytes 983040 | tf_op jit(solution)/shard_map/all_gather | solution.py:297
  887.8 17.5 %all_gather.163 = bf16[256,1536]{1,0:T(8,128)(2,1)} all-gather(bf16[64,1536]{1,0:T(8,128)(2,1)S(1)} %copy-done.29), channel_id=1, replica_groups=mesh['ctx'=8,'fsdp'=4] {'fsdp'}, dimensions={0}, use_global_device_ids=true | all-gather | bytes 983040 | tf_op jit(solution)/shard_map/all_gather | solution.py:297
  905.3 16.4 %all_gather.165 = bf16[256,1536]{1,0:T(8,128)(2,1)} all-gather(bf16[64,1536]{1,0:T(8,128)(2,1)S(1)} %copy-done.20), channel_id=1, replica_groups=mesh['ctx'=8,'fsdp'=4] {'fsdp'}, dimensions={0}, use_global_device_ids=true | all-gather | bytes 983040 | tf_op jit(solution)/shard_map/all_gather | solution.py:222
  929.7 28.7 %all_gather.154 = bf16[256,1536]{1,0:T(8,128)(2,1)S(1)} all-gather(bf16[64,1536]{1,0:T(8,128)(2,1)S(1)} %convert_element_type.344), channel_id=1, replica_groups=mesh['ctx'=8,'fsdp'=4] {'fsdp'}, dimensions={0}, use_global_device_ids=true | all-gather | bytes 983040 | tf_op jit(solution)/shard_map/all_gather | solution.py:299
  958.4 28.6 %all_gather.156 = bf16[256,1536]{1,0:T(8,128)(2,1)S(1)} all-gather(bf16[64,1536]{1,0:T(8,128)(2,1)S(1)} %convert_element_type.358), channel_id=1, replica_groups=mesh['ctx'=8,'fsdp'=4] {'fsdp'}, dimensions={0}, use_global_device_ids=true | all-gather | bytes 983040 | tf_op jit(solution)/shard_map/all_gather | solution.py:299
  997.3 29.8 %all_gather.167 = bf16[256,1536]{1,0:T(8,128)(2,1)} all-gather(bf16[64,1536]{1,0:T(8,128)(2,1)S(1)} %copy-done.18), channel_id=1, replica_groups=mesh['ctx'=8,'fsdp'=4] {'fsdp'}, dimensions={0}, use_global_device_ids=true | all-gather | bytes 983040 | tf_op jit(solution)/shard_map/all_gather | solution.py:222
  1029.4 27.9 %all_gather.162 = bf16[256,1536]{1,0:T(8,128)(2,1)S(1)} all-gather(bf16[64,1536]{1,0:T(8,128)(2,1)S(1)} %copy-done.35), channel_id=1, replica_groups=mesh['ctx'=8,'fsdp'=4] {'fsdp'}, dimensions={0}, use_global_device_ids=true | all-gather | bytes 983040 | tf_op jit(solution)/shard_map/all_gather | solution.py:298
  1057.4 21.4 %all_gather.164 = bf16[256,1536]{1,0:T(8,128)(2,1)S(1)} all-gather(bf16[64,1536]{1,0:T(8,128)(2,1)S(1)} %copy-done.33), channel_id=1, replica_groups=mesh['ctx'=8,'fsdp'=4] {'fsdp'}, dimensions={0}, use_global_device_ids=true | all-gather | bytes 983040 | tf_op jit(solution)/shard_map/all_gather | solution.py:298
  1085.1 20.8 %all_gather.157 = bf16[256,768]{1,0:T(8,128)(2,1)S(1)} all-gather(bf16[64,768]{1,0:T(8,128)(2,1)S(1)} %convert_element_type.348), channel_id=1, replica_groups=mesh['ctx'=8,'fsdp'=4] {'fsdp'}, dimensions={0}, use_global_device_ids=true | all-gather | bytes 491520 | tf_op jit(solution)/shard_map/all_gather | solution.py:300
  1105.9 18.3 %all_gather.158 = bf16[256,768]{1,0:T(8,128)(2,1)S(1)} all-gather(bf16[64,768]{1,0:T(8,128)(2,1)S(1)} %convert_element_type.362), channel_id=1, replica_groups=mesh['ctx'=8,'fsdp'=4] {'fsdp'}, dimensions={0}, use_global_device_ids=true | all-gather | bytes 491520 | tf_op jit(solution)/shard_map/all_gather | solution.py:300
  1126.7 17.1 %all_gather.159 = bf16[256,768]{1,0:T(8,128)(2,1)S(1)} all-gather(bf16[64,768]{1,0:T(8,128)(2,1)} %reduce-scatter.34.cloned.1.call-done), channel_id=1, replica_groups=mesh['ctx'=8,'fsdp'=4] {'fsdp'}, dimensions={0}, use_global_device_ids=true | all-gather | bytes 491520 | tf_op jit(solution)/shard_map/all_gather | solution.py:301
  1143.8 17.5 %all_gather.160 = bf16[256,768]{1,0:T(8,128)(2,1)S(1)} all-gather(bf16[64,768]{1,0:T(8,128)(2,1)} %reduce-scatter.36.cloned.1.call-done), channel_id=1, replica_groups=mesh['ctx'=8,'fsdp'=4] {'fsdp'}, dimensions={0}, use_global_device_ids=true | all-gather | bytes 491520 | tf_op jit(solution)/shard_map/all_gather | solution.py:301
  1186.1 28.9 %all-gather = bf16[1,1,256,1536]{3,2,1,0:T(8,128)(2,1)} all-gather(bf16[1,1,64,1536]{3,2,1,0:T(8,128)(2,1)S(1)} %get-tuple-element.1030), channel_id=2, replica_groups=mesh['ctx'=8,'fsdp'=4] {'fsdp'}, dimensions={2}, use_global_device_ids=true | all-gather | bytes 983040 | tf_op jit(solution)/shard_map/all_gather | solution.py:224
  1215.0 28.4 %all-gather.1 = bf16[1,1,256,1536]{3,2,1,0:T(8,128)(2,1)} all-gather(bf16[1,1,64,1536]{3,2,1,0:T(8,128)(2,1)S(1)} %get-tuple-element.1029), channel_id=3, replica_groups=mesh['ctx'=8,'fsdp'=4] {'fsdp'}, dimensions={2}, use_global_device_ids=true | all-gather | bytes 983040 | tf_op jit(solution)/shard_map/all_gather | solution.py:224
  1254.2 35.3 %all-gather.40.cloned.1.call-done = bf16[256,4096]{1,0:T(8,128)(2,1)} async-done(((bf16[64,4096]{1,0:T(8,128)(2,1)}), bf16[256,4096]{1,0:T(8,128)(2,1)}) %all-gather.40.cloned.1.call-update) | async-done | bytes 2097168 | tf_op jit(solution)/shard_map/all_gather | solution.py:223
  1327.0 39.5 %all-reduce.4 = (f32[1536]{0:T(1024)S(1)}, f32[1536]{0:T(1024)S(1)}) all-reduce(f32[1536]{0:T(1024)S(1)} %add.329, f32[1536]{0:T(1024)S(1)} %add.335), channel_id=8, replica_groups=mesh['ctx'=8,'fsdp'=4] {'ctx','fsdp'}, use_global_device_ids=true, to_apply=%region_28.29.clone | all-reduce | flops 3072 | bytes 24576
  1373.3 32.8 %reduce-scatter.22.cloned.1.call-done = bf16[48,768]{1,0:T(8,128)(2,1)} async-done(((bf16[384,768]{1,0:T(8,128)(2,1)}), bf16[48,768]{1,0:T(8,128)(2,1)}) %reduce-scatter.22.cloned.1.call-update) | async-done | bytes 73744 | tf_op jit(solution)/shard_map/reduce_scatter | solution.py:327
  1407.6 36.5 %reduce-scatter.24.cloned.1.call-done = bf16[48,768]{1,0:T(8,128)(2,1)} async-done(((bf16[384,768]{1,0:T(8,128)(2,1)}), bf16[48,768]{1,0:T(8,128)(2,1)}) %reduce-scatter.24.cloned.1.call-update) | async-done | bytes 73744 | tf_op jit(solution)/shard_map/reduce_scatter | solution.py:330
  1445.7 47.9 %reduce-scatter.28.cloned.1.call-done = bf16[48,4096]{1,0:T(8,128)(2,1)} async-done(((bf16[384,4096]{1,0:T(8,128)(2,1)}), bf16[48,4096]{1,0:T(8,128)(2,1)}) %reduce-scatter.28.cloned.1.call-update) | async-done | bytes 393232 | tf_op jit(solution)/shard_map/reduce_scatter | solution.py:311
  1495.5 47.6 %reduce-scatter.30.cloned.1.call-done = bf16[48,4096]{1,0:T(8,128)(2,1)} async-done(((bf16[384,4096]{1,0:T(8,128)(2,1)}), bf16[48,4096]{1,0:T(8,128)(2,1)}) %reduce-scatter.30.cloned.1.call-update) | async-done | bytes 393232 | tf_op jit(solution)/shard_map/reduce_scatter | solution.py:314
  1545.0 47.4 %reduce-scatter.32.cloned.1.call-done = bf16[128,1536]{1,0:T(8,128)(2,1)} async-done(((bf16[1024,1536]{1,0:T(8,128)(2,1)}), bf16[128,1536]{1,0:T(8,128)(2,1)}) %reduce-scatter.32.cloned.1.call-update) | async-done | bytes 393232 | tf_op jit(solution)/shard_map/reduce_scatter | solution.py:317
  (832 shorter events, 385.7 us)
Async XLA Ops:
  7.2 117.1 %copy-start.4 = (bf16[2,1,64,1536]{3,2,1,0:T(8,128)(2,1)S(1)}, bf16[2,1,64,1536]{3,2,1,0:T(8,128)(2,1)}, u32[]{:S(2)}) copy-start(bf16[2,1,64,1536]{3,2,1,0:T(8,128)(2,1)} %param.21) | copy-start | bytes 1179652
  7.2 114.2 %all-gather.18.cloned.1.call-start = ((), (), s32[]{:S(2)}) async-start(), calls=%async_computation.12 | async-start | bytes 2433024 | tf_op jit(solution)/shard_map/all_gather | solution.py:115
  7.9 121.6 %all-gather.16.cloned.1.call-start = ((), (), s32[]{:S(2)}) async-start(), calls=%async_computation.11 | async-start | bytes 2433024 | tf_op jit(solution)/shard_map/all_gather | solution.py:116
  8.7 187.7 %all-gather.20.cloned.1.call-start = ((), (), s32[]{:S(2)}) async-start(), calls=%async_computation.13 | async-start | bytes 4866048 | tf_op jit(solution)/shard_map/all_gather | solution.py:114
  9.4 269.5 %all-gather.22.cloned.1.call-start = ((), (), s32[]{:S(2)}) async-start(), calls=%async_computation.14 | async-start | bytes 4866048 | tf_op jit(solution)/shard_map/all_gather | solution.py:117
  10.0 347.9 %all-gather.24.cloned.1.call-start = ((), (), s32[]{:S(2)}) async-start(), calls=%async_computation.15 | async-start | bytes 12976128 | tf_op jit(solution)/shard_map/all_gather | solution.py:123
  10.6 443.9 %all-gather.26.cloned.1.call-start = ((), (), s32[]{:S(2)}) async-start(), calls=%async_computation.16 | async-start | bytes 12976128 | tf_op jit(solution)/shard_map/all_gather | solution.py:124
  11.1 540.0 %all-gather.28.cloned.1.call-start = ((), (), s32[]{:S(2)}) async-start(), calls=%async_computation.17 | async-start | bytes 12976128 | tf_op jit(solution)/shard_map/all_gather | solution.py:125
  11.9 1069.9 %reduce-scatter.18.cloned.1.call-start = ((), (), s32[]{:S(2)}) async-start(), calls=%async_computation.19 | async-start | bytes 884736 | tf_op jit(solution)/shard_map/reduce_scatter | solution.py:267
  59.8 187.8 %copy-start.46 = (f32[1536]{0:T(1024)}, f32[1536]{0:T(1024)S(1)}, u32[]{:S(2)}) copy-start(f32[1536]{0:T(1024)S(1)} %convert_element_type.312) | copy-start | bytes 18436
  119.1 450.7 %copy-start.48 = (f32[1536]{0:T(1024)}, f32[1536]{0:T(1024)S(1)}, u32[]{:S(2)}) copy-start(f32[1536]{0:T(1024)S(1)} %convert_element_type.322) | copy-start | bytes 18436
  121.4 85.8 %copy-start.44 = (f32[64,48]{1,0:T(8,128)}, f32[64,48]{1,0:T(8,128)S(1)}, u32[]{:S(2)}) copy-start(f32[64,48]{1,0:T(8,128)S(1)} %get-tuple-element.1051) | copy-start | bytes 36868
  282.4 287.4 %copy-start.7 = (f32[64,1536]{1,0:T(8,128)}, f32[64,1536]{1,0:T(8,128)S(1)}, u32[]{:S(2)}) copy-start(f32[64,1536]{1,0:T(8,128)S(1)} %get-tuple-element.1053) | copy-start | bytes 1179652
  282.7 287.1 %copy-start.81 = (f32[64]{0:T(128)}, f32[64]{0:T(128)S(1)}, u32[]{:S(2)}) copy-start(f32[64]{0:T(128)S(1)} %add_rsqrt_fusion.2) | copy-start | bytes 772
  283.8 286.0 %copy-start.5 = (f32[64,1536]{1,0:T(8,128)}, f32[64,1536]{1,0:T(8,128)S(1)}, u32[]{:S(2)}) copy-start(f32[64,1536]{1,0:T(8,128)S(1)} %get-tuple-element.1055) | copy-start | bytes 1179652
  283.8 286.0 %copy-start.78 = (f32[64]{0:T(128)}, f32[64]{0:T(128)S(1)}, u32[]{:S(2)}) copy-start(f32[64]{0:T(128)S(1)} %add_rsqrt_fusion) | copy-start | bytes 772
  284.0 170.5 %copy-start.19 = (bf16[64,1536]{1,0:T(8,128)(2,1)}, bf16[64,1536]{1,0:T(8,128)(2,1)S(1)}, u32[]{:S(2)}) copy-start(bf16[64,1536]{1,0:T(8,128)(2,1)S(1)} %multiply_convert_fusion.9) | copy-start | bytes 589828
  365.7 185.4 %copy-start.12 = (bf16[2,1,64,1536]{3,2,1,0:T(8,128)(2,1)S(1)}, bf16[2,1,64,1536]{3,2,1,0:T(8,128)(2,1)}, u32[]{:S(2)}) copy-start(bf16[2,1,64,1536]{3,2,1,0:T(8,128)(2,1)} %param.24) | copy-start | bytes 1179652
  628.0 90.9 %copy-start.34 = (bf16[64,1536]{1,0:T(8,128)(2,1)S(1)}, bf16[64,1536]{1,0:T(8,128)(2,1)}, u32[]{:S(2)}) copy-start(bf16[64,1536]{1,0:T(8,128)(2,1)} %get-tuple-element.1025) | copy-start | bytes 589828
  718.8 364.7 %reduce-scatter.16.cloned.1.call-start = ((), (), s32[]{:S(2)}) async-start(), calls=%async_computation.18 | async-start | bytes 884736 | tf_op jit(solution)/shard_map/reduce_scatter | solution.py:267
  815.2 311.5 %reduce-scatter.34.cloned.1.call-start = ((), (), s32[]{:S(2)}) async-start(), calls=%async_computation.33 | async-start | bytes 884736
  817.7 326.1 %reduce-scatter.36.cloned.1.call-start = ((), (), s32[]{:S(2)}) async-start(), calls=%async_computation.34 | async-start | bytes 884736
  820.0 47.2 %copy-start.31 = (bf16[64,1536]{1,0:T(8,128)(2,1)S(1)}, bf16[64,1536]{1,0:T(8,128)(2,1)}, u32[]{:S(2)}) copy-start(bf16[64,1536]{1,0:T(8,128)(2,1)} %copy-done.30) | copy-start | bytes 589828
  820.0 342.8 %all-gather.30.cloned.1.call-start = ((), (), s32[]{:S(2)}) async-start(), calls=%async_computation.24 | async-start | bytes 2621440 | tf_op jit(solution)/shard_map/all_gather | solution.py:225
  820.6 347.4 %all-gather.32.cloned.1.call-start = ((), (), s32[]{:S(2)}) async-start(), calls=%async_computation.25 | async-start | bytes 2621440 | tf_op jit(solution)/shard_map/all_gather | solution.py:225
  821.4 352.9 %all-gather.34.cloned.1.call-start = ((), (), s32[]{:S(2)}) async-start(), calls=%async_computation.27 | async-start | bytes 2621440 | tf_op jit(solution)/shard_map/all_gather | solution.py:226
  821.9 357.5 %all-gather.36.cloned.1.call-start = ((), (), s32[]{:S(2)}) async-start(), calls=%async_computation.28 | async-start | bytes 2621440 | tf_op jit(solution)/shard_map/all_gather | solution.py:226
  822.5 421.3 %all-gather.38.cloned.1.call-start = ((), (), s32[]{:S(2)}) async-start(), calls=%async_computation.30 | async-start | bytes 2621440 | tf_op jit(solution)/shard_map/all_gather | solution.py:223
  822.6 65.2 %copy-start.29 = (bf16[64,1536]{1,0:T(8,128)(2,1)S(1)}, bf16[64,1536]{1,0:T(8,128)(2,1)}, u32[]{:S(2)}) copy-start(bf16[64,1536]{1,0:T(8,128)(2,1)} %copy-done.28) | copy-start | bytes 589828
  823.1 466.3 %all-gather.40.cloned.1.call-start = ((), (), s32[]{:S(2)}) async-start(), calls=%async_computation.31 | async-start | bytes 2621440 | tf_op jit(solution)/shard_map/all_gather | solution.py:223
  841.8 63.5 %copy-start.20 = (bf16[64,1536]{1,0:T(8,128)(2,1)S(1)}, bf16[64,1536]{1,0:T(8,128)(2,1)}, u32[]{:S(2)}) copy-start(bf16[64,1536]{1,0:T(8,128)(2,1)} %copy-done.19) | copy-start | bytes 589828
  867.1 58.1 %copy-start.45 = (f32[64,48]{1,0:T(8,128)S(1)}, f32[64,48]{1,0:T(8,128)}, u32[]{:S(2)}) copy-start(f32[64,48]{1,0:T(8,128)} %copy-done.44) | copy-start | bytes 36868
  867.2 502.9 %reduce-scatter.20.cloned.1.call-start = ((), (), s32[]{:S(2)}) async-start(), calls=%async_computation.20 | async-start | bytes 1327104 | tf_op jit(solution)/shard_map/reduce_scatter | solution.py:324
  926.2 60.9 %copy-start.36 = (bf16[64,1536]{1,0:T(8,128)(2,1)}, bf16[64,1536]{1,0:T(8,128)(2,1)S(1)}, u32[]{:S(2)}) copy-start(bf16[64,1536]{1,0:T(8,128)(2,1)S(1)} %convert_element_type.358) | copy-start | bytes 589828
  929.7 57.9 %copy-start.38 = (bf16[64,1536]{1,0:T(8,128)(2,1)}, bf16[64,1536]{1,0:T(8,128)(2,1)S(1)}, u32[]{:S(2)}) copy-start(bf16[64,1536]{1,0:T(8,128)(2,1)S(1)} %convert_element_type.344) | copy-start | bytes 589828
  989.0 68.4 %copy-start.33 = (bf16[64,1536]{1,0:T(8,128)(2,1)S(1)}, bf16[64,1536]{1,0:T(8,128)(2,1)}, u32[]{:S(2)}) copy-start(bf16[64,1536]{1,0:T(8,128)(2,1)} %copy-done.32) | copy-start | bytes 589828
  989.0 382.6 %reduce-scatter.26.cloned.1.call-start = ((), (), s32[]{:S(2)}) async-start(), calls=%async_computation.23 | async-start | bytes 1327104 | tf_op jit(solution)/shard_map/reduce_scatter | solution.py:333
  1081.7 324.3 %reduce-scatter.22.cloned.1.call-start = ((), (), s32[]{:S(2)}) async-start(), calls=%async_computation.21 | async-start | bytes 663552 | tf_op jit(solution)/shard_map/reduce_scatter | solution.py:327
  1125.7 318.4 %reduce-scatter.24.cloned.1.call-start = ((), (), s32[]{:S(2)}) async-start(), calls=%async_computation.22 | async-start | bytes 663552 | tf_op jit(solution)/shard_map/reduce_scatter | solution.py:330
  1162.8 330.8 %reduce-scatter.28.cloned.1.call-start = ((), (), s32[]{:S(2)}) async-start(), calls=%async_computation.26 | async-start | bytes 3538944 | tf_op jit(solution)/shard_map/reduce_scatter | solution.py:311
  1174.2 368.9 %reduce-scatter.30.cloned.1.call-start = ((), (), s32[]{:S(2)}) async-start(), calls=%async_computation.29 | async-start | bytes 3538944 | tf_op jit(solution)/shard_map/reduce_scatter | solution.py:314
  1186.0 406.4 %reduce-scatter.32.cloned.1.call-start = ((), (), s32[]{:S(2)}) async-start(), calls=%async_computation.32 | async-start | bytes 3538944 | tf_op jit(solution)/shard_map/reduce_scatter | solution.py:317
  1323.5 44.1 %copy-start.22 = (f32[64,1536]{1,0:T(8,128)S(1)}, f32[64,1536]{1,0:T(8,128)}, u32[]{:S(2)}) copy-start(f32[64,1536]{1,0:T(8,128)} %copy-done.21) | copy-start | bytes 1179652
  1323.5 44.1 %copy-start.80 = (f32[64]{0:T(128)S(1)}, f32[64]{0:T(128)}, u32[]{:S(2)}) copy-start(f32[64]{0:T(128)} %copy-done.78) | copy-start | bytes 772
  1323.5 44.1 %copy-start.87 = (f32[64]{0:T(128)S(1)}, f32[64]{0:T(128)}, u32[]{:S(2)}) copy-start(f32[64]{0:T(128)} %copy-done.86) | copy-start | bytes 772
  1324.4 43.6 %copy-start.24 = (f32[64,1536]{1,0:T(8,128)S(1)}, f32[64,1536]{1,0:T(8,128)}, u32[]{:S(2)}) copy-start(f32[64,1536]{1,0:T(8,128)} %get-tuple-element.1056) | copy-start | bytes 1179652
  1324.4 43.6 %copy-start.83 = (f32[64]{0:T(128)S(1)}, f32[64]{0:T(128)}, u32[]{:S(2)}) copy-start(f32[64]{0:T(128)} %copy-done.81) | copy-start | bytes 772
  1324.4 43.6 %copy-start.85 = (f32[64]{0:T(128)S(1)}, f32[64]{0:T(128)}, u32[]{:S(2)}) copy-start(f32[64]{0:T(128)} %broadcast_multiply_fusion.3) | copy-start | bytes 772
  (71 other events, 625.1 us)
Sparse Core Ops, SparseCore 0:
  10.8 59.9 all-gather.17
  73.6 55.8 all-gather.15
  132.3 64.0 all-gather.19
  199.0 62.3 all-gather.21
  264.1 93.6 all-gather.23
  360.6 93.7 all-gather.25
  457.3 93.7 all-gather.27
  718.9 33.5 reduce-scatter.17
  815.3 33.5 reduce-scatter.15
  851.9 34.9 reduce-scatter.33
  890.6 34.9 reduce-scatter.35
  927.0 66.3 all-gather.29
  995.0 67.1 all-gather.31
  1063.6 60.4 all-gather.33
  1125.6 49.1 all-gather.35
  1176.2 67.5 all-gather.37
  1245.2 44.2 all-gather.39
  1292.5 35.5 reduce-scatter.19
  1331.4 36.7 reduce-scatter.25
  1371.7 34.3 reduce-scatter.21
  1409.8 34.3 reduce-scatter.23
  1447.5 46.0 reduce-scatter.27
  1497.0 46.0 reduce-scatter.29
  1546.3 46.0 reduce-scatter.31
where the time goes:
time: 1620 us; the launch traced here: 1600 us
  waiting for transfers between devices  522 us (32%)
  blocking collectives  503 us (31%)
  matrix products  271 us (17%)
  local copies, waits for them, and re-layouts  181 us (11%)
  loops' own time  74.9 us (5%)
  other arithmetic  32.4 us (2%)
  between operations  16.3 us (1%)
    all_gather x1, waiting for transfers between devices, fetch_mlp(): lax.all_gather(w_down, ('ctx', 'fsdp'), axis=0, tiled=True)  88.9 us
    all_gather x1, waiting for transfers between devices, fetch_mlp(): lax.all_gather(w_up, ('ctx', 'fsdp'), axis=0, tiled=True)  88.7 us
    unnamed x2, blocking collectives  81.7 us
    all_gather x1, waiting for transfers between devices, fetch_mlp(): lax.all_gather(w_gate, ('ctx', 'fsdp'), axis=0, tiled=True)  73.9 us
    dot_general x14, matrix products, back_product(): jnp.einsum('te,de->td', grad_rows, weight_rows, preferred_element_type=jn...  67.9 us
    all_gather x2, blocking collectives, on_device(): lax.all_gather(query_low, 'fsdp', axis=0, tiled=True)  57.4 us
    all_gather x2, blocking collectives, on_device(): lax.all_gather(grad_low, 'fsdp', axis=0, tiled=True)  57.3 us
    another operation x2, loops' own time, on_device(): query_grads, key_grads, value_grads = lax.map(backward_group, group_ids)  53 us
  transfers between devices with their start and end apart: 24, of which 12 were waited for; matrix products, arithmetic and copies ran while one was open for 21% of the time, Pallas kernels for 0%

commit v1 on v0

v1 whole, which is shorter than its diff:
```python
import math

import jax
import jax.numpy as jnp
from jax import lax
from jax.sharding import Mesh, PartitionSpec as P

HEADS = 16
KV_HEADS = 8
HEAD = 96
EPS = 1e-05
THETA = 100000.0
f32 = jnp.float32
bf16 = jnp.bfloat16


def rope_tables(position_ids):
    half = HEAD // 2
    ladder = jnp.arange(half).astype(f32) * (2.0 / HEAD)
    inverse = jnp.exp(-math.log(THETA) * ladder)
    angles = position_ids.astype(f32)[:, None] * inverse[None, :]
    return jnp.cos(angles)[:, None, :], jnp.sin(angles)[:, None, :]


def rotate(vectors, cosine, sine):
    half = HEAD // 2
    a, b = vectors[..., :half], vectors[..., half:]
    return jnp.concatenate([a * cosine - b * sine, b * cosine + a * sine], axis=-1)


def unrotate(grads, cosine, sine):
    half = HEAD // 2
    a, b = grads[..., :half], grads[..., half:]
    return jnp.concatenate([a * cosine + b * sine, b * cosine - a * sine], axis=-1)


def rms_scale(values):
    return lax.rsqrt(jnp.mean(values * values, axis=-1, keepdims=True) + EPS)


def norm_back(grad, normed, scale):
    return scale * (grad - normed * jnp.mean(grad * normed, axis=-1, keepdims=True))


def mm(a, b):
    return jnp.dot(a, b, preferred_element_type=f32)


def mm_tn(a, b):
    return jnp.einsum("td,te->de", a, b, preferred_element_type=f32)


def mm_nt(a, b):
    return jnp.einsum("te,de->td", a, b, preferred_element_type=f32)


def on_device(
    block_input,
    positions,
    segments,
    out_cotangent,
    attn_gain,
    w_query,
    w_key,
    w_value,
    w_out,
    mlp_gain,
    w_gate,
    w_up,
    w_down,
):
    chips = lax.axis_size("chip")
    rows_z = lax.axis_size("fsdp")
    chip = lax.axis_index("chip")
    core = lax.axis_index("core")
    place = lax.axis_index("fsdp")
    tok = block_input.shape[2]
    width = block_input.shape[3]
    d_rows = w_query.shape[0]
    q_cols = w_query.shape[1] // chips
    kv_cols = w_key.shape[1] // chips
    ff_cols = w_gate.shape[1] // chips
    kv_heads = KV_HEADS // chips
    factor = HEAD ** (-0.5)

    def core_swap(a):
        return lax.ppermute(a, "core", [(0, 1), (1, 0)])

    def chip_xor(a, j):
        return lax.ppermute(a, "chip", [(i, i ^ j) for i in range(chips)])

    def pick(a, index, axis=0):
        return lax.dynamic_index_in_dim(a, index, axis, keepdims=False)

    def gather_chips(a, axis=0):
        return jnp.concatenate([a] + [chip_xor(a, j) for j in range(1, chips)], axis=axis)

    def scatter_chips(a):
        step = a.shape[0] // chips
        total = a[:step]
        for j in range(1, chips):
            total = total + chip_xor(a[j * step : (j + 1) * step].astype(bf16), j).astype(f32)
        return total

    def by_chip(pieces):
        stacked = jnp.stack(pieces)
        bit = 1
        while bit < chips:
            view = stacked.reshape((chips // (2 * bit), 2, bit) + stacked.shape[1:])
            flipped = jnp.flip(view, axis=1)
            stacked = jnp.where((chip & bit) != 0, flipped, view).reshape(stacked.shape)
            bit *= 2
        return stacked

    def exchange_chips(pack):
        pieces = [pick(pack, chip)]
        for j in range(1, chips):
            pieces.append(chip_xor(pick(pack, chip ^ j), j))
        return by_chip(pieces)

    def both_cores(a):
        other = core_swap(a)
        first = core == 0
        return jnp.where(first, a, other), jnp.where(first, other, a)

    def chip_slices(weights, cols):
        return jnp.stack(
            [
                jnp.concatenate([w[:, k * n : (k + 1) * n] for w, n in zip(weights, cols)], axis=1)
                for k in range(chips)
            ]
        )

    def fetch_columns(pack):
        mine = exchange_chips(pack)
        cols = mine.shape[-1]
        along = lax.all_gather(mine.reshape(-1, cols), "fsdp", axis=0, tiled=True)
        along = along.reshape(rows_z, chips, d_rows, cols)
        zero, one = both_cores(along)
        full = jnp.stack([zero, one])
        return jnp.transpose(full, (2, 0, 1, 3, 4)).reshape(chips * 2 * rows_z * d_rows, cols)

    def fetch_rows(weight):
        along = lax.all_gather(weight, "fsdp", axis=0, tiled=True)
        return jnp.concatenate(both_cores(along), axis=0)

    pair = jnp.stack([block_input[:, 0], out_cotangent[:, 0]], axis=1)
    pair = jnp.concatenate([pick(pair, core), core_swap(pick(pair, 1 - core))], axis=1)
    x_low, dy_low = pair[0], pair[1]
    marks = jnp.stack([positions[:, 0], segments[:, 0]], axis=1)
    marks = jnp.concatenate([pick(marks, core), core_swap(pick(marks, 1 - core))], axis=1)

    owner = (chip * 2 + core) * rows_z + place
    gains = jnp.zeros((2, width), bf16)
    gains = lax.dynamic_update_slice(
        gains, jnp.stack([attn_gain, mlp_gain]), (0, owner * d_rows)
    )

    def sum_everywhere(a):
        a = a + core_swap(a)
        bit = 1
        while bit < chips:
            a = a + chip_xor(a, bit)
            bit *= 2
        bit = 1
        while bit < rows_z:
            a = a + lax.ppermute(a, "fsdp", [(i, i ^ bit) for i in range(rows_z)])
            bit *= 2
        return a

    w_qkv = fetch_columns(chip_slices((w_query, w_key, w_value), (q_cols, kv_cols, kv_cols)))
    x_all = gather_chips(x_low)
    marks_all = gather_chips(marks, axis=1)
    gains = sum_everywhere(gains).astype(f32)
    gain_one, gain_two = gains[0], gains[1]
    out_w = fetch_rows(w_out)
    w_gu = fetch_columns(chip_slices((w_gate, w_up), (ff_cols, ff_cols)))
    down_w = fetch_rows(w_down)
    dy_all = gather_chips(dy_low)
    own = x_low.shape[0]
    seq = x_all.shape[0]

    pos_all, seg_all = marks_all[0], marks_all[1]
    allowed = (seg_all[:, None] == seg_all[None, :]) & (pos_all[None, :] <= pos_all[:, None])
    cosine, sine = rope_tables(pos_all)
    x_full = x_all.astype(f32)
    h_one = (x_full * rms_scale(x_full) * gain_one).astype(bf16)
    qkv = mm(h_one, w_qkv)
    q_rot = rotate(qkv[:, :q_cols].reshape(seq, kv_heads * 2, HEAD), cosine, sine)
    q_rot = q_rot.astype(bf16).reshape(seq, kv_heads, 2, HEAD)
    k_rot = rotate(
        qkv[:, q_cols : q_cols + kv_cols].reshape(seq, kv_heads, HEAD), cosine, sine
    ).astype(bf16)
    value = qkv[:, q_cols + kv_cols :].astype(bf16).reshape(seq, kv_heads, HEAD)
    scores = jnp.einsum("sgrh,tgh->grst", q_rot, k_rot, preferred_element_type=f32) * factor
    scores = jnp.where(allowed, scores, -1e30)
    raised = jnp.exp(scores - jnp.max(scores, axis=-1, keepdims=True))
    soft = raised / jnp.sum(raised, axis=-1, keepdims=True)
    soft_low = soft.astype(bf16)
    mixed = jnp.einsum("grst,tgh->sgrh", soft_low, value, preferred_element_type=f32)
    mixed = mixed.astype(bf16).reshape(seq, q_cols)
    x_own = x_low.astype(f32)
    middle = x_own + scatter_chips(mm(mixed, out_w))

    scale_two = rms_scale(middle)
    n_two = middle * scale_two
    h_two = gather_chips((n_two * gain_two).astype(bf16))
    gu = mm(h_two, w_gu)
    gate, up = gu[:, :ff_cols], gu[:, ff_cols:]
    sigma = jax.nn.sigmoid(gate)
    act = (gate * sigma * up).astype(bf16)
    result = (middle + scatter_chips(mm(act, down_w))).astype(bf16)

    d_act = mm_nt(dy_all, down_w)
    d_gate = (d_act * up * sigma * (1.0 + gate * (1.0 - sigma))).astype(bf16)
    d_up = (d_act * gate * sigma).astype(bf16)
    d_gu = jnp.concatenate([d_gate, d_up], axis=1)
    d_h_two = scatter_chips(mm_nt(d_gu, w_gu))

    def reduce_columns(left, right):
        grad = mm_tn(left, right).astype(bf16)
        cols = grad.shape[1]
        grad = grad.reshape(chips, 2, rows_z, d_rows, cols)
        other = core_swap(pick(grad, 1 - core, 1))
        total = pick(grad, core, 1) + other
        total = jnp.transpose(total, (1, 0, 2, 3)).reshape(rows_z * chips * d_rows, cols)
        total = lax.psum_scatter(total, "fsdp", scatter_dimension=0, tiled=True)
        return exchange_chips(total.reshape(chips, d_rows, cols))

    def reduce_rows(left, right):
        grad = mm_tn(left, right).astype(bf16)
        grad = grad.reshape(2, grad.shape[0] // 2, grad.shape[1])
        total = pick(grad, core) + core_swap(pick(grad, 1 - core))
        return lax.psum_scatter(total, "fsdp", scatter_dimension=0, tiled=True).astype(f32)

    g_gu = reduce_columns(h_two, d_gu)
    g_down = reduce_rows(act, dy_all)
    dy_own = dy_low.astype(f32)
    gain_two_part = jnp.sum(d_h_two * n_two, axis=0)
    d_middle = dy_own + norm_back(d_h_two * gain_two, n_two, scale_two)
    branch = gather_chips(d_middle.astype(bf16))

    g_out = reduce_rows(mixed, branch)
    d_mixed = mm_nt(branch, out_w).astype(bf16).reshape(seq, kv_heads, 2, HEAD)
    d_soft = jnp.einsum("sgrh,tgh->grst", d_mixed, value, preferred_element_type=f32)
    d_value = jnp.einsum("grst,sgrh->tgh", soft_low, d_mixed, preferred_element_type=f32)
    inner = jnp.sum(soft * d_soft, axis=-1, keepdims=True)
    d_scores = (soft * (d_soft - inner)).astype(bf16)
    d_q = jnp.einsum("grst,tgh->sgrh", d_scores, k_rot, preferred_element_type=f32) * factor
    d_k = jnp.einsum("grst,sgrh->tgh", d_scores, q_rot, preferred_element_type=f32) * factor
    d_q = unrotate(d_q.reshape(seq, kv_heads * 2, HEAD), cosine, sine)
    d_k = unrotate(d_k, cosine, sine)
    d_qkv = jnp.concatenate(
        [
            d_q.reshape(seq, q_cols).astype(bf16),
            d_k.reshape(seq, kv_cols).astype(bf16),
            d_value.reshape(seq, kv_cols).astype(bf16),
        ],
        axis=1,
    )
    d_h_one = scatter_chips(mm_nt(d_qkv, w_qkv))
    g_qkv = reduce_columns(h_one, d_qkv)
    scale_one = rms_scale(x_own)
    n_one = x_own * scale_one
    gain_one_part = jnp.sum(d_h_one * n_one, axis=0)
    d_input = (d_middle + norm_back(d_h_one * gain_one, n_one, scale_one)).astype(bf16)

    def give_back(a):
        mine, theirs = a[:tok], core_swap(a[tok:])
        first = core == 0
        return jnp.stack([jnp.where(first, mine, theirs), jnp.where(first, theirs, mine)])[:, None]

    def spread(grad, start, cols):
        part = grad[:, :, start : start + cols].astype(f32)
        return jnp.transpose(part, (1, 0, 2)).reshape(d_rows, chips * cols)

    gain_parts = sum_everywhere(jnp.stack([gain_one_part, gain_two_part]))
    gain_parts = lax.dynamic_slice_in_dim(gain_parts, owner * d_rows, d_rows, 1)
    return (
        give_back(result),
        give_back(d_input),
        gain_parts[0],
        spread(g_qkv, 0, q_cols),
        spread(g_qkv, q_cols, kv_cols),
        spread(g_qkv, q_cols + kv_cols, kv_cols),
        g_out,
        gain_parts[1],
        spread(g_gu, 0, ff_cols),
        spread(g_gu, ff_cols, ff_cols),
        g_down,
    )


def solution(mesh):
    ctx, fsdp = mesh.shape["ctx"], mesh.shape["fsdp"]
    split = Mesh(mesh.devices.reshape(ctx // 2, 2, fsdp), ("chip", "core", "fsdp"))
    ctx_axes = ("chip", "core")
    all_axes = ("chip", "core", "fsdp")
    tokens = P(None, "fsdp", ctx_axes, None)
    marks = P(None, "fsdp", ctx_axes)
    vector, matrix = P(all_axes), P(all_axes, None)
    return jax.shard_map(
        on_device,
        mesh=split,
        in_specs=(
            tokens, marks, marks, tokens, vector, matrix, matrix, matrix, matrix,
            vector, matrix, matrix, matrix,
        ),
        out_specs=(
            tokens, tokens, vector, matrix, matrix, matrix, matrix, vector,
            matrix, matrix, matrix,
        ),
        check_vma=False,
    )
```

time: 1620 us -> 460 us (0.28)
  blocking collectives: 503 us -> 24.5 us
  waiting for transfers between devices: 522 us -> 258 us
  matrix products: 271 us -> 41.1 us
  local copies, waits for them, and re-layouts: 181 us -> 27 us
  loops' own time: 74.9 us -> 0 us
  starting transfers between devices: 0.95 us -> 59.3 us
    all_gather x22 -> x1, blocking collectives: 421 us -> 24.5 us  [fetch_rows(): along = lax.all_gather(weight, 'fsdp', axis=0, tiled=True)]
    all_gather x13 -> x3, waiting for transfers between devices: 302 us -> 57.9 us  [the longest x2 53.2 us: fetch_columns(): along = lax.all_gather(mine.reshape(-1, cols), 'fsdp', axis=0, tiled=True)]
    dot_general x154 -> x17, matrix products: 271 us -> 36.2 us  [the longest x4 12.1 us: mm_tn(): return jnp.einsum('td,te->de', a, b, preferred_element_type=f32)]
    reduce_scatter x9 -> x4, waiting for transfers between devices: 212 us -> 58.8 us  [the longest x2 30.9 us: reduce_rows(): lax.psum_scatter(total, 'fsdp', scatter_dimension=0, tiled=True).astype(f32)]
    ppermute x0 -> x61, waiting for transfers between devices: none -> 141 us  [the longest x43 128 us: chip_xor(): return lax.ppermute(a, 'chip', [(i, i ^ j) for i in range(chips)])]
    unnamed x2 -> x0, blocking collectives: 81.7 us -> none
    another operation x4 -> x0, loops' own time: 74.9 us -> none  [the longest x2 53 us: on_device(): query_grads, key_grads, value_grads = lax.map(backward_group, group_ids)]
    ppermute x0 -> x61, starting transfers between devices: none -> 59 us  [the longest x43 52.4 us: chip_xor(): return lax.ppermute(a, 'chip', [(i, i ^ j) for i in range(chips)])]
  transfers between devices with their start and end apart: 24 -> 68, of which waited for: 12 -> 36; matrix products, arithmetic and copies ran while one was open for 21% -> 15% of each run, Pallas kernels for 0% -> 0%
where the time goes in v1:
time: 460 us; the launch traced here: 457 us
  waiting for transfers between devices  258 us (56%)
  starting transfers between devices  59.3 us (13%)
  matrix products  41.1 us (9%)
  other arithmetic  31.2 us (7%)
  local copies, waits for them, and re-layouts  27 us (6%)
  blocking collectives  24.5 us (5%)
  between operations  16 us (3%)
    ppermute x43, waiting for transfers between devices, chip_xor(): return lax.ppermute(a, 'chip', [(i, i ^ j) for i in range(chips)])  128 us
    all_gather x2, waiting for transfers between devices, fetch_columns(): along = lax.all_gather(mine.reshape(-1, cols), 'fsdp', axis=0, tiled=True)  53.2 us
    ppermute x43, starting transfers between devices, chip_xor(): return lax.ppermute(a, 'chip', [(i, i ^ j) for i in range(chips)])  52.4 us
    reduce_scatter x2, waiting for transfers between devices, reduce_rows(): lax.psum_scatter(total, 'fsdp', scatter_dimension=0, tiled=True).astype(f32)  30.9 us
    reduce_scatter x2, waiting for transfers between devices, reduce_columns(): total = lax.psum_scatter(total, 'fsdp', scatter_dimension=0, tiled=True)  27.9 us
    all_gather x1, blocking collectives, fetch_rows(): along = lax.all_gather(weight, 'fsdp', axis=0, tiled=True)  24.5 us
    dot_general x4, matrix products, mm_tn(): return jnp.einsum('td,te->de', a, b, preferred_element_type=f32)  12.1 us
    unnamed x157, local copies, waits for them, and re-layouts  11 us
  transfers between devices with their start and end apart: 68, of which 36 were waited for; matrix products, arithmetic and copies ran while one was open for 15% of the time, Pallas kernels for 0%

profile of v1, /device:TPU:0, one launch (start us, length us, event | category | flops | bytes accessed | tf_op | source)
XLA Modules:
  0.0 456.8 jit_solution(14278591957215461566)
XLA Ops:
  10.3 4.0 collective-permute-start.11
  16.6 2.0 collective-permute-done.10
  25.1 24.5 %all_gather.13 = bf16[192,1536]{1,0:T(8,128)(2,1)S(1)} all-gather(bf16[48,1536]{1,0:T(8,128)(2,1)S(1)} %copy-done.42), channel_id=1, replica_groups=mesh['chip'=4,'core'=2,'fsdp'=4] {'fsdp'}, dimensions={0}, use_global_device_ids=true | all-gather | bytes 737280 | tf_op jit(solution)/shard_map/all_gather | solution.py:144
  56.9 1.9 collective-permute-done.5
  60.4 2.1 collective-permute-done.6
  66.2 2.1 collective-permute-start.8
  68.9 2.0 collective-permute-done.8
  76.1 8.5 %collective-permute-done.3 = bf16[128,1536]{1,0:T(8,128)(2,1)S(1)} collective-permute-done((bf16[128,1536]{1,0:T(8,128)(2,1)S(1)}, bf16[128,1536]{1,0:T(8,128)(2,1)S(1)}, u32[]{:S(2)}, u32[]{:S(2)}) %collective-permute-start.3) | collective-permute-done | bytes 393248 | tf_op jit(solution)/shard_map/ppermute | solution.py:90
  84.6 5.7 %collective-permute-done.2 = bf16[128,1536]{1,0:T(8,128)(2,1)S(1)} collective-permute-done((bf16[128,1536]{1,0:T(8,128)(2,1)S(1)}, bf16[128,1536]{1,0:T(8,128)(2,1)S(1)}, u32[]{:S(2)}, u32[]{:S(2)}) %collective-permute-start.2) | collective-permute-done | bytes 393248 | tf_op jit(solution)/shard_map/ppermute | solution.py:90
  91.7 4.7 %all-gather.8.cloned.1.call-done = bf16[512,1536]{1,0:T(8,128)(2,1)} async-done(((bf16[128,1536]{1,0:T(8,128)(2,1)}), bf16[512,1536]{1,0:T(8,128)(2,1)}) %all-gather.8.cloned.1.call-update) | async-done | bytes 1572880 | tf_op jit(solution)/shard_map/all_gather | solution.py:144
  96.4 1.8 select_bitcast_fusion.3
  102.8 4.9 %fusion.95 = (f32[2,2,512]{2,1,0:T(2,128)S(1)}, f32[2,2,512,512]{2,3,1,0:T(8,128)}) fusion(pred[512,512]{0,1:T(8,128)(4,1)} %compare_and_fusion, bf16[512,2,2,48]{0,3,2,1:T(8,128)(2,1)S(1)} %bitcast.289, bf16[512,2,2,48]{0,3,2,1:T(8,128)(2,1)S(1)} %bitcast.287, bf16[512,2,48]{0,2,1:T(8,128)(2,1)S(1)} %get-tuple-element.108, ...), kind=kOutput, calls=%fused_computation.244 | convolution fusion | flops 206701056 | bytes 5054464 | tf_op jit(solution)/shard_map/sub | solution.py:197
  107.7 53.1 %all-gather.6.cloned.1.call-done = bf16[768,2048]{1,0:T(8,128)(2,1)} async-done(((bf16[192,2048]{1,0:T(8,128)(2,1)}), bf16[768,2048]{1,0:T(8,128)(2,1)}) %all-gather.6.cloned.1.call-update) | async-done | bytes 3145744 | tf_op jit(solution)/shard_map/all_gather | solution.py:137
  160.8 2.7 convolution_convert_fusion.4
  168.3 8.5 %collective-permute-done.18 = bf16[128,1536]{1,0:T(8,128)(2,1)S(1)} collective-permute-done((bf16[128,1536]{1,0:T(8,128)(2,1)S(1)}, bf16[128,1536]{1,0:T(8,128)(2,1)S(1)}, u32[]{:S(2)}, u32[]{:S(2)}) %collective-permute-start.18) | collective-permute-done | bytes 393248 | tf_op jit(solution)/shard_map/ppermute | solution.py:90
  176.8 2.4 collective-permute-start.35
  179.2 7.1 %collective-permute-done.20 = bf16[128,1536]{1,0:T(8,128)(2,1)S(1)} collective-permute-done((bf16[128,1536]{1,0:T(8,128)(2,1)S(1)}, bf16[128,1536]{1,0:T(8,128)(2,1)S(1)}, u32[]{:S(2)}, u32[]{:S(2)}) %collective-permute-start.20) | collective-permute-done | bytes 393248 | tf_op jit(solution)/shard_map/ppermute | solution.py:90
  186.8 9.8 %collective-permute-done.19 = bf16[128,1536]{1,0:T(8,128)(2,1)S(1)} collective-permute-done((bf16[128,1536]{1,0:T(8,128)(2,1)S(1)}, bf16[128,1536]{1,0:T(8,128)(2,1)S(1)}, u32[]{:S(2)}, u32[]{:S(2)}) %collective-permute-start.19) | collective-permute-done | bytes 393248 | tf_op jit(solution)/shard_map/ppermute | solution.py:90
  200.1 3.2 broadcast_select_fusion.1
  206.0 4.0 collective-permute-done.23
  211.5 9.4 %collective-permute-done.22 = bf16[128,1536]{1,0:T(8,128)(2,1)} collective-permute-done((bf16[128,1536]{1,0:T(8,128)(2,1)S(1)}, bf16[128,1536]{1,0:T(8,128)(2,1)}, u32[]{:S(2)}, u32[]{:S(2)}) %collective-permute-start.22) | collective-permute-done | bytes 393248 | tf_op jit(solution)/shard_map/ppermute | solution.py:90
  221.7 5.1 %fusion.53 = f32[512,2048]{1,0:T(8,128)S(1)} fusion(bf16[1536,2048]{1,0:T(8,128)(2,1)S(1)} %bitcast.249, bf16[128,1536]{1,0:T(8,128)(2,1)S(1)} %collective-permute-done.23, bf16[128,1536]{1,0:T(8,128)(2,1)} %collective-permute-done.22, bf16[128,1536]{1,0:T(8,128)(2,1)} %copy-done.62, bf16[128,1536]{1,0:T(8,128)(2,1)S(1)} %multiply_convert_fusion.3), kind=kOutput, calls=%fused_computation.139 | convolution fusion | flops 3227516928 | bytes 12058624 | tf_op jit(solution)/shard_map/dot_general | solution.py:46
  226.9 3.5 multiply_convert_fusion.1
  230.4 3.5 fusion.97
  237.6 8.5 %collective-permute-done.36 = bf16[128,1536]{1,0:T(8,128)(2,1)S(1)} collective-permute-done((bf16[128,1536]{1,0:T(8,128)(2,1)S(1)}, bf16[128,1536]{1,0:T(8,128)(2,1)S(1)}, u32[]{:S(2)}, u32[]{:S(2)}) %collective-permute-start.36) | collective-permute-done | bytes 393248 | tf_op jit(solution)/shard_map/ppermute | solution.py:90
  246.1 6.6 %collective-permute-done.38 = bf16[128,1536]{1,0:T(8,128)(2,1)S(1)} collective-permute-done((bf16[128,1536]{1,0:T(8,128)(2,1)S(1)}, bf16[128,1536]{1,0:T(8,128)(2,1)S(1)}, u32[]{:S(2)}, u32[]{:S(2)}) %collective-permute-start.38) | collective-permute-done | bytes 393248 | tf_op jit(solution)/shard_map/ppermute | solution.py:90
  255.3 2.4 collective-permute-start.41
  258.9 9.4 %collective-permute-done.41 = bf16[128,1536]{1,0:T(8,128)(2,1)S(1)} collective-permute-done((bf16[128,1536]{1,0:T(8,128)(2,1)S(1)}, bf16[128,1536]{1,0:T(8,128)(2,1)S(1)}, u32[]{:S(2)}, u32[]{:S(2)}) %collective-permute-start.41) | collective-permute-done | bytes 393248 | tf_op jit(solution)/shard_map/ppermute | solution.py:90
  268.3 4.3 collective-permute-done.40
  279.1 1.8 convolution_convert_fusion.2
  282.9 4.8 %convolution_convert_fusion = bf16[1536,2048]{1,0:T(8,128)(2,1)S(1)} fusion(bf16[512,1024]{1,0:T(8,128)(2,1)S(1)} %copy-done.73, bf16[512,1024]{1,0:T(8,128)(2,1)S(1)} %copy-done.71, bf16[128,1536]{1,0:T(8,128)(2,1)S(1)} %copy-done.61, bf16[128,1536]{1,0:T(8,128)(2,1)} %collective-permute-done.22, bf16[128,1536]{1,0:T(8,128)(2,1)S(1)} %copy-done.63, ...), kind=kOutput, calls=%fused_computation.1 | convolution fusion | flops 3234856960 | bytes 9961472 | tf_op jit(solution)/shard_map/td,te->de/dot_general | solution.py:50
  287.7 2.6 constant_dynamic-slice_fusion.5
  290.3 1.9 copy.108
  293.5 2.0 convolution_convert_fusion.3
  296.2 2.7 collective-permute-done.55
  299.9 4.9 %bitcast_add_fusion = bf16[4,4,48,2048]{3,2,0,1:T(8,128)(2,1)} fusion(bf16[4,4,48,2048]{3,2,0,1:T(8,128)(2,1)} %collective-permute-done.56, bf16[4,1,4,48,2048]{4,3,2,1,0:T(8,128)(2,1)} %get-tuple-element.56), kind=kLoop, calls=%fused_computation.19 | loop fusion | flops 1572864 | bytes 9437184 | tf_op jit(solution)/shard_map/add | solution.py:225
  305.4 3.5 convolution_convert_fusion.1
  314.2 1.8 fusion.99
  316.0 6.6 %collective-permute-done.42 = bf16[128,1536]{1,0:T(8,128)(2,1)S(1)} collective-permute-done((bf16[128,1536]{1,0:T(8,128)(2,1)S(1)}, bf16[128,1536]{1,0:T(8,128)(2,1)S(1)}, u32[]{:S(2)}, u32[]{:S(2)}) %collective-permute-start.42) | collective-permute-done | bytes 393248 | tf_op jit(solution)/shard_map/ppermute | solution.py:90
  322.6 8.6 %collective-permute-done.44 = bf16[128,1536]{1,0:T(8,128)(2,1)S(1)} collective-permute-done((bf16[128,1536]{1,0:T(8,128)(2,1)S(1)}, bf16[128,1536]{1,0:T(8,128)(2,1)S(1)}, u32[]{:S(2)}, u32[]{:S(2)}) %collective-permute-start.44) | collective-permute-done | bytes 393248 | tf_op jit(solution)/shard_map/ppermute | solution.py:90
  340.2 16.9 %collective-permute-done.48 = f32[2,1536]{1,0:T(2,128)S(1)} collective-permute-done((f32[2,1536]{1,0:T(2,128)S(1)}, f32[2,1536]{1,0:T(2,128)S(1)}, u32[]{:S(2)}, u32[]{:S(2)}) %collective-permute-start.48) | collective-permute-done | bytes 12320 | tf_op jit(solution)/shard_map/ppermute | solution.py:90
  358.5 3.3 collective-permute-done.49
  363.8 3.0 collective-permute-done.50
  369.4 2.5 collective-permute-start.54
  377.9 27.9 %reduce-scatter.9.cloned.1.call-done = bf16[192,2048]{1,0:T(8,128)(2,1)} async-done(((bf16[768,2048]{1,0:T(8,128)(2,1)}), bf16[192,2048]{1,0:T(8,128)(2,1)}) %reduce-scatter.9.cloned.1.call-update) | async-done | bytes 786448 | tf_op jit(solution)/shard_map/reduce_scatter | solution.py:227
  407.1 2.5 collective-permute-start.59
  412.6 30.9 %reduce-scatter.11.cloned.1.call-done = bf16[128,1536]{1,0:T(8,128)(2,1)} async-done(((bf16[512,1536]{1,0:T(8,128)(2,1)}), bf16[128,1536]{1,0:T(8,128)(2,1)}) %reduce-scatter.11.cloned.1.call-update) | async-done | bytes 393232 | tf_op jit(solution)/shard_map/reduce_scatter | solution.py:234
  443.5 2.0 convert_element_type.198
  (389 shorter events, 102.7 us)
Async XLA Ops:
  7.2 61.6 %all-gather.4.cloned.1.call-start = ((), (), s32[]{:S(2)}) async-start(), calls=%async_computation.4 | async-start | bytes 1474560 | tf_op jit(solution)/shard_map/all_gather | solution.py:137
  20.0 76.4 %all-gather.8.cloned.1.call-start = ((), (), s32[]{:S(2)}) async-start(), calls=%async_computation.6 | async-start | bytes 1966080 | tf_op jit(solution)/shard_map/all_gather | solution.py:144
  20.1 31.0 %collective-permute-start.13 = (s32[2,64]{1,0:T(2,128)S(1)}, s32[2,64]{1,0:T(2,128)S(1)}, u32[]{:S(2)}, u32[]{:S(2)}) collective-permute-start(s32[2,64]{1,0:T(2,128)S(1)} %get-tuple-element.143), channel_id=1, source_target_pairs={{0,4},{4,0},{1,5},{5,1},{2,6},{6,2},{3,7},{7,3},{8,12},{12,8},{9,1... | collective-permute-start | bytes 1544 | tf_op jit(solution)/shard_map/ppermute | solution.py:87
  20.5 34.3 %collective-permute-start.4 = (bf16[2,1536]{1,0:T(2,128)(2,1)S(1)}, bf16[2,1536]{1,0:T(2,128)(2,1)S(1)}, u32[]{:S(2)}, u32[]{:S(2)}) collective-permute-start(bf16[2,1536]{1,0:T(2,128)(2,1)S(1)} %dynamic_update_slice.5), channel_id=1, source_target_pairs={{0,4},{4,0},{1,5},{5,1},{2,6},{6,2},{3,7},{7,3},{8,12},{12,8},{9,1... | collective-permute-start | bytes 18440 | tf_op jit(solution)/shard_map/ppermute | solution.py:87
  21.1 139.7 %all-gather.6.cloned.1.call-start = ((), (), s32[]{:S(2)}) async-start(), calls=%async_computation.5 | async-start | bytes 3932160 | tf_op jit(solution)/shard_map/all_gather | solution.py:137
  21.5 28.1 %collective-permute-start.26 = (bf16[48,2048]{1,0:T(8,128)(2,1)S(1)}, bf16[48,2048]{1,0:T(8,128)(2,1)S(1)}, u32[]{:S(2)}, u32[]{:S(2)}) collective-permute-start(bf16[48,2048]{1,0:T(8,128)(2,1)S(1)} %get-tuple-element.96), channel_id=1, source_target_pairs={{0,24},{8,16},{16,8},{24,0},{1,25},{9,17},{17,9},{25,1},{2,26},{10... | collective-permute-start | bytes 589832 | tf_op jit(solution)/shard_map/ppermute | solution.py:90
  23.1 26.5 %collective-permute-start.25 = (bf16[48,2048]{1,0:T(8,128)(2,1)S(1)}, bf16[48,2048]{1,0:T(8,128)(2,1)S(1)}, u32[]{:S(2)}, u32[]{:S(2)}) collective-permute-start(bf16[48,2048]{1,0:T(8,128)(2,1)S(1)} %get-tuple-element.97), channel_id=1, source_target_pairs={{0,16},{8,24},{16,0},{24,8},{1,17},{9,25},{17,1},{25,9},{2,18},{10... | collective-permute-start | bytes 589832 | tf_op jit(solution)/shard_map/ppermute | solution.py:90
  23.8 25.9 %collective-permute-start.24 = (bf16[48,2048]{1,0:T(8,128)(2,1)S(1)}, bf16[48,2048]{1,0:T(8,128)(2,1)S(1)}, u32[]{:S(2)}, u32[]{:S(2)}) collective-permute-start(bf16[48,2048]{1,0:T(8,128)(2,1)S(1)} %get-tuple-element.98), channel_id=1, source_target_pairs={{0,8},{8,0},{16,24},{24,16},{1,9},{9,1},{17,25},{25,17},{2,10},{10... | collective-permute-start | bytes 589832 | tf_op jit(solution)/shard_map/ppermute | solution.py:90
  49.6 25.5 %collective-permute-start.17 = (bf16[192,1536]{1,0:T(8,128)(2,1)S(1)}, bf16[192,1536]{1,0:T(8,128)(2,1)S(1)}, u32[]{:S(2)}, u32[]{:S(2)}) collective-permute-start(bf16[192,1536]{1,0:T(8,128)(2,1)S(1)} %all_gather.13), channel_id=1, source_target_pairs={{0,4},{4,0},{1,5},{5,1},{2,6},{6,2},{3,7},{7,3},{8,12},{12,8},{9,1... | collective-permute-start | bytes 1769480 | tf_op jit(solution)/shard_map/ppermute | solution.py:87
  51.0 317.4 %reduce-scatter.5.cloned.1.call-start = ((), (), s32[]{:S(2)}) async-start(), calls=%async_computation.7 | async-start | bytes 1474560 | tf_op jit(solution)/shard_map/reduce_scatter | solution.py:227
  55.7 15.3 %collective-permute-start = (bf16[2,64,1536]{2,1,0:T(8,128)(2,1)S(1)}, bf16[2,64,1536]{2,1,0:T(8,128)(2,1)S(1)}, u32[]{:S(2)}, u32[]{:S(2)}) collective-permute-start(bf16[2,64,1536]{2,1,0:T(8,128)(2,1)S(1)} %get-tuple-element.100), channel_id=1, source_target_pairs={{0,4},{4,0},{1,5},{5,1},{2,6},{6,2},{3,7},{7,3},{8,12},{12,8},{9,1... | collective-permute-start | bytes 1179656 | tf_op jit(solution)/shard_map/ppermute | solution.py:87
  68.8 27.6 %collective-permute-start.12 = (bf16[4,4,48,768]{3,2,1,0:T(8,128)(2,1)}, bf16[4,4,48,768]{3,2,1,0:T(8,128)(2,1)}, u32[]{:S(2)}, u32[]{:S(2)}) collective-permute-start(bf16[4,4,48,768]{3,2,1,0:T(8,128)(2,1)} %bitcast.271), channel_id=1, source_target_pairs={{0,4},{4,0},{1,5},{5,1},{2,6},{6,2},{3,7},{7,3},{8,12},{12,8},{9,1... | collective-permute-start | bytes 3538952 | tf_op jit(solution)/shard_map/ppermute | solution.py:87
  71.7 12.9 %collective-permute-start.3 = (bf16[128,1536]{1,0:T(8,128)(2,1)S(1)}, bf16[128,1536]{1,0:T(8,128)(2,1)S(1)}, u32[]{:S(2)}, u32[]{:S(2)}) collective-permute-start(bf16[128,1536]{1,0:T(8,128)(2,1)S(1)} %get-tuple-element.52), channel_id=1, source_target_pairs={{0,24},{8,16},{16,8},{24,0},{1,25},{9,17},{17,9},{25,1},{2,26},{10... | collective-permute-start | bytes 1179656 | tf_op jit(solution)/shard_map/ppermute | solution.py:90
  72.9 17.4 %collective-permute-start.2 = (bf16[128,1536]{1,0:T(8,128)(2,1)S(1)}, bf16[128,1536]{1,0:T(8,128)(2,1)S(1)}, u32[]{:S(2)}, u32[]{:S(2)}) collective-permute-start(bf16[128,1536]{1,0:T(8,128)(2,1)S(1)} %get-tuple-element.52), channel_id=1, source_target_pairs={{0,16},{8,24},{16,0},{24,8},{1,17},{9,25},{17,1},{25,9},{2,18},{10... | collective-permute-start | bytes 1179656 | tf_op jit(solution)/shard_map/ppermute | solution.py:90
  73.6 16.9 %collective-permute-start.1 = (bf16[128,1536]{1,0:T(8,128)(2,1)S(1)}, bf16[128,1536]{1,0:T(8,128)(2,1)S(1)}, u32[]{:S(2)}, u32[]{:S(2)}) collective-permute-start(bf16[128,1536]{1,0:T(8,128)(2,1)S(1)} %get-tuple-element.52), channel_id=1, source_target_pairs={{0,8},{8,0},{16,24},{24,16},{1,9},{9,1},{17,25},{25,17},{2,10},{10... | collective-permute-start | bytes 1179656 | tf_op jit(solution)/shard_map/ppermute | solution.py:90
  96.4 102.2 %collective-permute-start.28 = (bf16[512,1536]{1,0:T(8,128)(2,1)}, bf16[512,1536]{1,0:T(8,128)(2,1)}, u32[]{:S(2)}, u32[]{:S(2)}) collective-permute-start(bf16[512,1536]{1,0:T(8,128)(2,1)} %all-gather.8.cloned.1.call-done), channel_id=1, source_target_pairs={{0,4},{4,0},{1,5},{5,1},{2,6},{6,2},{3,7},{7,3},{8,12},{12,8},{9,1... | collective-permute-start | bytes 4718600 | tf_op jit(solution)/shard_map/ppermute | solution.py:87
  160.8 42.5 %collective-permute-start.27 = (bf16[4,4,48,2048]{3,2,1,0:T(8,128)(2,1)}, bf16[4,4,48,2048]{3,2,1,0:T(8,128)(2,1)S(1)}, u32[]{:S(2)}, u32[]{:S(2)}) collective-permute-start(bf16[4,4,48,2048]{3,2,1,0:T(8,128)(2,1)} %bitcast.262), channel_id=1, source_target_pairs={{0,4},{4,0},{1,5},{5,1},{2,6},{6,2},{3,7},{7,3},{8,12},{12,8},{9,1... | collective-permute-start | bytes 9437192 | tf_op jit(solution)/shard_map/ppermute | solution.py:87
  164.7 12.1 %collective-permute-start.18 = (bf16[128,1536]{1,0:T(8,128)(2,1)S(1)}, bf16[128,1536]{1,0:T(8,128)(2,1)S(1)}, u32[]{:S(2)}, u32[]{:S(2)}) collective-permute-start(bf16[128,1536]{1,0:T(8,128)(2,1)S(1)} %get-tuple-element.78), channel_id=1, source_target_pairs={{0,8},{8,0},{16,24},{24,16},{1,9},{9,1},{17,25},{25,17},{2,10},{10... | collective-permute-start | bytes 1179656 | tf_op jit(solution)/shard_map/ppermute | solution.py:90
  166.3 20.0 %collective-permute-start.20 = (bf16[128,1536]{1,0:T(8,128)(2,1)S(1)}, bf16[128,1536]{1,0:T(8,128)(2,1)S(1)}, u32[]{:S(2)}, u32[]{:S(2)}) collective-permute-start(bf16[128,1536]{1,0:T(8,128)(2,1)S(1)} %get-tuple-element.79), channel_id=1, source_target_pairs={{0,24},{8,16},{16,8},{24,0},{1,25},{9,17},{17,9},{25,1},{2,26},{10... | collective-permute-start | bytes 1179656 | tf_op jit(solution)/shard_map/ppermute | solution.py:90
  167.7 28.8 %collective-permute-start.19 = (bf16[128,1536]{1,0:T(8,128)(2,1)S(1)}, bf16[128,1536]{1,0:T(8,128)(2,1)S(1)}, u32[]{:S(2)}, u32[]{:S(2)}) collective-permute-start(bf16[128,1536]{1,0:T(8,128)(2,1)S(1)} %get-tuple-element.80), channel_id=1, source_target_pairs={{0,16},{8,24},{16,0},{24,8},{1,17},{9,25},{17,1},{25,9},{2,18},{10... | collective-permute-start | bytes 1179656 | tf_op jit(solution)/shard_map/ppermute | solution.py:90
  176.8 50.0 %collective-permute-start.35 = (bf16[128,1536]{1,0:T(8,128)(2,1)S(1)}, bf16[128,1536]{1,0:T(8,128)(2,1)S(1)}, u32[]{:S(2)}, u32[]{:S(2)}) collective-permute-start(bf16[128,1536]{1,0:T(8,128)(2,1)S(1)} %fusion.49), channel_id=1, source_target_pairs={{0,24},{8,16},{16,8},{24,0},{1,25},{9,17},{17,9},{25,1},{2,26},{10... | collective-permute-start | bytes 1179656 | tf_op jit(solution)/shard_map/ppermute | solution.py:90
  186.2 40.6 %collective-permute-start.34 = (bf16[128,1536]{1,0:T(8,128)(2,1)S(1)}, bf16[128,1536]{1,0:T(8,128)(2,1)S(1)}, u32[]{:S(2)}, u32[]{:S(2)}) collective-permute-start(bf16[128,1536]{1,0:T(8,128)(2,1)S(1)} %fusion.49), channel_id=1, source_target_pairs={{0,16},{8,24},{16,0},{24,8},{1,17},{9,25},{17,1},{25,9},{2,18},{10... | collective-permute-start | bytes 1179656 | tf_op jit(solution)/shard_map/ppermute | solution.py:90
  197.1 13.0 %collective-permute-start.23 = (bf16[128,1536]{1,0:T(8,128)(2,1)S(1)}, bf16[128,1536]{1,0:T(8,128)(2,1)S(1)}, u32[]{:S(2)}, u32[]{:S(2)}) collective-permute-start(bf16[128,1536]{1,0:T(8,128)(2,1)S(1)} %multiply_convert_fusion.3), channel_id=1, source_target_pairs={{0,24},{8,16},{16,8},{24,0},{1,25},{9,17},{17,9},{25,1},{2,26},{10... | collective-permute-start | bytes 1179656 | tf_op jit(solution)/shard_map/ppermute | solution.py:90
  198.6 22.3 %collective-permute-start.22 = (bf16[128,1536]{1,0:T(8,128)(2,1)S(1)}, bf16[128,1536]{1,0:T(8,128)(2,1)}, u32[]{:S(2)}, u32[]{:S(2)}) collective-permute-start(bf16[128,1536]{1,0:T(8,128)(2,1)S(1)} %multiply_convert_fusion.3), channel_id=1, source_target_pairs={{0,16},{8,24},{16,0},{24,8},{1,17},{9,25},{17,1},{25,9},{2,18},{10... | collective-permute-start | bytes 1179656 | tf_op jit(solution)/shard_map/ppermute | solution.py:90
  203.3 17.6 %collective-permute-start.21 = (bf16[128,1536]{1,0:T(8,128)(2,1)S(1)}, bf16[128,1536]{1,0:T(8,128)(2,1)S(1)}, u32[]{:S(2)}, u32[]{:S(2)}) collective-permute-start(bf16[128,1536]{1,0:T(8,128)(2,1)S(1)} %multiply_convert_fusion.3), channel_id=1, source_target_pairs={{0,8},{8,0},{16,24},{24,16},{1,9},{9,1},{17,25},{25,17},{2,10},{10... | collective-permute-start | bytes 1179656 | tf_op jit(solution)/shard_map/ppermute | solution.py:90
  210.1 16.8 %collective-permute-start.33 = (bf16[128,1536]{1,0:T(8,128)(2,1)S(1)}, bf16[128,1536]{1,0:T(8,128)(2,1)S(1)}, u32[]{:S(2)}, u32[]{:S(2)}) collective-permute-start(bf16[128,1536]{1,0:T(8,128)(2,1)S(1)} %fusion.49), channel_id=1, source_target_pairs={{0,8},{8,0},{16,24},{24,16},{1,9},{9,1},{17,25},{25,17},{2,10},{10... | collective-permute-start | bytes 1179656 | tf_op jit(solution)/shard_map/ppermute | solution.py:90
  234.0 12.1 %collective-permute-start.36 = (bf16[128,1536]{1,0:T(8,128)(2,1)S(1)}, bf16[128,1536]{1,0:T(8,128)(2,1)S(1)}, u32[]{:S(2)}, u32[]{:S(2)}) collective-permute-start(bf16[128,1536]{1,0:T(8,128)(2,1)S(1)} %get-tuple-element.72), channel_id=1, source_target_pairs={{0,8},{8,0},{16,24},{24,16},{1,9},{9,1},{17,25},{25,17},{2,10},{10... | collective-permute-start | bytes 1179656 | tf_op jit(solution)/shard_map/ppermute | solution.py:90
  235.6 17.2 %collective-permute-start.38 = (bf16[128,1536]{1,0:T(8,128)(2,1)S(1)}, bf16[128,1536]{1,0:T(8,128)(2,1)S(1)}, u32[]{:S(2)}, u32[]{:S(2)}) collective-permute-start(bf16[128,1536]{1,0:T(8,128)(2,1)S(1)} %get-tuple-element.73), channel_id=1, source_target_pairs={{0,24},{8,16},{16,8},{24,0},{1,25},{9,17},{17,9},{25,1},{2,26},{10... | collective-permute-start | bytes 1179656 | tf_op jit(solution)/shard_map/ppermute | solution.py:90
  236.1 18.0 %collective-permute-start.37 = (bf16[128,1536]{1,0:T(8,128)(2,1)S(1)}, bf16[128,1536]{1,0:T(8,128)(2,1)S(1)}, u32[]{:S(2)}, u32[]{:S(2)}) collective-permute-start(bf16[128,1536]{1,0:T(8,128)(2,1)S(1)} %get-tuple-element.74), channel_id=1, source_target_pairs={{0,16},{8,24},{16,0},{24,8},{1,17},{9,25},{17,1},{25,9},{2,18},{10... | collective-permute-start | bytes 1179656 | tf_op jit(solution)/shard_map/ppermute | solution.py:90
  255.3 13.0 %collective-permute-start.41 = (bf16[128,1536]{1,0:T(8,128)(2,1)S(1)}, bf16[128,1536]{1,0:T(8,128)(2,1)S(1)}, u32[]{:S(2)}, u32[]{:S(2)}) collective-permute-start(bf16[128,1536]{1,0:T(8,128)(2,1)S(1)} %fusion.81), channel_id=1, source_target_pairs={{0,24},{8,16},{16,8},{24,0},{1,25},{9,17},{17,9},{25,1},{2,26},{10... | collective-permute-start | bytes 1179656 | tf_op jit(solution)/shard_map/ppermute | solution.py:90
  257.8 14.8 %collective-permute-start.40 = (bf16[128,1536]{1,0:T(8,128)(2,1)S(1)}, bf16[128,1536]{1,0:T(8,128)(2,1)S(1)}, u32[]{:S(2)}, u32[]{:S(2)}) collective-permute-start(bf16[128,1536]{1,0:T(8,128)(2,1)S(1)} %fusion.81), channel_id=1, source_target_pairs={{0,16},{8,24},{16,0},{24,8},{1,17},{9,25},{17,1},{25,9},{2,18},{10... | collective-permute-start | bytes 1179656 | tf_op jit(solution)/shard_map/ppermute | solution.py:90
  258.3 14.3 %collective-permute-start.39 = (bf16[128,1536]{1,0:T(8,128)(2,1)S(1)}, bf16[128,1536]{1,0:T(8,128)(2,1)S(1)}, u32[]{:S(2)}, u32[]{:S(2)}) collective-permute-start(bf16[128,1536]{1,0:T(8,128)(2,1)S(1)} %fusion.81), channel_id=1, source_target_pairs={{0,8},{8,0},{16,24},{24,16},{1,9},{9,1},{17,25},{25,17},{2,10},{10... | collective-permute-start | bytes 1179656 | tf_op jit(solution)/shard_map/ppermute | solution.py:90
  281.3 10.9 %collective-permute-start.51 = (bf16[4,4,48,768]{3,2,0,1:T(8,128)(2,1)S(1)}, bf16[4,4,48,768]{3,2,0,1:T(8,128)(2,1)S(1)}, u32[]{:S(2)}, u32[]{:S(2)}) collective-permute-start(bf16[4,4,48,768]{3,2,0,1:T(8,128)(2,1)S(1)} %bitcast.273), channel_id=1, source_target_pairs={{0,4},{4,0},{1,5},{5,1},{2,6},{6,2},{3,7},{7,3},{8,12},{12,8},{9,1... | collective-permute-start | bytes 3538952 | tf_op jit(solution)/shard_map/ppermute | solution.py:87
  293.4 80.3 %reduce-scatter.7.cloned.1.call-start = ((), (), s32[]{:S(2)}) async-start(), calls=%async_computation.8 | async-start | bytes 737280 | tf_op jit(solution)/shard_map/reduce_scatter | solution.py:234
  299.8 105.9 %reduce-scatter.9.cloned.1.call-start = ((), (), s32[]{:S(2)}) async-start(), calls=%async_computation.9 | async-start | bytes 3932160 | tf_op jit(solution)/shard_map/reduce_scatter | solution.py:227
  304.8 138.7 %reduce-scatter.11.cloned.1.call-start = ((), (), s32[]{:S(2)}) async-start(), calls=%async_computation.10 | async-start | bytes 1966080 | tf_op jit(solution)/shard_map/reduce_scatter | solution.py:234
  310.6 12.1 %collective-permute-start.42 = (bf16[128,1536]{1,0:T(8,128)(2,1)S(1)}, bf16[128,1536]{1,0:T(8,128)(2,1)S(1)}, u32[]{:S(2)}, u32[]{:S(2)}) collective-permute-start(bf16[128,1536]{1,0:T(8,128)(2,1)S(1)} %get-tuple-element.69), channel_id=1, source_target_pairs={{0,8},{8,0},{16,24},{24,16},{1,9},{9,1},{17,25},{25,17},{2,10},{10... | collective-permute-start | bytes 1179656 | tf_op jit(solution)/shard_map/ppermute | solution.py:90
  312.1 19.1 %collective-permute-start.44 = (bf16[128,1536]{1,0:T(8,128)(2,1)S(1)}, bf16[128,1536]{1,0:T(8,128)(2,1)S(1)}, u32[]{:S(2)}, u32[]{:S(2)}) collective-permute-start(bf16[128,1536]{1,0:T(8,128)(2,1)S(1)} %get-tuple-element.70), channel_id=1, source_target_pairs={{0,24},{8,16},{16,8},{24,0},{1,25},{9,17},{17,9},{25,1},{2,26},{10... | collective-permute-start | bytes 1179656 | tf_op jit(solution)/shard_map/ppermute | solution.py:90
  313.6 19.0 %collective-permute-start.43 = (bf16[128,1536]{1,0:T(8,128)(2,1)S(1)}, bf16[128,1536]{1,0:T(8,128)(2,1)S(1)}, u32[]{:S(2)}, u32[]{:S(2)}) collective-permute-start(bf16[128,1536]{1,0:T(8,128)(2,1)S(1)} %get-tuple-element.71), channel_id=1, source_target_pairs={{0,16},{8,24},{16,0},{24,8},{1,17},{9,25},{17,1},{25,9},{2,18},{10... | collective-permute-start | bytes 1179656 | tf_op jit(solution)/shard_map/ppermute | solution.py:90
  333.3 29.1 %collective-permute-start.60 = (bf16[512,1536]{1,0:T(8,128)(2,1)S(1)}, bf16[512,1536]{1,0:T(8,128)(2,1)S(1)}, u32[]{:S(2)}, u32[]{:S(2)}) collective-permute-start(bf16[512,1536]{1,0:T(8,128)(2,1)S(1)} %dynamic-slice_bitcast_fusion), channel_id=1, source_target_pairs={{0,4},{4,0},{1,5},{5,1},{2,6},{6,2},{3,7},{7,3},{8,12},{12,8},{9,1... | collective-permute-start | bytes 4718600 | tf_op jit(solution)/shard_map/ppermute | solution.py:87
  335.3 21.9 %collective-permute-start.29 = (bf16[128,1536]{1,0:T(8,128)(2,1)S(1)}, bf16[128,1536]{1,0:T(8,128)(2,1)S(1)}, u32[]{:S(2)}, u32[]{:S(2)}) collective-permute-start(bf16[128,1536]{1,0:T(8,128)(2,1)S(1)} %get-tuple-element.75), channel_id=1, source_target_pairs={{0,8},{8,0},{16,24},{24,16},{1,9},{9,1},{17,25},{25,17},{2,10},{10... | collective-permute-start | bytes 1179656 | tf_op jit(solution)/shard_map/ppermute | solution.py:90
  336.6 20.6 %collective-permute-start.31 = (bf16[128,1536]{1,0:T(8,128)(2,1)S(1)}, bf16[128,1536]{1,0:T(8,128)(2,1)S(1)}, u32[]{:S(2)}, u32[]{:S(2)}) collective-permute-start(bf16[128,1536]{1,0:T(8,128)(2,1)S(1)} %get-tuple-element.76), channel_id=1, source_target_pairs={{0,24},{8,16},{16,8},{24,0},{1,25},{9,17},{17,9},{25,1},{2,26},{10... | collective-permute-start | bytes 1179656 | tf_op jit(solution)/shard_map/ppermute | solution.py:90
  338.1 19.1 %collective-permute-start.30 = (bf16[128,1536]{1,0:T(8,128)(2,1)S(1)}, bf16[128,1536]{1,0:T(8,128)(2,1)S(1)}, u32[]{:S(2)}, u32[]{:S(2)}) collective-permute-start(bf16[128,1536]{1,0:T(8,128)(2,1)S(1)} %get-tuple-element.77), channel_id=1, source_target_pairs={{0,16},{8,24},{16,0},{24,8},{1,17},{9,25},{17,1},{25,9},{2,18},{10... | collective-permute-start | bytes 1179656 | tf_op jit(solution)/shard_map/ppermute | solution.py:90
  338.9 18.2 %collective-permute-start.48 = (f32[2,1536]{1,0:T(2,128)S(1)}, f32[2,1536]{1,0:T(2,128)S(1)}, u32[]{:S(2)}, u32[]{:S(2)}) collective-permute-start(f32[2,1536]{1,0:T(2,128)S(1)} %fusion.114), channel_id=1, source_target_pairs={{0,16},{8,24},{16,0},{24,8},{1,17},{9,25},{17,1},{25,9},{2,18},{10... | collective-permute-start | bytes 36872 | tf_op jit(solution)/shard_map/ppermute | solution.py:90
  358.0 10.3 %collective-permute-start.45 = (bf16[64,1536]{1,0:T(8,128)(2,1)S(1)}, bf16[64,1536]{1,0:T(8,128)(2,1)S(1)}, u32[]{:S(2)}, u32[]{:S(2)}) collective-permute-start(bf16[64,1536]{1,0:T(8,128)(2,1)S(1)} %slice.315), channel_id=1, source_target_pairs={{0,4},{4,0},{1,5},{5,1},{2,6},{6,2},{3,7},{7,3},{8,12},{12,8},{9,1... | collective-permute-start | bytes 589832 | tf_op jit(solution)/shard_map/ppermute | solution.py:87
  407.1 38.4 %collective-permute-start.59 = (bf16[48,2048]{1,0:T(8,128)(2,1)S(1)}, bf16[48,2048]{1,0:T(8,128)(2,1)S(1)}, u32[]{:S(2)}, u32[]{:S(2)}) collective-permute-start(bf16[48,2048]{1,0:T(8,128)(2,1)S(1)} %get-tuple-element.90), channel_id=1, source_target_pairs={{0,24},{8,16},{16,8},{24,0},{1,25},{9,17},{17,9},{25,1},{2,26},{10... | collective-permute-start | bytes 589832 | tf_op jit(solution)/shard_map/ppermute | solution.py:90
  409.6 35.9 %collective-permute-start.58 = (bf16[48,2048]{1,0:T(8,128)(2,1)S(1)}, bf16[48,2048]{1,0:T(8,128)(2,1)S(1)}, u32[]{:S(2)}, u32[]{:S(2)}) collective-permute-start(bf16[48,2048]{1,0:T(8,128)(2,1)S(1)} %get-tuple-element.91), channel_id=1, source_target_pairs={{0,16},{8,24},{16,0},{24,8},{1,17},{9,25},{17,1},{25,9},{2,18},{10... | collective-permute-start | bytes 589832 | tf_op jit(solution)/shard_map/ppermute | solution.py:90
  410.1 35.4 %collective-permute-start.57 = (bf16[48,2048]{1,0:T(8,128)(2,1)S(1)}, bf16[48,2048]{1,0:T(8,128)(2,1)S(1)}, u32[]{:S(2)}, u32[]{:S(2)}) collective-permute-start(bf16[48,2048]{1,0:T(8,128)(2,1)S(1)} %get-tuple-element.92), channel_id=1, source_target_pairs={{0,8},{8,0},{16,24},{24,16},{1,9},{9,1},{17,25},{25,17},{2,10},{10... | collective-permute-start | bytes 589832 | tf_op jit(solution)/shard_map/ppermute | solution.py:90
  (94 other events, 713.9 us)
Sparse Core Ops, SparseCore 0:
  20.2 38.3 all-gather.3
  60.1 36.2 all-gather.7
  98.6 62.2 all-gather.5
  293.5 27.4 reduce-scatter.4
  323.7 20.7 reduce-scatter.6
  346.7 59.0 reduce-scatter.8
  408.1 35.3 reduce-scatter.10

commit v2 on v1

--- a/solution.py
+++ b/solution.py
@@ -79,7 +79,7 @@
     d_rows = w_query.shape[0]
     q_cols = w_query.shape[1] // chips
     kv_cols = w_key.shape[1] // chips
-    ff_cols = w_gate.shape[1] // chips
+    ff_cols = w_gate.shape[1] // (2 * chips)
     kv_heads = KV_HEADS // chips
     factor = HEAD ** (-0.5)
 
@@ -118,10 +118,12 @@
             pieces.append(chip_xor(pick(pack, chip ^ j), j))
         return by_chip(pieces)
 
+    def core_pair(mine, other, axis):
+        first = core == 0
+        return jnp.stack([jnp.where(first, mine, other), jnp.where(first, other, mine)], axis)
+
     def both_cores(a):
-        other = core_swap(a)
-        first = core == 0
-        return jnp.where(first, a, other), jnp.where(first, other, a)
+        return core_pair(a, core_swap(a), 0)
 
     def chip_slices(weights, cols):
         return jnp.stack(
@@ -131,51 +133,94 @@
             ]
         )
 
-    def fetch_columns(pack):
-        mine = exchange_chips(pack)
-        cols = mine.shape[-1]
-        along = lax.all_gather(mine.reshape(-1, cols), "fsdp", axis=0, tiled=True)
-        along = along.reshape(rows_z, chips, d_rows, cols)
-        zero, one = both_cores(along)
-        full = jnp.stack([zero, one])
+    def after(value, *others):
+        return lax.optimization_barrier((value,) + others)[0]
+
+    def along_z(a, step):
+        return lax.ppermute(a, "fsdp", [(i, (i + step) % rows_z) for i in range(rows_z)])
+
+    def ring_gather(a):
+        found = {0: a}
+        right, left = a, a
+        for step in range(1, rows_z // 2 + 1):
+            if 2 * step == rows_z:
+                half = a.shape[-1] // 2
+                low = along_z(right[..., :half], 1)
+                high = along_z(left[..., half:], -1)
+                found[step] = jnp.concatenate([low, high], axis=-1)
+            else:
+                right, left = along_z(right, 1), along_z(left, -1)
+                found[rows_z - step], found[step] = right, left
+        return jnp.stack([found[step] for step in range(rows_z)])
+
+    def by_place(a):
+        doubled = jnp.concatenate([a, a])
+        return lax.dynamic_slice_in_dim(doubled, rows_z - place, rows_z, 0)
+
+    def order_columns(along):
+        cols = along.shape[-1]
+        full = both_cores(along.reshape(rows_z, chips, d_rows, cols))
         return jnp.transpose(full, (2, 0, 1, 3, 4)).reshape(chips * 2 * rows_z * d_rows, cols)
-
-    def fetch_rows(weight):
-        along = lax.all_gather(weight, "fsdp", axis=0, tiled=True)
-        return jnp.concatenate(both_cores(along), axis=0)
 
     pair = jnp.stack([block_input[:, 0], out_cotangent[:, 0]], axis=1)
     pair = jnp.concatenate([pick(pair, core), core_swap(pick(pair, 1 - core))], axis=1)
     x_low, dy_low = pair[0], pair[1]
-    marks = jnp.stack([positions[:, 0], segments[:, 0]], axis=1)
-    marks = jnp.concatenate([pick(marks, core), core_swap(pick(marks, 1 - core))], axis=1)
 
     owner = (chip * 2 + core) * rows_z + place
-    gains = jnp.zeros((2, width), bf16)
+    spot = chip * 2 + core
     gains = lax.dynamic_update_slice(
-        gains, jnp.stack([attn_gain, mlp_gain]), (0, owner * d_rows)
-    )
-
-    def sum_everywhere(a):
+        jnp.zeros((2, width), f32),
+        jnp.stack([attn_gain, mlp_gain]).astype(f32),
+        (0, owner * d_rows),
+    )
+    marks = lax.dynamic_update_slice(
+        jnp.zeros((4, chips * 2 * tok), f32),
+        jnp.concatenate([positions[:, 0], segments[:, 0]]).astype(f32),
+        (0, spot * tok),
+    )
+    table = jnp.concatenate([gains.reshape(-1), marks.reshape(-1)]).reshape(-1, 128)
+
+    def sum_plane(a):
         a = a + core_swap(a)
         bit = 1
         while bit < chips:
             a = a + chip_xor(a, bit)
             bit *= 2
+        return a
+
+    def sum_z(a):
         bit = 1
         while bit < rows_z:
             a = a + lax.ppermute(a, "fsdp", [(i, i ^ bit) for i in range(rows_z)])
             bit *= 2
         return a
 
-    w_qkv = fetch_columns(chip_slices((w_query, w_key, w_value), (q_cols, kv_cols, kv_cols)))
+    pack_qkv = chip_slices((w_query, w_key, w_value), (q_cols, kv_cols, kv_cols))
+    piece_qkv = exchange_chips(pack_qkv).reshape(-1, pack_qkv.shape[-1])
+    out_rel = ring_gather(w_out)
+    qkv_rel = ring_gather(piece_qkv)
+    along_down = lax.all_gather(w_down, "fsdp", axis=0, tiled=True)
     x_all = gather_chips(x_low)
-    marks_all = gather_chips(marks, axis=1)
-    gains = sum_everywhere(gains).astype(f32)
-    gain_one, gain_two = gains[0], gains[1]
-    out_w = fetch_rows(w_out)
-    w_gu = fetch_columns(chip_slices((w_gate, w_up), (ff_cols, ff_cols)))
-    down_w = fetch_rows(w_down)
+    w_qkv = order_columns(by_place(qkv_rel))
+    out_w = both_cores(by_place(out_rel)).reshape(-1, width)
+    pack_gu = jnp.stack(
+        [
+            jnp.concatenate([w[:, n * ff_cols : (n + 1) * ff_cols] for w in (w_gate, w_up)], axis=1)
+            for n in range(2 * chips)
+        ]
+    ).reshape(chips, 2, d_rows, 2 * ff_cols)
+    piece_gu = exchange_chips(after(pack_gu, piece_qkv))
+    piece_gu = core_pair(pick(piece_gu, core, 1), core_swap(pick(piece_gu, 1 - core, 1)), 1)
+    along_gu = lax.all_gather(
+        piece_gu.reshape(2 * chips * d_rows, 2 * ff_cols), "fsdp", axis=0, tiled=True
+    )
+    table = sum_plane(table).reshape(-1)
+    gain_one, gain_two = sum_z(table[: 2 * width].reshape(2, width))
+    marks = table[2 * width :].reshape(2, 2, chips, 2, tok)
+    marks = pick(marks, core, 1)
+    marks = jnp.where(core == 0, marks, jnp.flip(marks, axis=2)).reshape(2, chips, 2 * tok)
+    marks_all = by_chip([marks[:, k] for k in range(chips)])
+    marks_all = jnp.transpose(marks_all, (1, 0, 2)).reshape(2, chips * 2 * tok)
     dy_all = gather_chips(dy_low)
     own = x_low.shape[0]
     seq = x_all.shape[0]
@@ -205,17 +250,47 @@
     scale_two = rms_scale(middle)
     n_two = middle * scale_two
     h_two = gather_chips((n_two * gain_two).astype(bf16))
-    gu = mm(h_two, w_gu)
-    gate, up = gu[:, :ff_cols], gu[:, ff_cols:]
-    sigma = jax.nn.sigmoid(gate)
-    act = (gate * sigma * up).astype(bf16)
-    result = (middle + scatter_chips(mm(act, down_w))).astype(bf16)
-
-    d_act = mm_nt(dy_all, down_w)
-    d_gate = (d_act * up * sigma * (1.0 + gate * (1.0 - sigma))).astype(bf16)
-    d_up = (d_act * gate * sigma).astype(bf16)
-    d_gu = jnp.concatenate([d_gate, d_up], axis=1)
-    d_h_two = scatter_chips(mm_nt(d_gu, w_gu))
+    dy_other = core_swap(dy_all)
+    h_two, along_down, along_gu = lax.optimization_barrier((h_two, along_down, along_gu))
+    h_other = core_swap(h_two)
+    down_w = along_down
+    w_gu = along_gu.reshape(rows_z, 2 * chips, d_rows, 2 * ff_cols)
+    w_gu = jnp.transpose(w_gu, (1, 0, 2, 3)).reshape(width, 2 * ff_cols)
+
+    def mlp_forward(h):
+        gu = mm(h, w_gu)
+        gate, up = gu[:, :ff_cols], gu[:, ff_cols:]
+        sigma = jax.nn.sigmoid(gate)
+        return gate, up, sigma, (gate * sigma * up).astype(bf16)
+
+    def mlp_backward(dy, gate, up, sigma):
+        d_act = mm_nt(dy, down_w)
+        d_gate = (d_act * up * sigma * (1.0 + gate * (1.0 - sigma))).astype(bf16)
+        d_up = (d_act * gate * sigma).astype(bf16)
+        return jnp.concatenate([d_gate, d_up], axis=1)
+
+    def give_partial(other_part, own_part):
+        return scatter_chips(own_part + core_swap(other_part.astype(bf16)).astype(f32))
+
+    *keep, act = mlp_forward(h_two)
+    *keep_other, act_other = mlp_forward(h_other)
+    d_gu_other = mlp_backward(dy_other, *keep_other)
+    d_gu = mlp_backward(dy_all, *keep)
+    d_h_two = give_partial(mm_nt(d_gu_other, w_gu), mm_nt(d_gu, w_gu))
+    result = middle + give_partial(mm(act_other, down_w), mm(act, down_w))
+    result = result.astype(bf16)
+
+    act_both = jnp.concatenate([act, act_other])
+    dy_both = jnp.concatenate([dy_all, dy_other])
+    g_down = mm_tn(act_both, dy_both).astype(bf16)
+    g_down = lax.psum_scatter(g_down, "fsdp", scatter_dimension=0, tiled=True).astype(f32)
+    g_gu = mm_tn(jnp.concatenate([h_two, h_other]), jnp.concatenate([d_gu, d_gu_other]))
+    g_gu = g_gu.astype(bf16).reshape(2 * chips, rows_z, d_rows, 2 * ff_cols)
+    g_gu = jnp.transpose(g_gu, (1, 0, 2, 3)).reshape(width, 2 * ff_cols)
+    g_gu = lax.psum_scatter(g_gu, "fsdp", scatter_dimension=0, tiled=True)
+    g_gu = g_gu.reshape(chips, 2, d_rows, 2 * ff_cols)
+    g_gu = core_pair(pick(g_gu, core, 1), core_swap(pick(g_gu, 1 - core, 1)), 1)
+    g_gu = exchange_chips(g_gu)
 
     def reduce_columns(left, right):
         grad = mm_tn(left, right).astype(bf16)
@@ -233,8 +308,6 @@
         total = pick(grad, core) + core_swap(pick(grad, 1 - core))
         return lax.psum_scatter(total, "fsdp", scatter_dimension=0, tiled=True).astype(f32)
 
-    g_gu = reduce_columns(h_two, d_gu)
-    g_down = reduce_rows(act, dy_all)
     dy_own = dy_low.astype(f32)
     gain_two_part = jnp.sum(d_h_two * n_two, axis=0)
     d_middle = dy_own + norm_back(d_h_two * gain_two, n_two, scale_two)
@@ -274,7 +347,11 @@
         part = grad[:, :, start : start + cols].astype(f32)
         return jnp.transpose(part, (1, 0, 2)).reshape(d_rows, chips * cols)
 
-    gain_parts = sum_everywhere(jnp.stack([gain_one_part, gain_two_part]))
+    def spread_ff(grad):
+        grad = jnp.transpose(grad.astype(f32), (2, 0, 1, 3))
+        return grad.reshape(d_rows, 2 * chips * ff_cols)
+
+    gain_parts = sum_z(sum_plane(jnp.stack([gain_one_part, gain_two_part])))
     gain_parts = lax.dynamic_slice_in_dim(gain_parts, owner * d_rows, d_rows, 1)
     return (
         give_back(result),
@@ -285,8 +362,8 @@
         spread(g_qkv, q_cols + kv_cols, kv_cols),
         g_out,
         gain_parts[1],
-        spread(g_gu, 0, ff_cols),
-        spread(g_gu, ff_cols, ff_cols),
+        spread_ff(g_gu[..., :ff_cols]),
+        spread_ff(g_gu[..., ff_cols:]),
         g_down,
     )
 

time: 460 us -> 436 us (0.948)
  waiting for transfers between devices: 258 us -> 226 us
  blocking collectives: 24.5 us -> 0 us
  matrix products: 41.1 us -> 52.1 us
  local copies, waits for them, and re-layouts: 27 us -> 37.6 us
    all_gather x3 -> x2, waiting for transfers between devices: 57.9 us -> 0.01 us  [the longest x1 0.01 us: on_device(): along_down = lax.all_gather(w_down, 'fsdp', axis=0, tiled=True)]
    reduce_scatter x0 -> x2, waiting for transfers between devices: none -> 55.4 us  [the longest x1 55.4 us: on_device(): g_gu = lax.psum_scatter(g_gu, 'fsdp', scatter_dimension=0, tiled=True)]
    reduce_scatter x2 -> x1, waiting for transfers between devices: 30.9 us -> 0.01 us  [reduce_rows(): lax.psum_scatter(total, 'fsdp', scatter_dimension=0, tiled=True).astype(f32)]
    reduce_scatter x2 -> x1, waiting for transfers between devices: 27.9 us -> 0.02 us  [reduce_columns(): total = lax.psum_scatter(total, 'fsdp', scatter_dimension=0, tiled=True)]
    all_gather x1 -> x0, blocking collectives: 24.5 us -> none  [fetch_rows(): along = lax.all_gather(weight, 'fsdp', axis=0, tiled=True)]
    ppermute x4 -> x12, waiting for transfers between devices: 9.9 us -> 30.3 us  [the longest x4 24.3 us: sum_z(): a = a + lax.ppermute(a, 'fsdp', [(i, i ^ bit) for i in range(rows_z)])]
    ppermute x4 -> x12, starting transfers between devices: 3.98 us -> 15.8 us  [the longest x8 14.9 us: along_z(): lax.ppermute(a, 'fsdp', [(i, (i + step) % rows_z) for i in range(rows_z)])]
    ppermute x43 -> x40, starting transfers between devices: 52.4 us -> 45 us  [chip_xor(): return lax.ppermute(a, 'chip', [(i, i ^ j) for i in range(chips)])]
  transfers between devices with their start and end apart: 68 -> 73, of which waited for: 36 -> 35; matrix products, arithmetic and copies ran while one was open for 15% -> 23% of each run, Pallas kernels for 0% -> 0%
where the time goes in v2:
time: 436 us; the launch traced here: 430 us
  waiting for transfers between devices  226 us (52%)
  starting transfers between devices  63.7 us (15%)
  matrix products  52.1 us (12%)
  local copies, waits for them, and re-layouts  37.6 us (9%)
  other arithmetic  34.2 us (8%)
  between operations  16.2 us (4%)
    ppermute x40, waiting for transfers between devices, chip_xor(): return lax.ppermute(a, 'chip', [(i, i ^ j) for i in range(chips)])  134 us
    reduce_scatter x1, waiting for transfers between devices, on_device(): g_gu = lax.psum_scatter(g_gu, 'fsdp', scatter_dimension=0, tiled=True)  55.4 us
    ppermute x40, starting transfers between devices, chip_xor(): return lax.ppermute(a, 'chip', [(i, i ^ j) for i in range(chips)])  45 us
    ppermute x4, waiting for transfers between devices, sum_z(): a = a + lax.ppermute(a, 'fsdp', [(i, i ^ bit) for i in range(rows_z)])  24.3 us
    dot_general x4, matrix products, mm_tn(): return jnp.einsum('td,te->de', a, b, preferred_element_type=f32)  15.7 us
    ppermute x8, starting transfers between devices, along_z(): lax.ppermute(a, 'fsdp', [(i, (i + step) % rows_z) for i in range(rows_z)])  14.9 us
    dot_general x6, matrix products, mm(): return jnp.dot(a, b, preferred_element_type=f32)  13.2 us
    dot_general x6, matrix products, mm_nt(): return jnp.einsum('te,de->td', a, b, preferred_element_type=f32)  12.9 us
  transfers between devices with their start and end apart: 73, of which 35 were waited for; matrix products, arithmetic and copies ran while one was open for 23% of the time, Pallas kernels for 0%

profile of v2, /device:TPU:0, one launch (start us, length us, event | category | flops | bytes accessed | tf_op | source)
XLA Modules:
  0.0 429.7 jit_solution(15173345791217843258)
XLA Ops:
  7.3 3.1 collective-permute-start.18
  10.4 2.1 collective-permute-start.17
  27.9 3.2 collective-permute-done.5
  32.3 3.3 collective-permute-done.6
  38.5 2.6 collective-permute-done.11
  42.2 1.9 collective-permute-start.12
  44.4 17.6 %collective-permute-done.8 = f32[2,1536]{1,0:T(2,128)S(1)} collective-permute-done((f32[2,1536]{1,0:T(2,128)S(1)}, f32[2,1536]{1,0:T(2,128)S(1)}, u32[]{:S(2)}, u32[]{:S(2)}) %collective-permute-start.8) | collective-permute-done | bytes 12320 | tf_op jit(solution)/shard_map/ppermute | solution.py:194
  65.3 3.8 collective-permute-start.20
  76.4 3.8 collective-permute-done.29
  81.5 4.1 collective-permute-done.13
  85.7 3.9 collective-permute-start.15
  97.3 5.0 %collective-permute-done.1 = bf16[128,1536]{1,0:T(8,128)(2,1)} collective-permute-done((bf16[128,1536]{1,0:T(8,128)(2,1)S(1)}, bf16[128,1536]{1,0:T(8,128)(2,1)}, u32[]{:S(2)}, u32[]{:S(2)}) %collective-permute-start.1) | collective-permute-done | bytes 393248 | tf_op jit(solution)/shard_map/ppermute | solution.py:90
  102.4 6.0 %collective-permute-done.2 = bf16[128,1536]{1,0:T(8,128)(2,1)} collective-permute-done((bf16[128,1536]{1,0:T(8,128)(2,1)S(1)}, bf16[128,1536]{1,0:T(8,128)(2,1)}, u32[]{:S(2)}, u32[]{:S(2)}) %collective-permute-start.2) | collective-permute-done | bytes 393248 | tf_op jit(solution)/shard_map/ppermute | solution.py:90
  113.2 3.6 fusion.63
  122.5 4.8 %fusion.133 = (f32[2,2,512]{2,1,0:T(2,128)S(1)}, f32[2,2,512,512]{2,3,1,0:T(8,128)}) fusion(pred[512,512]{0,1:T(8,128)(4,1)} %compare_and_fusion, bf16[512,2,2,48]{0,3,2,1:T(8,128)(2,1)S(1)} %bitcast.403, bf16[512,2,2,48]{0,3,2,1:T(8,128)(2,1)S(1)} %bitcast.401, bf16[512,2,48]{0,2,1:T(8,128)(2,1)S(1)} %get-tuple-element.121, ...), kind=kOutput, calls=%fused_computation.311 | convolution fusion | flops 206701056 | bytes 5054464 | tf_op jit(solution)/shard_map/sub | solution.py:242
  127.4 2.7 convolution_convert_fusion.6
  134.8 4.8 %collective-permute-done.22 = bf16[128,1536]{1,0:T(8,128)(2,1)S(1)} collective-permute-done((bf16[128,1536]{1,0:T(8,128)(2,1)S(1)}, bf16[128,1536]{1,0:T(8,128)(2,1)S(1)}, u32[]{:S(2)}, u32[]{:S(2)}) %collective-permute-start.22) | collective-permute-done | bytes 393248 | tf_op jit(solution)/shard_map/ppermute | solution.py:90
  139.5 7.3 %collective-permute-done.23 = bf16[128,1536]{1,0:T(8,128)(2,1)S(1)} collective-permute-done((bf16[128,1536]{1,0:T(8,128)(2,1)S(1)}, bf16[128,1536]{1,0:T(8,128)(2,1)S(1)}, u32[]{:S(2)}, u32[]{:S(2)}) %collective-permute-start.23) | collective-permute-done | bytes 393248 | tf_op jit(solution)/shard_map/ppermute | solution.py:90
  146.8 2.0 collective-permute-done.24
  150.8 2.1 collective-permute-start.27
  155.1 6.3 %collective-permute-done.25 = bf16[128,1536]{1,0:T(8,128)(2,1)S(1)} collective-permute-done((bf16[128,1536]{1,0:T(8,128)(2,1)S(1)}, bf16[128,1536]{1,0:T(8,128)(2,1)S(1)}, u32[]{:S(2)}, u32[]{:S(2)}) %collective-permute-start.25) | collective-permute-done | bytes 393248 | tf_op jit(solution)/shard_map/ppermute | solution.py:90
  162.2 8.2 %collective-permute-done.26 = bf16[128,1536]{1,0:T(8,128)(2,1)S(1)} collective-permute-done((bf16[128,1536]{1,0:T(8,128)(2,1)S(1)}, bf16[128,1536]{1,0:T(8,128)(2,1)S(1)}, u32[]{:S(2)}, u32[]{:S(2)}) %collective-permute-start.26) | collective-permute-done | bytes 393248 | tf_op jit(solution)/shard_map/ppermute | solution.py:90
  173.4 7.0 %collective-permute-done.39 = bf16[128,1536]{1,0:T(8,128)(2,1)S(1)} collective-permute-done((bf16[128,1536]{1,0:T(8,128)(2,1)S(1)}, bf16[128,1536]{1,0:T(8,128)(2,1)S(1)}, u32[]{:S(2)}, u32[]{:S(2)}) %collective-permute-start.39) | collective-permute-done | bytes 393248 | tf_op jit(solution)/shard_map/ppermute | solution.py:90
  185.1 2.2 multiply_convert_fusion.1
  190.3 2.2 fusion.137
  192.5 3.2 multiply_convert_fusion.3
  201.2 8.5 %collective-permute-done.43 = bf16[128,1536]{1,0:T(8,128)(2,1)S(1)} collective-permute-done((bf16[128,1536]{1,0:T(8,128)(2,1)S(1)}, bf16[128,1536]{1,0:T(8,128)(2,1)S(1)}, u32[]{:S(2)}, u32[]{:S(2)}) %collective-permute-start.43) | collective-permute-done | bytes 393248 | tf_op jit(solution)/shard_map/ppermute | solution.py:90
  209.7 8.3 %collective-permute-done.44 = bf16[128,1536]{1,0:T(8,128)(2,1)S(1)} collective-permute-done((bf16[128,1536]{1,0:T(8,128)(2,1)S(1)}, bf16[128,1536]{1,0:T(8,128)(2,1)S(1)}, u32[]{:S(2)}, u32[]{:S(2)}) %collective-permute-start.44) | collective-permute-done | bytes 393248 | tf_op jit(solution)/shard_map/ppermute | solution.py:90
  222.9 8.5 %collective-permute-done.46 = bf16[128,1536]{1,0:T(8,128)(2,1)S(1)} collective-permute-done((bf16[128,1536]{1,0:T(8,128)(2,1)S(1)}, bf16[128,1536]{1,0:T(8,128)(2,1)S(1)}, u32[]{:S(2)}, u32[]{:S(2)}) %collective-permute-start.46) | collective-permute-done | bytes 393248 | tf_op jit(solution)/shard_map/ppermute | solution.py:90
  231.4 6.0 %collective-permute-done.47 = bf16[128,1536]{1,0:T(8,128)(2,1)S(1)} collective-permute-done((bf16[128,1536]{1,0:T(8,128)(2,1)S(1)}, bf16[128,1536]{1,0:T(8,128)(2,1)S(1)}, u32[]{:S(2)}, u32[]{:S(2)}) %collective-permute-start.47) | collective-permute-done | bytes 393248 | tf_op jit(solution)/shard_map/ppermute | solution.py:90
  245.0 2.8 convolution_convert_fusion.1
  248.2 2.8 collective-permute-done.58
  257.0 5.1 %convolution_convert_fusion.3 = bf16[512,1536]{1,0:T(8,128)(2,1)} fusion(bf16[1024,1536]{1,0:T(8,128)(2,1)} %constant_dynamic-update-slice_fusion.4, bf16[512,512]{1,0:T(8,128)(2,1)S(1)} %copy-done.70, bf16[512,512]{1,0:T(8,128)(2,1)S(1)} %copy-done.26), kind=kOutput, calls=%fused_computation.22 | convolution fusion | flops 1613496320 | bytes 5767168 | tf_op jit(solution)/shard_map/td,te->de/dot_general | solution.py:50
  262.2 2.0 convolution_convert_fusion.5
  267.5 5.8 %convolution_convert_fusion = bf16[1536,1024]{1,0:T(8,128)(2,1)S(1)} fusion(bf16[512,1536]{1,0:T(8,128)(2,1)} %copy-done.64, bf16[512,1536]{1,0:T(8,128)(2,1)} %pad_maximum_fusion.1, bf16[512,512]{1,0:T(8,128)(2,1)} %copy-done.76, bf16[512,512]{1,0:T(8,128)(2,1)} %copy-done.75, bf16[512,512]{1,0:T(8,128)(2,1)} %copy-done.74, bf16[512,512]{1,0:T(8,128)(2,1)S(1)} %copy-done.73), kind=kOutput, calls=%fused_computation.10 | convolution fusion | flops 3237478400 | bytes 8388608 | tf_op jit(solution)/shard_map/td,te->de/dot_general | solution.py:50
  273.3 2.0 copy.100
  275.5 2.2 convolution_convert_fusion.2
  278.8 3.1 fusion.136
  285.6 8.5 %collective-permute-done.49 = bf16[128,1536]{1,0:T(8,128)(2,1)S(1)} collective-permute-done((bf16[128,1536]{1,0:T(8,128)(2,1)S(1)}, bf16[128,1536]{1,0:T(8,128)(2,1)S(1)}, u32[]{:S(2)}, u32[]{:S(2)}) %collective-permute-start.49) | collective-permute-done | bytes 393248 | tf_op jit(solution)/shard_map/ppermute | solution.py:90
  294.1 7.2 %collective-permute-done.50 = bf16[128,1536]{1,0:T(8,128)(2,1)S(1)} collective-permute-done((bf16[128,1536]{1,0:T(8,128)(2,1)S(1)}, bf16[128,1536]{1,0:T(8,128)(2,1)S(1)}, u32[]{:S(2)}, u32[]{:S(2)}) %collective-permute-start.50) | collective-permute-done | bytes 393248 | tf_op jit(solution)/shard_map/ppermute | solution.py:90
  303.0 2.4 fusion.121
  311.5 15.9 %collective-permute-done.55 = f32[2,1536]{1,0:T(2,128)S(1)} collective-permute-done((f32[2,1536]{1,0:T(2,128)S(1)}, f32[2,1536]{1,0:T(2,128)S(1)}, u32[]{:S(2)}, u32[]{:S(2)}) %collective-permute-start.55) | collective-permute-done | bytes 12320 | tf_op jit(solution)/shard_map/ppermute | solution.py:90
  327.5 3.9 collective-permute-done.56
  333.4 2.8 collective-permute-done.57
  343.1 2.0 convert_element_type.222
  346.8 55.4 %reduce-scatter.9.cloned.1.call-done = bf16[384,1024]{1,0:T(8,128)(2,1)} async-done(((bf16[1536,1024]{1,0:T(8,128)(2,1)}), bf16[384,1024]{1,0:T(8,128)(2,1)}) %reduce-scatter.9.cloned.1.call-update) | async-done | bytes 786448 | tf_op jit(solution)/shard_map/reduce_scatter | solution.py:290
  410.8 2.3 collective-permute-done.64
  413.1 4.5 %collective-permute-done.65 = bf16[2,48,1024]{2,1,0:T(8,128)(2,1)S(1)} collective-permute-done((bf16[2,48,1024]{2,1,0:T(8,128)(2,1)S(1)}, bf16[2,48,1024]{2,1,0:T(8,128)(2,1)S(1)}, u32[]{:S(2)}, u32[]{:S(2)}) %collective-permute-start.65) | collective-permute-done | bytes 196640 | tf_op jit(solution)/shard_map/ppermute | solution.py:90
  (453 shorter events, 134.5 us)
Async XLA Ops:
  7.3 164.4 %all-gather.3.cloned.1.call-start = ((), (), s32[]{:S(2)}) async-start(), calls=%async_computation.4 | async-start | bytes 1966080 | tf_op jit(solution)/shard_map/all_gather | solution.py:202
  7.3 56.2 %collective-permute-start.18 = (bf16[48,1536]{1,0:T(8,128)(2,1)}, bf16[48,1536]{1,0:T(8,128)(2,1)}, u32[]{:S(2)}, u32[]{:S(2)}) collective-permute-start(bf16[48,1536]{1,0:T(8,128)(2,1)} %param.21), channel_id=1, source_target_pairs={{0,1},{1,2},{2,3},{3,0},{4,5},{5,6},{6,7},{7,4},{8,9},{9,10},{10,1... | collective-permute-start | bytes 442376 | tf_op jit(solution)/shard_map/ppermute | solution.py:140
  10.4 54.0 %collective-permute-start.17 = (bf16[48,1536]{1,0:T(8,128)(2,1)}, bf16[48,1536]{1,0:T(8,128)(2,1)}, u32[]{:S(2)}, u32[]{:S(2)}) collective-permute-start(bf16[48,1536]{1,0:T(8,128)(2,1)} %param.21), channel_id=1, source_target_pairs={{0,3},{1,0},{2,1},{3,2},{4,7},{5,4},{6,5},{7,6},{8,11},{9,8},{10,9... | collective-permute-start | bytes 442376 | tf_op jit(solution)/shard_map/ppermute | solution.py:140
  16.2 22.1 %collective-permute-start.9 = (bf16[48,768]{1,0:T(8,128)(2,1)}, bf16[48,768]{1,0:T(8,128)(2,1)}, u32[]{:S(2)}, u32[]{:S(2)}) collective-permute-start(bf16[48,768]{1,0:T(8,128)(2,1)} %get-tuple-element.147), channel_id=1, source_target_pairs={{0,8},{8,0},{16,24},{24,16},{1,9},{9,1},{17,25},{25,17},{2,10},{10... | collective-permute-start | bytes 221192 | tf_op jit(solution)/shard_map/ppermute | solution.py:90
  17.8 20.6 %collective-permute-start.10 = (bf16[48,768]{1,0:T(8,128)(2,1)}, bf16[48,768]{1,0:T(8,128)(2,1)}, u32[]{:S(2)}, u32[]{:S(2)}) collective-permute-start(bf16[48,768]{1,0:T(8,128)(2,1)} %get-tuple-element.146), channel_id=1, source_target_pairs={{0,16},{8,24},{16,0},{24,8},{1,17},{9,25},{17,1},{25,9},{2,18},{10... | collective-permute-start | bytes 221192 | tf_op jit(solution)/shard_map/ppermute | solution.py:90
  20.5 151.3 %all-gather.5.cloned.1.call-start = ((), (), s32[]{:S(2)}) async-start(), calls=%async_computation.5 | async-start | bytes 3932160 | tf_op jit(solution)/shard_map/all_gather | solution.py:214
  38.3 51.3 %collective-permute-start = (bf16[2,64,1536]{2,1,0:T(8,128)(2,1)}, bf16[2,64,1536]{2,1,0:T(8,128)(2,1)S(1)}, u32[]{:S(2)}, u32[]{:S(2)}) collective-permute-start(bf16[2,64,1536]{2,1,0:T(8,128)(2,1)} %get-tuple-element.113), channel_id=1, source_target_pairs={{0,4},{4,0},{1,5},{5,1},{2,6},{6,2},{3,7},{7,3},{8,12},{12,8},{9,1... | collective-permute-start | bytes 1179656 | tf_op jit(solution)/shard_map/ppermute | solution.py:87
  42.2 43.4 %collective-permute-start.12 = (bf16[192,768]{1,0:T(8,128)(2,1)S(1)}, bf16[192,768]{1,0:T(8,128)(2,1)S(1)}, u32[]{:S(2)}, u32[]{:S(2)}) collective-permute-start(bf16[192,768]{1,0:T(8,128)(2,1)S(1)} %bitcast.381), channel_id=1, source_target_pairs={{0,3},{1,0},{2,1},{3,2},{4,7},{5,4},{6,5},{7,6},{8,11},{9,8},{10,9... | collective-permute-start | bytes 884744 | tf_op jit(solution)/shard_map/ppermute | solution.py:140
  44.2 17.8 %collective-permute-start.8 = (f32[2,1536]{1,0:T(2,128)S(1)}, f32[2,1536]{1,0:T(2,128)S(1)}, u32[]{:S(2)}, u32[]{:S(2)}) collective-permute-start(f32[2,1536]{1,0:T(2,128)S(1)} %add.226), channel_id=1, source_target_pairs={{0,2},{1,3},{2,0},{3,1},{4,6},{5,7},{6,4},{7,5},{8,10},{9,11},{10,... | collective-permute-start | bytes 36872 | tf_op jit(solution)/shard_map/ppermute | solution.py:194
  62.0 14.5 %collective-permute-start.28 = (bf16[2,48,1024]{2,1,0:T(8,128)(2,1)S(1)}, bf16[2,48,1024]{2,1,0:T(8,128)(2,1)S(1)}, u32[]{:S(2)}, u32[]{:S(2)}) collective-permute-start(bf16[2,48,1024]{2,1,0:T(8,128)(2,1)S(1)} %get-tuple-element.111), channel_id=1, source_target_pairs={{0,8},{8,0},{16,24},{24,16},{1,9},{9,1},{17,25},{25,17},{2,10},{10... | collective-permute-start | bytes 589832 | tf_op jit(solution)/shard_map/ppermute | solution.py:90
  71.0 9.3 %collective-permute-start.29 = (bf16[2,48,1024]{2,1,0:T(8,128)(2,1)S(1)}, bf16[2,48,1024]{2,1,0:T(8,128)(2,1)S(1)}, u32[]{:S(2)}, u32[]{:S(2)}) collective-permute-start(bf16[2,48,1024]{2,1,0:T(8,128)(2,1)S(1)} %get-tuple-element.110), channel_id=1, source_target_pairs={{0,16},{8,24},{16,0},{24,8},{1,17},{9,25},{17,1},{25,9},{2,18},{10... | collective-permute-start | bytes 589832 | tf_op jit(solution)/shard_map/ppermute | solution.py:90
  76.4 9.2 %collective-permute-start.13 = (bf16[192,768]{1,0:T(8,128)(2,1)S(1)}, bf16[192,768]{1,0:T(8,128)(2,1)S(1)}, u32[]{:S(2)}, u32[]{:S(2)}) collective-permute-start(bf16[192,768]{1,0:T(8,128)(2,1)S(1)} %bitcast.382), channel_id=1, source_target_pairs={{0,1},{1,2},{2,3},{3,0},{4,5},{5,6},{6,7},{7,4},{8,9},{9,10},{10,1... | collective-permute-start | bytes 884744 | tf_op jit(solution)/shard_map/ppermute | solution.py:140
  80.3 29.8 %collective-permute-start.21 = (bf16[4,48,1536]{2,1,0:T(8,128)(2,1)}, bf16[4,48,1536]{2,1,0:T(8,128)(2,1)}, u32[]{:S(2)}, u32[]{:S(2)}) collective-permute-start(bf16[4,48,1536]{2,1,0:T(8,128)(2,1)} %constant_dynamic-slice_fusion.6), channel_id=1, source_target_pairs={{0,4},{4,0},{1,5},{5,1},{2,6},{6,2},{3,7},{7,3},{8,12},{12,8},{9,1... | collective-permute-start | bytes 1769480 | tf_op jit(solution)/shard_map/ppermute | solution.py:87
  80.9 15.0 %collective-permute-start.31 = (bf16[4,48,1024]{2,1,0:T(8,128)(2,1)S(1)}, bf16[4,48,1024]{2,1,0:T(8,128)(2,1)S(1)}, u32[]{:S(2)}, u32[]{:S(2)}) collective-permute-start(bf16[4,48,1024]{2,1,0:T(8,128)(2,1)S(1)} %dynamic-slice_bitcast_fusion.2), channel_id=1, source_target_pairs={{0,4},{4,0},{1,5},{5,1},{2,6},{6,2},{3,7},{7,3},{8,12},{12,8},{9,1... | collective-permute-start | bytes 1179656 | tf_op jit(solution)/shard_map/ppermute | solution.py:87
  90.3 12.1 %collective-permute-start.1 = (bf16[128,1536]{1,0:T(8,128)(2,1)S(1)}, bf16[128,1536]{1,0:T(8,128)(2,1)}, u32[]{:S(2)}, u32[]{:S(2)}) collective-permute-start(bf16[128,1536]{1,0:T(8,128)(2,1)S(1)} %get-tuple-element.62), channel_id=1, source_target_pairs={{0,8},{8,0},{16,24},{24,16},{1,9},{9,1},{17,25},{25,17},{2,10},{10... | collective-permute-start | bytes 1179656 | tf_op jit(solution)/shard_map/ppermute | solution.py:90
  92.7 15.7 %collective-permute-start.2 = (bf16[128,1536]{1,0:T(8,128)(2,1)S(1)}, bf16[128,1536]{1,0:T(8,128)(2,1)}, u32[]{:S(2)}, u32[]{:S(2)}) collective-permute-start(bf16[128,1536]{1,0:T(8,128)(2,1)S(1)} %get-tuple-element.62), channel_id=1, source_target_pairs={{0,16},{8,24},{16,0},{24,8},{1,17},{9,25},{17,1},{25,9},{2,18},{10... | collective-permute-start | bytes 1179656 | tf_op jit(solution)/shard_map/ppermute | solution.py:90
  93.8 14.6 %collective-permute-start.3 = (bf16[128,1536]{1,0:T(8,128)(2,1)S(1)}, bf16[128,1536]{1,0:T(8,128)(2,1)}, u32[]{:S(2)}, u32[]{:S(2)}) collective-permute-start(bf16[128,1536]{1,0:T(8,128)(2,1)S(1)} %get-tuple-element.62), channel_id=1, source_target_pairs={{0,24},{8,16},{16,8},{24,0},{1,25},{9,17},{17,9},{25,1},{2,26},{10... | collective-permute-start | bytes 1179656 | tf_op jit(solution)/shard_map/ppermute | solution.py:90
  95.9 15.4 %collective-permute-start.16 = (bf16[4,4,48,768]{3,2,1,0:T(8,128)(2,1)S(1)}, bf16[4,4,48,768]{3,2,1,0:T(8,128)(2,1)}, u32[]{:S(2)}, u32[]{:S(2)}) collective-permute-start(bf16[4,4,48,768]{3,2,1,0:T(8,128)(2,1)S(1)} %bitcast.359), channel_id=1, source_target_pairs={{0,4},{4,0},{1,5},{5,1},{2,6},{6,2},{3,7},{7,3},{8,12},{12,8},{9,1... | collective-permute-start | bytes 3538952 | tf_op jit(solution)/shard_map/ppermute | solution.py:87
  97.1 240.6 %reduce-scatter.5.cloned.1.call-start = ((), (), s32[]{:S(2)}) async-start(), calls=%async_computation.6 | async-start | bytes 1474560 | tf_op jit(solution)/shard_map/reduce_scatter | solution.py:302
  131.2 8.3 %collective-permute-start.22 = (bf16[128,1536]{1,0:T(8,128)(2,1)S(1)}, bf16[128,1536]{1,0:T(8,128)(2,1)S(1)}, u32[]{:S(2)}, u32[]{:S(2)}) collective-permute-start(bf16[128,1536]{1,0:T(8,128)(2,1)S(1)} %get-tuple-element.87), channel_id=1, source_target_pairs={{0,8},{8,0},{16,24},{24,16},{1,9},{9,1},{17,25},{25,17},{2,10},{10... | collective-permute-start | bytes 1179656 | tf_op jit(solution)/shard_map/ppermute | solution.py:90
  132.6 14.2 %collective-permute-start.23 = (bf16[128,1536]{1,0:T(8,128)(2,1)S(1)}, bf16[128,1536]{1,0:T(8,128)(2,1)S(1)}, u32[]{:S(2)}, u32[]{:S(2)}) collective-permute-start(bf16[128,1536]{1,0:T(8,128)(2,1)S(1)} %get-tuple-element.89), channel_id=1, source_target_pairs={{0,16},{8,24},{16,0},{24,8},{1,17},{9,25},{17,1},{25,9},{2,18},{10... | collective-permute-start | bytes 1179656 | tf_op jit(solution)/shard_map/ppermute | solution.py:90
  133.4 15.5 %collective-permute-start.24 = (bf16[128,1536]{1,0:T(8,128)(2,1)S(1)}, bf16[128,1536]{1,0:T(8,128)(2,1)S(1)}, u32[]{:S(2)}, u32[]{:S(2)}) collective-permute-start(bf16[128,1536]{1,0:T(8,128)(2,1)S(1)} %get-tuple-element.88), channel_id=1, source_target_pairs={{0,24},{8,16},{16,8},{24,0},{1,25},{9,17},{17,9},{25,1},{2,26},{10... | collective-permute-start | bytes 1179656 | tf_op jit(solution)/shard_map/ppermute | solution.py:90
  149.4 12.1 %collective-permute-start.25 = (bf16[128,1536]{1,0:T(8,128)(2,1)S(1)}, bf16[128,1536]{1,0:T(8,128)(2,1)S(1)}, u32[]{:S(2)}, u32[]{:S(2)}) collective-permute-start(bf16[128,1536]{1,0:T(8,128)(2,1)S(1)} %multiply_convert_fusion.6), channel_id=1, source_target_pairs={{0,8},{8,0},{16,24},{24,16},{1,9},{9,1},{17,25},{25,17},{2,10},{10... | collective-permute-start | bytes 1179656 | tf_op jit(solution)/shard_map/ppermute | solution.py:90
  150.1 20.4 %collective-permute-start.26 = (bf16[128,1536]{1,0:T(8,128)(2,1)S(1)}, bf16[128,1536]{1,0:T(8,128)(2,1)S(1)}, u32[]{:S(2)}, u32[]{:S(2)}) collective-permute-start(bf16[128,1536]{1,0:T(8,128)(2,1)S(1)} %multiply_convert_fusion.6), channel_id=1, source_target_pairs={{0,16},{8,24},{16,0},{24,8},{1,17},{9,25},{17,1},{25,9},{2,18},{10... | collective-permute-start | bytes 1179656 | tf_op jit(solution)/shard_map/ppermute | solution.py:90
  150.8 19.6 %collective-permute-start.27 = (bf16[128,1536]{1,0:T(8,128)(2,1)S(1)}, bf16[128,1536]{1,0:T(8,128)(2,1)S(1)}, u32[]{:S(2)}, u32[]{:S(2)}) collective-permute-start(bf16[128,1536]{1,0:T(8,128)(2,1)S(1)} %multiply_convert_fusion.6), channel_id=1, source_target_pairs={{0,24},{8,16},{16,8},{24,0},{1,25},{9,17},{17,9},{25,1},{2,26},{10... | collective-permute-start | bytes 1179656 | tf_op jit(solution)/shard_map/ppermute | solution.py:90
  153.7 19.6 %collective-permute-start.38 = (bf16[128,1536]{1,0:T(8,128)(2,1)S(1)}, bf16[128,1536]{1,0:T(8,128)(2,1)S(1)}, u32[]{:S(2)}, u32[]{:S(2)}) collective-permute-start(bf16[128,1536]{1,0:T(8,128)(2,1)S(1)} %get-tuple-element.59), channel_id=1, source_target_pairs={{0,8},{8,0},{16,24},{24,16},{1,9},{9,1},{17,25},{25,17},{2,10},{10... | collective-permute-start | bytes 1179656 | tf_op jit(solution)/shard_map/ppermute | solution.py:90
  154.4 26.0 %collective-permute-start.39 = (bf16[128,1536]{1,0:T(8,128)(2,1)S(1)}, bf16[128,1536]{1,0:T(8,128)(2,1)S(1)}, u32[]{:S(2)}, u32[]{:S(2)}) collective-permute-start(bf16[128,1536]{1,0:T(8,128)(2,1)S(1)} %get-tuple-element.59), channel_id=1, source_target_pairs={{0,16},{8,24},{16,0},{24,8},{1,17},{9,25},{17,1},{25,9},{2,18},{10... | collective-permute-start | bytes 1179656 | tf_op jit(solution)/shard_map/ppermute | solution.py:90
  161.4 19.0 %collective-permute-start.40 = (bf16[128,1536]{1,0:T(8,128)(2,1)S(1)}, bf16[128,1536]{1,0:T(8,128)(2,1)}, u32[]{:S(2)}, u32[]{:S(2)}) collective-permute-start(bf16[128,1536]{1,0:T(8,128)(2,1)S(1)} %get-tuple-element.59), channel_id=1, source_target_pairs={{0,24},{8,16},{16,8},{24,0},{1,25},{9,17},{17,9},{25,1},{2,26},{10... | collective-permute-start | bytes 1179656 | tf_op jit(solution)/shard_map/ppermute | solution.py:90
  171.7 10.5 %collective-permute-start.32 = (bf16[512,1536]{1,0:T(8,128)(2,1)}, bf16[512,1536]{1,0:T(8,128)(2,1)S(1)}, u32[]{:S(2)}, u32[]{:S(2)}) collective-permute-start(bf16[512,1536]{1,0:T(8,128)(2,1)} %pad_maximum_fusion.1), channel_id=1, source_target_pairs={{0,4},{4,0},{1,5},{5,1},{2,6},{6,2},{3,7},{7,3},{8,12},{12,8},{9,1... | collective-permute-start | bytes 4718600 | tf_op jit(solution)/shard_map/ppermute | solution.py:87
  197.7 12.1 %collective-permute-start.43 = (bf16[128,1536]{1,0:T(8,128)(2,1)S(1)}, bf16[128,1536]{1,0:T(8,128)(2,1)S(1)}, u32[]{:S(2)}, u32[]{:S(2)}) collective-permute-start(bf16[128,1536]{1,0:T(8,128)(2,1)S(1)} %get-tuple-element.81), channel_id=1, source_target_pairs={{0,8},{8,0},{16,24},{24,16},{1,9},{9,1},{17,25},{25,17},{2,10},{10... | collective-permute-start | bytes 1179656 | tf_op jit(solution)/shard_map/ppermute | solution.py:90
  198.5 19.5 %collective-permute-start.44 = (bf16[128,1536]{1,0:T(8,128)(2,1)S(1)}, bf16[128,1536]{1,0:T(8,128)(2,1)S(1)}, u32[]{:S(2)}, u32[]{:S(2)}) collective-permute-start(bf16[128,1536]{1,0:T(8,128)(2,1)S(1)} %get-tuple-element.83), channel_id=1, source_target_pairs={{0,16},{8,24},{16,0},{24,8},{1,17},{9,25},{17,1},{25,9},{2,18},{10... | collective-permute-start | bytes 1179656 | tf_op jit(solution)/shard_map/ppermute | solution.py:90
  199.5 18.6 %collective-permute-start.45 = (bf16[128,1536]{1,0:T(8,128)(2,1)S(1)}, bf16[128,1536]{1,0:T(8,128)(2,1)S(1)}, u32[]{:S(2)}, u32[]{:S(2)}) collective-permute-start(bf16[128,1536]{1,0:T(8,128)(2,1)S(1)} %get-tuple-element.82), channel_id=1, source_target_pairs={{0,24},{8,16},{16,8},{24,0},{1,25},{9,17},{17,9},{25,1},{2,26},{10... | collective-permute-start | bytes 1179656 | tf_op jit(solution)/shard_map/ppermute | solution.py:90
  219.3 12.1 %collective-permute-start.46 = (bf16[128,1536]{1,0:T(8,128)(2,1)S(1)}, bf16[128,1536]{1,0:T(8,128)(2,1)S(1)}, u32[]{:S(2)}, u32[]{:S(2)}) collective-permute-start(bf16[128,1536]{1,0:T(8,128)(2,1)S(1)} %fusion.116), channel_id=1, source_target_pairs={{0,8},{8,0},{16,24},{24,16},{1,9},{9,1},{17,25},{25,17},{2,10},{10... | collective-permute-start | bytes 1179656 | tf_op jit(solution)/shard_map/ppermute | solution.py:90
  220.6 16.8 %collective-permute-start.47 = (bf16[128,1536]{1,0:T(8,128)(2,1)S(1)}, bf16[128,1536]{1,0:T(8,128)(2,1)S(1)}, u32[]{:S(2)}, u32[]{:S(2)}) collective-permute-start(bf16[128,1536]{1,0:T(8,128)(2,1)S(1)} %fusion.116), channel_id=1, source_target_pairs={{0,16},{8,24},{16,0},{24,8},{1,17},{9,25},{17,1},{25,9},{2,18},{10... | collective-permute-start | bytes 1179656 | tf_op jit(solution)/shard_map/ppermute | solution.py:90
  221.2 17.5 %collective-permute-start.48 = (bf16[128,1536]{1,0:T(8,128)(2,1)S(1)}, bf16[128,1536]{1,0:T(8,128)(2,1)S(1)}, u32[]{:S(2)}, u32[]{:S(2)}) collective-permute-start(bf16[128,1536]{1,0:T(8,128)(2,1)S(1)} %fusion.116), channel_id=1, source_target_pairs={{0,24},{8,16},{16,8},{24,0},{1,25},{9,17},{17,9},{25,1},{2,26},{10... | collective-permute-start | bytes 1179656 | tf_op jit(solution)/shard_map/ppermute | solution.py:90
  252.3 90.8 %reduce-scatter.11.cloned.1.call-start = ((), (), s32[]{:S(2)}) async-start(), calls=%async_computation.9 | async-start | bytes 1966080 | tf_op jit(solution)/shard_map/reduce_scatter | solution.py:286
  262.1 82.9 %reduce-scatter.7.cloned.1.call-start = ((), (), s32[]{:S(2)}) async-start(), calls=%async_computation.7 | async-start | bytes 737280 | tf_op jit(solution)/shard_map/reduce_scatter | solution.py:309
  267.2 135.0 %reduce-scatter.9.cloned.1.call-start = ((), (), s32[]{:S(2)}) async-start(), calls=%async_computation.8 | async-start | bytes 3932160 | tf_op jit(solution)/shard_map/reduce_scatter | solution.py:290
  277.7 25.2 %collective-permute-start.33 = (bf16[512,1536]{1,0:T(8,128)(2,1)}, bf16[512,1536]{1,0:T(8,128)(2,1)}, u32[]{:S(2)}, u32[]{:S(2)}) collective-permute-start(bf16[512,1536]{1,0:T(8,128)(2,1)} %convolution_convert_fusion.2), channel_id=1, source_target_pairs={{0,4},{4,0},{1,5},{5,1},{2,6},{6,2},{3,7},{7,3},{8,12},{12,8},{9,1... | collective-permute-start | bytes 4718600 | tf_op jit(solution)/shard_map/ppermute | solution.py:87
  282.0 12.1 %collective-permute-start.49 = (bf16[128,1536]{1,0:T(8,128)(2,1)S(1)}, bf16[128,1536]{1,0:T(8,128)(2,1)S(1)}, u32[]{:S(2)}, u32[]{:S(2)}) collective-permute-start(bf16[128,1536]{1,0:T(8,128)(2,1)S(1)} %get-tuple-element.78), channel_id=1, source_target_pairs={{0,8},{8,0},{16,24},{24,16},{1,9},{9,1},{17,25},{25,17},{2,10},{10... | collective-permute-start | bytes 1179656 | tf_op jit(solution)/shard_map/ppermute | solution.py:90
  283.1 18.2 %collective-permute-start.50 = (bf16[128,1536]{1,0:T(8,128)(2,1)S(1)}, bf16[128,1536]{1,0:T(8,128)(2,1)S(1)}, u32[]{:S(2)}, u32[]{:S(2)}) collective-permute-start(bf16[128,1536]{1,0:T(8,128)(2,1)S(1)} %get-tuple-element.80), channel_id=1, source_target_pairs={{0,16},{8,24},{16,0},{24,8},{1,17},{9,25},{17,1},{25,9},{2,18},{10... | collective-permute-start | bytes 1179656 | tf_op jit(solution)/shard_map/ppermute | solution.py:90
  284.5 17.9 %collective-permute-start.51 = (bf16[128,1536]{1,0:T(8,128)(2,1)S(1)}, bf16[128,1536]{1,0:T(8,128)(2,1)S(1)}, u32[]{:S(2)}, u32[]{:S(2)}) collective-permute-start(bf16[128,1536]{1,0:T(8,128)(2,1)S(1)} %get-tuple-element.79), channel_id=1, source_target_pairs={{0,24},{8,16},{16,8},{24,0},{1,25},{9,17},{17,9},{25,1},{2,26},{10... | collective-permute-start | bytes 1179656 | tf_op jit(solution)/shard_map/ppermute | solution.py:90
  306.7 25.3 %collective-permute-start.34 = (bf16[128,1536]{1,0:T(8,128)(2,1)S(1)}, bf16[128,1536]{1,0:T(8,128)(2,1)S(1)}, u32[]{:S(2)}, u32[]{:S(2)}) collective-permute-start(bf16[128,1536]{1,0:T(8,128)(2,1)S(1)} %get-tuple-element.84), channel_id=1, source_target_pairs={{0,8},{8,0},{16,24},{24,16},{1,9},{9,1},{17,25},{25,17},{2,10},{10... | collective-permute-start | bytes 1179656 | tf_op jit(solution)/shard_map/ppermute | solution.py:90
  307.7 24.3 %collective-permute-start.35 = (bf16[128,1536]{1,0:T(8,128)(2,1)S(1)}, bf16[128,1536]{1,0:T(8,128)(2,1)S(1)}, u32[]{:S(2)}, u32[]{:S(2)}) collective-permute-start(bf16[128,1536]{1,0:T(8,128)(2,1)S(1)} %get-tuple-element.86), channel_id=1, source_target_pairs={{0,16},{8,24},{16,0},{24,8},{1,17},{9,25},{17,1},{25,9},{2,18},{10... | collective-permute-start | bytes 1179656 | tf_op jit(solution)/shard_map/ppermute | solution.py:90
  309.1 23.0 %collective-permute-start.36 = (bf16[128,1536]{1,0:T(8,128)(2,1)S(1)}, bf16[128,1536]{1,0:T(8,128)(2,1)S(1)}, u32[]{:S(2)}, u32[]{:S(2)}) collective-permute-start(bf16[128,1536]{1,0:T(8,128)(2,1)S(1)} %get-tuple-element.85), channel_id=1, source_target_pairs={{0,24},{8,16},{16,8},{24,0},{1,25},{9,17},{17,9},{25,1},{2,26},{10... | collective-permute-start | bytes 1179656 | tf_op jit(solution)/shard_map/ppermute | solution.py:90
  310.3 17.1 %collective-permute-start.55 = (f32[2,1536]{1,0:T(2,128)S(1)}, f32[2,1536]{1,0:T(2,128)S(1)}, u32[]{:S(2)}, u32[]{:S(2)}) collective-permute-start(f32[2,1536]{1,0:T(2,128)S(1)} %fusion.165), channel_id=1, source_target_pairs={{0,16},{8,24},{16,0},{24,8},{1,17},{9,25},{17,1},{25,9},{2,18},{10... | collective-permute-start | bytes 36872 | tf_op jit(solution)/shard_map/ppermute | solution.py:90
  406.8 10.9 %collective-permute-start.65 = (bf16[2,48,1024]{2,1,0:T(8,128)(2,1)S(1)}, bf16[2,48,1024]{2,1,0:T(8,128)(2,1)S(1)}, u32[]{:S(2)}, u32[]{:S(2)}) collective-permute-start(bf16[2,48,1024]{2,1,0:T(8,128)(2,1)S(1)} %get-tuple-element.104), channel_id=1, source_target_pairs={{0,16},{8,24},{16,0},{24,8},{1,17},{9,25},{17,1},{25,9},{2,18},{10... | collective-permute-start | bytes 589832 | tf_op jit(solution)/shard_map/ppermute | solution.py:90
  408.2 9.4 %collective-permute-start.66 = (bf16[2,48,1024]{2,1,0:T(8,128)(2,1)S(1)}, bf16[2,48,1024]{2,1,0:T(8,128)(2,1)S(1)}, u32[]{:S(2)}, u32[]{:S(2)}) collective-permute-start(bf16[2,48,1024]{2,1,0:T(8,128)(2,1)S(1)} %get-tuple-element.105), channel_id=1, source_target_pairs={{0,24},{8,16},{16,8},{24,0},{1,25},{9,17},{17,9},{25,1},{2,26},{10... | collective-permute-start | bytes 589832 | tf_op jit(solution)/shard_map/ppermute | solution.py:90
  (102 other events, 720.2 us)
Sparse Core Ops, SparseCore 0:
  20.6 39.1 all-gather.2
  97.2 62.5 all-gather.4
  252.4 28.5 reduce-scatter.4
  283.1 34.0 reduce-scatter.10
  319.9 21.2 reduce-scatter.6
  343.4 58.7 reduce-scatter.8

commit v3 on v2

--- a/solution.py
+++ b/solution.py
@@ -133,16 +133,18 @@
             ]
         )
 
-    def after(value, *others):
-        return lax.optimization_barrier((value,) + others)[0]
+    def tie(*values):
+        return lax.optimization_barrier(values)
 
     def along_z(a, step):
         return lax.ppermute(a, "fsdp", [(i, (i + step) % rows_z) for i in range(rows_z)])
 
-    def ring_gather(a):
-        found = {0: a}
-        right, left = a, a
-        for step in range(1, rows_z // 2 + 1):
+    def ring_first(a):
+        return along_z(a, 1), along_z(a, -1)
+
+    def ring_rest(a, right, left):
+        found = {0: a, rows_z - 1: right, 1: left}
+        for step in range(2, rows_z // 2 + 1):
             if 2 * step == rows_z:
                 half = a.shape[-1] // 2
                 low = along_z(right[..., :half], 1)
@@ -162,10 +164,6 @@
         full = both_cores(along.reshape(rows_z, chips, d_rows, cols))
         return jnp.transpose(full, (2, 0, 1, 3, 4)).reshape(chips * 2 * rows_z * d_rows, cols)
 
-    pair = jnp.stack([block_input[:, 0], out_cotangent[:, 0]], axis=1)
-    pair = jnp.concatenate([pick(pair, core), core_swap(pick(pair, 1 - core))], axis=1)
-    x_low, dy_low = pair[0], pair[1]
-
     owner = (chip * 2 + core) * rows_z + place
     spot = chip * 2 + core
     gains = lax.dynamic_update_slice(
@@ -180,8 +178,7 @@
     )
     table = jnp.concatenate([gains.reshape(-1), marks.reshape(-1)]).reshape(-1, 128)
 
-    def sum_plane(a):
-        a = a + core_swap(a)
+    def sum_chips(a):
         bit = 1
         while bit < chips:
             a = a + chip_xor(a, bit)
@@ -195,36 +192,52 @@
             bit *= 2
         return a
 
+    along_down = lax.all_gather(w_down, "fsdp", axis=0, tiled=True)
+    pair = jnp.stack([block_input[:, 0], out_cotangent[:, 0]], axis=1)
+    pair = jnp.concatenate([pick(pair, core), core_swap(pick(pair, 1 - core))], axis=1)
     pack_qkv = chip_slices((w_query, w_key, w_value), (q_cols, kv_cols, kv_cols))
     piece_qkv = exchange_chips(pack_qkv).reshape(-1, pack_qkv.shape[-1])
-    out_rel = ring_gather(w_out)
-    qkv_rel = ring_gather(piece_qkv)
-    along_down = lax.all_gather(w_down, "fsdp", axis=0, tiled=True)
-    x_all = gather_chips(x_low)
-    w_qkv = order_columns(by_place(qkv_rel))
-    out_w = both_cores(by_place(out_rel)).reshape(-1, width)
+    out_right, out_left = ring_first(w_out)
+    table = table + core_swap(table)
     pack_gu = jnp.stack(
         [
             jnp.concatenate([w[:, n * ff_cols : (n + 1) * ff_cols] for w in (w_gate, w_up)], axis=1)
             for n in range(2 * chips)
         ]
     ).reshape(chips, 2, d_rows, 2 * ff_cols)
-    piece_gu = exchange_chips(after(pack_gu, piece_qkv))
+    pair, piece_qkv, out_right, out_left, table, pack_gu = tie(
+        pair, piece_qkv, out_right, out_left, table, pack_gu
+    )
+
+    x_low, dy_low = pair[0], pair[1]
+    x_all = gather_chips(x_low)
+    qkv_right, qkv_left = ring_first(piece_qkv)
+    x_all, qkv_right, qkv_left, pack_gu, table = tie(x_all, qkv_right, qkv_left, pack_gu, table)
+
+    piece_gu = exchange_chips(pack_gu)
+    qkv_rel = ring_rest(piece_qkv, qkv_right, qkv_left)
+    piece_gu, qkv_rel, table = tie(piece_gu, qkv_rel, table)
     piece_gu = core_pair(pick(piece_gu, core, 1), core_swap(pick(piece_gu, 1 - core, 1)), 1)
     along_gu = lax.all_gather(
         piece_gu.reshape(2 * chips * d_rows, 2 * ff_cols), "fsdp", axis=0, tiled=True
     )
-    table = sum_plane(table).reshape(-1)
+    table = sum_chips(table).reshape(-1)
+    w_qkv = order_columns(by_place(qkv_rel))
+    w_qkv, table, piece_gu, out_right, out_left, dy_low = tie(
+        w_qkv, table, piece_gu, out_right, out_left, dy_low
+    )
+    out_rel = ring_rest(w_out, out_right, out_left)
+    out_w = both_cores(by_place(out_rel)).reshape(-1, width)
     gain_one, gain_two = sum_z(table[: 2 * width].reshape(2, width))
     marks = table[2 * width :].reshape(2, 2, chips, 2, tok)
     marks = pick(marks, core, 1)
     marks = jnp.where(core == 0, marks, jnp.flip(marks, axis=2)).reshape(2, chips, 2 * tok)
     marks_all = by_chip([marks[:, k] for k in range(chips)])
     marks_all = jnp.transpose(marks_all, (1, 0, 2)).reshape(2, chips * 2 * tok)
-    dy_all = gather_chips(dy_low)
     own = x_low.shape[0]
     seq = x_all.shape[0]
 
+    dy_all = gather_chips(dy_low)
     pos_all, seg_all = marks_all[0], marks_all[1]
     allowed = (seg_all[:, None] == seg_all[None, :]) & (pos_all[None, :] <= pos_all[:, None])
     cosine, sine = rope_tables(pos_all)
@@ -244,76 +257,52 @@
     soft_low = soft.astype(bf16)
     mixed = jnp.einsum("grst,tgh->sgrh", soft_low, value, preferred_element_type=f32)
     mixed = mixed.astype(bf16).reshape(seq, q_cols)
+    mixed, dy_all = tie(mixed, dy_all)
     x_own = x_low.astype(f32)
     middle = x_own + scatter_chips(mm(mixed, out_w))
 
+    dy_both = jnp.concatenate([dy_all, core_swap(dy_all)])
+    d_act = mm_nt(dy_both, along_down)
+    middle, dy_both, d_act = tie(middle, dy_both, d_act)
     scale_two = rms_scale(middle)
     n_two = middle * scale_two
     h_two = gather_chips((n_two * gain_two).astype(bf16))
-    dy_other = core_swap(dy_all)
-    h_two, along_down, along_gu = lax.optimization_barrier((h_two, along_down, along_gu))
-    h_other = core_swap(h_two)
-    down_w = along_down
+    h_both = jnp.concatenate([h_two, core_swap(h_two)])
+    h_both, along_gu = tie(h_both, along_gu)
     w_gu = along_gu.reshape(rows_z, 2 * chips, d_rows, 2 * ff_cols)
     w_gu = jnp.transpose(w_gu, (1, 0, 2, 3)).reshape(width, 2 * ff_cols)
-
-    def mlp_forward(h):
-        gu = mm(h, w_gu)
-        gate, up = gu[:, :ff_cols], gu[:, ff_cols:]
-        sigma = jax.nn.sigmoid(gate)
-        return gate, up, sigma, (gate * sigma * up).astype(bf16)
-
-    def mlp_backward(dy, gate, up, sigma):
-        d_act = mm_nt(dy, down_w)
-        d_gate = (d_act * up * sigma * (1.0 + gate * (1.0 - sigma))).astype(bf16)
-        d_up = (d_act * gate * sigma).astype(bf16)
-        return jnp.concatenate([d_gate, d_up], axis=1)
-
-    def give_partial(other_part, own_part):
-        return scatter_chips(own_part + core_swap(other_part.astype(bf16)).astype(f32))
-
-    *keep, act = mlp_forward(h_two)
-    *keep_other, act_other = mlp_forward(h_other)
-    d_gu_other = mlp_backward(dy_other, *keep_other)
-    d_gu = mlp_backward(dy_all, *keep)
-    d_h_two = give_partial(mm_nt(d_gu_other, w_gu), mm_nt(d_gu, w_gu))
-    result = middle + give_partial(mm(act_other, down_w), mm(act, down_w))
-    result = result.astype(bf16)
-
-    act_both = jnp.concatenate([act, act_other])
-    dy_both = jnp.concatenate([dy_all, dy_other])
-    g_down = mm_tn(act_both, dy_both).astype(bf16)
-    g_down = lax.psum_scatter(g_down, "fsdp", scatter_dimension=0, tiled=True).astype(f32)
-    g_gu = mm_tn(jnp.concatenate([h_two, h_other]), jnp.concatenate([d_gu, d_gu_other]))
-    g_gu = g_gu.astype(bf16).reshape(2 * chips, rows_z, d_rows, 2 * ff_cols)
+    gu = mm(h_both, w_gu)
+    gate, up = gu[:, :ff_cols], gu[:, ff_cols:]
+    sigma = jax.nn.sigmoid(gate)
+    act = (gate * sigma * up).astype(bf16)
+    d_gate = (d_act * up * sigma * (1.0 + gate * (1.0 - sigma))).astype(bf16)
+    d_up = (d_act * gate * sigma).astype(bf16)
+    d_gu = jnp.concatenate([d_gate, d_up], axis=1)
+    g_down = mm_tn(act, dy_both).astype(bf16)
+    g_down, d_gu, act = tie(g_down, d_gu, act)
+    g_down = lax.psum_scatter(g_down, "fsdp", scatter_dimension=0, tiled=True)
+
+    def give_partial(rows, weights, product):
+        other = core_swap(product(rows[seq:], weights).astype(bf16)).astype(f32)
+        return product(rows[:seq], weights) + other
+
+    d_h_two = scatter_chips(give_partial(d_gu, w_gu, mm_nt))
+    g_gu = mm_tn(h_both, d_gu).astype(bf16).reshape(2 * chips, rows_z, d_rows, 2 * ff_cols)
     g_gu = jnp.transpose(g_gu, (1, 0, 2, 3)).reshape(width, 2 * ff_cols)
+    d_h_two, g_gu = tie(d_h_two, g_gu)
     g_gu = lax.psum_scatter(g_gu, "fsdp", scatter_dimension=0, tiled=True)
-    g_gu = g_gu.reshape(chips, 2, d_rows, 2 * ff_cols)
-    g_gu = core_pair(pick(g_gu, core, 1), core_swap(pick(g_gu, 1 - core, 1)), 1)
-    g_gu = exchange_chips(g_gu)
-
-    def reduce_columns(left, right):
-        grad = mm_tn(left, right).astype(bf16)
-        cols = grad.shape[1]
-        grad = grad.reshape(chips, 2, rows_z, d_rows, cols)
-        other = core_swap(pick(grad, 1 - core, 1))
-        total = pick(grad, core, 1) + other
-        total = jnp.transpose(total, (1, 0, 2, 3)).reshape(rows_z * chips * d_rows, cols)
-        total = lax.psum_scatter(total, "fsdp", scatter_dimension=0, tiled=True)
-        return exchange_chips(total.reshape(chips, d_rows, cols))
-
-    def reduce_rows(left, right):
-        grad = mm_tn(left, right).astype(bf16)
-        grad = grad.reshape(2, grad.shape[0] // 2, grad.shape[1])
-        total = pick(grad, core) + core_swap(pick(grad, 1 - core))
-        return lax.psum_scatter(total, "fsdp", scatter_dimension=0, tiled=True).astype(f32)
 
     dy_own = dy_low.astype(f32)
     gain_two_part = jnp.sum(d_h_two * n_two, axis=0)
     d_middle = dy_own + norm_back(d_h_two * gain_two, n_two, scale_two)
     branch = gather_chips(d_middle.astype(bf16))
-
-    g_out = reduce_rows(mixed, branch)
+    partial = give_partial(act, along_down, mm)
+    branch, partial = tie(branch, partial)
+    result = (middle + scatter_chips(partial)).astype(bf16)
+
+    g_out = mm_tn(mixed, branch).astype(bf16)
+    g_out = g_out.reshape(2, g_out.shape[0] // 2, g_out.shape[1])
+    g_out = pick(g_out, core) + core_swap(pick(g_out, 1 - core))
     d_mixed = mm_nt(branch, out_w).astype(bf16).reshape(seq, kv_heads, 2, HEAD)
     d_soft = jnp.einsum("sgrh,tgh->grst", d_mixed, value, preferred_element_type=f32)
     d_value = jnp.einsum("grst,sgrh->tgh", soft_low, d_mixed, preferred_element_type=f32)
@@ -331,8 +320,18 @@
         ],
         axis=1,
     )
+    d_qkv, result, g_out = tie(d_qkv, result, g_out)
+    cols_qkv = d_qkv.shape[1]
+    g_qkv = mm_tn(h_one, d_qkv).astype(bf16).reshape(chips, 2, rows_z, d_rows, cols_qkv)
+    g_qkv = pick(g_qkv, core, 1) + core_swap(pick(g_qkv, 1 - core, 1))
+    g_qkv = jnp.transpose(g_qkv, (1, 0, 2, 3)).reshape(rows_z, chips * d_rows, cols_qkv)
+    folds = width // cols_qkv
+    g_out = g_out.reshape(rows_z, d_rows, width)
+    g_rest = [g_out[:, :, k * cols_qkv : (k + 1) * cols_qkv] for k in range(folds)]
+    g_rest = jnp.concatenate([g_qkv] + g_rest, axis=1)
+    g_rest, d_qkv = tie(g_rest.reshape(-1, cols_qkv), d_qkv)
+    g_rest = lax.psum_scatter(g_rest, "fsdp", scatter_dimension=0, tiled=True)
     d_h_one = scatter_chips(mm_nt(d_qkv, w_qkv))
-    g_qkv = reduce_columns(h_one, d_qkv)
     scale_one = rms_scale(x_own)
     n_one = x_own * scale_one
     gain_one_part = jnp.sum(d_h_one * n_one, axis=0)
@@ -351,19 +350,32 @@
         grad = jnp.transpose(grad.astype(f32), (2, 0, 1, 3))
         return grad.reshape(d_rows, 2 * chips * ff_cols)
 
-    gain_parts = sum_z(sum_plane(jnp.stack([gain_one_part, gain_two_part])))
+    g_down = g_down.astype(f32)
+    g_gu = g_gu.reshape(chips, 2, d_rows, 2 * ff_cols)
+    g_gu = core_pair(pick(g_gu, core, 1), core_swap(pick(g_gu, 1 - core, 1)), 1)
+    g_gu = exchange_chips(g_gu)
+    g_gate, g_up = spread_ff(g_gu[..., :ff_cols]), spread_ff(g_gu[..., ff_cols:])
+    gain_parts = jnp.stack([gain_one_part, gain_two_part])
+    gain_parts = sum_z(sum_chips(gain_parts + core_swap(gain_parts)))
     gain_parts = lax.dynamic_slice_in_dim(gain_parts, owner * d_rows, d_rows, 1)
+    result, d_input = give_back(result), give_back(d_input)
+    g_rest, g_gate, g_up, g_down, gain_parts, result, d_input = tie(
+        g_rest, g_gate, g_up, g_down, gain_parts, result, d_input
+    )
+    g_qkv = exchange_chips(g_rest[: chips * d_rows].reshape(chips, d_rows, cols_qkv))
+    g_out = g_rest[chips * d_rows :].reshape(folds, d_rows, cols_qkv)
+    g_out = jnp.transpose(g_out, (1, 0, 2)).reshape(d_rows, width).astype(f32)
     return (
-        give_back(result),
-        give_back(d_input),
+        result,
+        d_input,
         gain_parts[0],
         spread(g_qkv, 0, q_cols),
         spread(g_qkv, q_cols, kv_cols),
         spread(g_qkv, q_cols + kv_cols, kv_cols),
         g_out,
         gain_parts[1],
-        spread_ff(g_gu[..., :ff_cols]),
-        spread_ff(g_gu[..., ff_cols:]),
+        g_gate,
+        g_up,
         g_down,
     )
 

time: 436 us -> 417 us (0.956)
  waiting for transfers between devices: 226 us -> 151 us
  local copies, waits for them, and re-layouts: 37.6 us -> 60.9 us
  other arithmetic: 34.2 us -> 56.3 us
  matrix products: 52.1 us -> 57.9 us
    reduce_scatter x1, waiting for transfers between devices: 55.4 us -> 0.01 us  [on_device(): g_gu = lax.psum_scatter(g_gu, 'fsdp', scatter_dimension=0, tiled=True)]
    ppermute x4, waiting for transfers between devices: 24.3 us -> 9.71 us  [sum_z(): a = a + lax.ppermute(a, 'fsdp', [(i, i ^ bit) for i in range(rows_z)])]
    ppermute x40, waiting for transfers between devices: 134 us -> 119 us  [chip_xor(): return lax.ppermute(a, 'chip', [(i, i ^ j) for i in range(chips)])]
    all_gather x1, waiting for transfers between devices: 0.01 us -> 9.98 us  [on_device(): lax.all_gather(piece_gu.reshape(2 * chips * d_rows, 2 * ff_cols), 'fsdp',...]
    unnamed x175 -> x135, local copies, waits for them, and re-layouts: 11.8 us -> 21.4 us
    dot_general x6 -> x5, matrix products: 13.2 us -> 19 us  [mm(): return jnp.dot(a, b, preferred_element_type=f32)]
    concatenate x0 -> x5, other arithmetic: none -> 4.5 us  [the longest x1 1.64 us: on_device(): d_gu = jnp.concatenate([d_gate, d_up], axis=1)]
    dot_general x6 -> x5, matrix products: 12.9 us -> 15.6 us  [mm_nt(): return jnp.einsum('te,de->td', a, b, preferred_element_type=f32)]
  transfers between devices with their start and end apart: 73 -> 72, of which waited for: 35 -> 39; matrix products, arithmetic and copies ran while one was open for 23% -> 34% of each run, Pallas kernels for 0% -> 0%
where the time goes in v3:
time: 417 us; the launch traced here: 409 us
  waiting for transfers between devices  151 us (36%)
  starting transfers between devices  67.2 us (16%)
  local copies, waits for them, and re-layouts  60.9 us (15%)
  matrix products  57.9 us (14%)
  other arithmetic  56.3 us (14%)
  between operations  15.6 us (4%)
    ppermute x40, waiting for transfers between devices, chip_xor(): return lax.ppermute(a, 'chip', [(i, i ^ j) for i in range(chips)])  119 us
    ppermute x40, starting transfers between devices, chip_xor(): return lax.ppermute(a, 'chip', [(i, i ^ j) for i in range(chips)])  47 us
    unnamed x135, local copies, waits for them, and re-layouts  21.4 us
    dot_general x5, matrix products, mm(): return jnp.dot(a, b, preferred_element_type=f32)  19 us
    dot_general x5, matrix products, mm_nt(): return jnp.einsum('te,de->td', a, b, preferred_element_type=f32)  15.6 us
    ppermute x8, starting transfers between devices, along_z(): lax.ppermute(a, 'fsdp', [(i, (i + step) % rows_z) for i in range(rows_z)])  15 us
    dot_general x4, matrix products, mm_tn(): return jnp.einsum('td,te->de', a, b, preferred_element_type=f32)  12.9 us
    all_gather x1, waiting for transfers between devices, on_device(): lax.all_gather(piece_gu.reshape(2 * chips * d_rows, 2 * ff_cols), 'fsdp',...  9.98 us
  transfers between devices with their start and end apart: 72, of which 39 were waited for; matrix products, arithmetic and copies ran while one was open for 34% of the time, Pallas kernels for 0%

profile of v3, /device:TPU:0, one launch (start us, length us, event | category | flops | bytes accessed | tf_op | source)
XLA Modules:
  0.0 409.0 jit_solution(13858114373610001155)
XLA Ops:
  7.2 3.1 collective-permute-start.4
  10.3 2.1 collective-permute-start.5
  18.0 2.6 collective-permute-start.3
  32.9 7.3 %collective-permute-done.9 = bf16[128,1536]{1,0:T(8,128)(2,1)S(1)} collective-permute-done((bf16[128,1536]{1,0:T(8,128)(2,1)S(1)}, bf16[128,1536]{1,0:T(8,128)(2,1)S(1)}, u32[]{:S(2)}, u32[]{:S(2)}) %collective-permute-start.9) | collective-permute-done | bytes 393248 | tf_op jit(solution)/shard_map/ppermute | solution.py:90
  40.2 6.6 %collective-permute-done.8 = bf16[128,1536]{1,0:T(8,128)(2,1)S(1)} collective-permute-done((bf16[128,1536]{1,0:T(8,128)(2,1)S(1)}, bf16[128,1536]{1,0:T(8,128)(2,1)S(1)}, u32[]{:S(2)}, u32[]{:S(2)}) %collective-permute-start.8) | collective-permute-done | bytes 393248 | tf_op jit(solution)/shard_map/ppermute | solution.py:90
  51.0 2.3 collective-permute-start.15
  57.7 2.1 collective-permute-start.14
  62.8 5.8 %collective-permute-done.16 = bf16[192,384]{1,0:T(8,128)(2,1)} collective-permute-done((bf16[192,384]{1,0:T(8,128)(2,1)S(1)}, bf16[192,384]{1,0:T(8,128)(2,1)}, u32[]{:S(2)}, u32[]{:S(2)}) %collective-permute-start.16) | collective-permute-done | bytes 147488 | tf_op jit(solution)/shard_map/ppermute | solution.py:140
  76.5 2.2 collective-permute-done.18
  104.4 2.1 collective-permute-done.22
  106.6 2.3 collective-permute-start.27
  108.9 3.1 fusion.48
  116.9 4.9 %fusion.101 = (f32[2,2,512]{2,1,0:T(2,128)S(1)}, f32[2,2,512,512]{2,3,1,0:T(8,128)}) fusion(pred[512,512]{0,1:T(8,128)(4,1)} %compare_and_fusion, bf16[512,2,2,48]{0,3,2,1:T(8,128)(2,1)S(1)} %bitcast.412, bf16[512,2,2,48]{0,3,2,1:T(8,128)(2,1)S(1)} %bitcast.410, bf16[512,2,48]{0,2,1:T(8,128)(2,1)S(1)} %get-tuple-element.197, ...), kind=kOutput, calls=%fused_computation.278 | convolution fusion | flops 206701056 | bytes 5054464 | tf_op jit(solution)/shard_map/sub | solution.py:255
  130.2 2.7 convolution_convert_fusion.6
  133.0 2.6 pad_maximum_fusion.3
  137.4 2.6 fusion.102
  145.8 2.7 constant_dynamic-update-slice_fusion.3
  148.5 4.9 %collective-permute-done.29 = bf16[128,1536]{1,0:T(8,128)(2,1)} collective-permute-done((bf16[128,1536]{1,0:T(8,128)(2,1)}, bf16[128,1536]{1,0:T(8,128)(2,1)}, u32[]{:S(2)}, u32[]{:S(2)}) %collective-permute-start.29) | collective-permute-done | bytes 393248 | tf_op jit(solution)/shard_map/ppermute | solution.py:90
  153.4 8.7 %collective-permute-done.31 = bf16[128,1536]{1,0:T(8,128)(2,1)} collective-permute-done((bf16[128,1536]{1,0:T(8,128)(2,1)}, bf16[128,1536]{1,0:T(8,128)(2,1)}, u32[]{:S(2)}, u32[]{:S(2)}) %collective-permute-start.31) | collective-permute-done | bytes 393248 | tf_op jit(solution)/shard_map/ppermute | solution.py:90
  163.5 2.3 fusion.32
  167.1 5.5 %fusion.105 = f32[1024,512]{1,0:T(8,128)} fusion(bf16[1024,1536]{1,0:T(8,128)(2,1)} %constant_dynamic-update-slice_fusion.2, bf16[512,1536]{1,0:T(8,128)(2,1)} %all-gather.3.cloned.1.call-done), kind=kOutput, calls=%fused_computation.282 | convolution fusion | flops 1610612736 | bytes 6815744 | tf_op jit(solution)/shard_map/te,de->td/dot_general | solution.py:54
  177.2 9.4 %collective-permute-done.35 = bf16[128,1536]{1,0:T(8,128)(2,1)S(1)} collective-permute-done((bf16[128,1536]{1,0:T(8,128)(2,1)S(1)}, bf16[128,1536]{1,0:T(8,128)(2,1)S(1)}, u32[]{:S(2)}, u32[]{:S(2)}) %collective-permute-start.35) | collective-permute-done | bytes 393248 | tf_op jit(solution)/shard_map/ppermute | solution.py:90
  186.6 5.2 %collective-permute-done.34 = bf16[128,1536]{1,0:T(8,128)(2,1)S(1)} collective-permute-done((bf16[128,1536]{1,0:T(8,128)(2,1)S(1)}, bf16[128,1536]{1,0:T(8,128)(2,1)S(1)}, u32[]{:S(2)}, u32[]{:S(2)}) %collective-permute-start.34) | collective-permute-done | bytes 393248 | tf_op jit(solution)/shard_map/ppermute | solution.py:90
  196.7 10.0 %all-gather.5.cloned.1.call-done = bf16[1536,1024]{1,0:T(8,128)(2,1)} async-done(((bf16[384,1024]{1,0:T(8,128)(2,1)}), bf16[1536,1024]{1,0:T(8,128)(2,1)}) %all-gather.5.cloned.1.call-update) | async-done | bytes 3145744 | tf_op jit(solution)/shard_map/all_gather | solution.py:221
  206.6 2.4 copy.80
  210.7 5.4 %fusion.106 = f32[1024,1024]{1,0:T(8,128)S(1)} fusion(bf16[1024,1536]{1,0:T(8,128)(2,1)} %constant_dynamic-update-slice_fusion.4, bf16[1536,1024]{1,0:T(8,128)(2,1)S(1)} %bitcast.372), kind=kOutput, calls=%fused_computation.283 | convolution fusion | flops 3221225472 | bytes 10485760 | tf_op jit(solution)/shard_map/dot_general | solution.py:46
  216.2 2.3 multiply_convert_fusion.1
  219.5 4.9 %convolution_convert_fusion.4 = bf16[512,1536]{1,0:T(8,128)(2,1)} fusion(bf16[1024,512]{1,0:T(8,128)(2,1)S(1)} %get-tuple-element.84, bf16[1024,1536]{1,0:T(8,128)(2,1)} %constant_dynamic-update-slice_fusion.2), kind=kOutput, calls=%fused_computation.20 | convolution fusion | flops 1611399168 | bytes 5767168 | tf_op jit(solution)/shard_map/td,te->de/dot_general | solution.py:50
  226.6 3.0 convolution_convert_fusion.3
  230.2 3.8 convolution_convert_fusion.2
  234.5 3.3 fusion.103
  241.4 5.6 %convolution_convert_fusion = bf16[1536,1024]{1,0:T(8,128)(2,1)S(1)} fusion(bf16[1024,1536]{1,0:T(8,128)(2,1)} %constant_dynamic-update-slice_fusion.4, bf16[1024,1024]{1,0:T(8,128)(2,1)S(1)} %copy-done.16), kind=kOutput, calls=%fused_computation.10 | convolution fusion | flops 3222798336 | bytes 8388608 | tf_op jit(solution)/shard_map/td,te->de/dot_general | solution.py:50
  247.0 2.2 copy.83
  249.9 8.6 %collective-permute-done.40 = bf16[128,1536]{1,0:T(8,128)(2,1)S(1)} collective-permute-done((bf16[128,1536]{1,0:T(8,128)(2,1)S(1)}, bf16[128,1536]{1,0:T(8,128)(2,1)S(1)}, u32[]{:S(2)}, u32[]{:S(2)}) %collective-permute-start.40) | collective-permute-done | bytes 393248 | tf_op jit(solution)/shard_map/ppermute | solution.py:90
  265.3 4.1 convert_add_fusion
  269.6 5.1 %collective-permute-done.43 = bf16[128,1536]{1,0:T(8,128)(2,1)S(1)} collective-permute-done((bf16[128,1536]{1,0:T(8,128)(2,1)S(1)}, bf16[128,1536]{1,0:T(8,128)(2,1)S(1)}, u32[]{:S(2)}, u32[]{:S(2)}) %collective-permute-start.43) | collective-permute-done | bytes 393248 | tf_op jit(solution)/shard_map/ppermute | solution.py:90
  274.6 5.3 %collective-permute-done.42 = bf16[128,1536]{1,0:T(8,128)(2,1)} collective-permute-done((bf16[128,1536]{1,0:T(8,128)(2,1)S(1)}, bf16[128,1536]{1,0:T(8,128)(2,1)}, u32[]{:S(2)}, u32[]{:S(2)}) %collective-permute-start.42) | collective-permute-done | bytes 393248 | tf_op jit(solution)/shard_map/ppermute | solution.py:90
  294.4 8.2 %collective-permute-done.45 = bf16[128,1536]{1,0:T(8,128)(2,1)S(1)} collective-permute-done((bf16[128,1536]{1,0:T(8,128)(2,1)S(1)}, bf16[128,1536]{1,0:T(8,128)(2,1)S(1)}, u32[]{:S(2)}, u32[]{:S(2)}) %collective-permute-start.45) | collective-permute-done | bytes 393248 | tf_op jit(solution)/shard_map/ppermute | solution.py:90
  302.6 7.6 %collective-permute-done.47 = bf16[128,1536]{1,0:T(8,128)(2,1)S(1)} collective-permute-done((bf16[128,1536]{1,0:T(8,128)(2,1)S(1)}, bf16[128,1536]{1,0:T(8,128)(2,1)S(1)}, u32[]{:S(2)}, u32[]{:S(2)}) %collective-permute-start.47) | collective-permute-done | bytes 393248 | tf_op jit(solution)/shard_map/ppermute | solution.py:90
  314.7 2.8 collective-permute-done.49
  318.9 3.1 fusion.104
  325.7 8.5 %collective-permute-done.54 = bf16[128,1536]{1,0:T(8,128)(2,1)S(1)} collective-permute-done((bf16[128,1536]{1,0:T(8,128)(2,1)S(1)}, bf16[128,1536]{1,0:T(8,128)(2,1)S(1)}, u32[]{:S(2)}, u32[]{:S(2)}) %collective-permute-start.54) | collective-permute-done | bytes 393248 | tf_op jit(solution)/shard_map/ppermute | solution.py:90
  334.2 8.6 %collective-permute-done.56 = bf16[128,1536]{1,0:T(8,128)(2,1)S(1)} collective-permute-done((bf16[128,1536]{1,0:T(8,128)(2,1)S(1)}, bf16[128,1536]{1,0:T(8,128)(2,1)S(1)}, u32[]{:S(2)}, u32[]{:S(2)}) %collective-permute-start.56) | collective-permute-done | bytes 393248 | tf_op jit(solution)/shard_map/ppermute | solution.py:90
  359.5 4.2 %collective-permute-done.60 = f32[2,1536]{1,0:T(2,128)S(1)} collective-permute-done((f32[2,1536]{1,0:T(2,128)S(1)}, f32[2,1536]{1,0:T(2,128)S(1)}, u32[]{:S(2)}, u32[]{:S(2)}) %collective-permute-start.60) | collective-permute-done | bytes 12320 | tf_op jit(solution)/shard_map/ppermute | solution.py:191
  365.9 3.4 collective-permute-done.61
  374.3 2.6 collective-permute-start.53
  377.9 3.3 collective-permute-done.51
  381.2 3.5 collective-permute-done.52
  (422 shorter events, 178.7 us)
Async XLA Ops:
  7.2 159.9 %all-gather.3.cloned.1.call-start = ((), (), s32[]{:S(2)}) async-start(), calls=%async_computation.3 | async-start | bytes 1966080 | tf_op jit(solution)/shard_map/all_gather | solution.py:195
  7.2 19.8 %collective-permute-start.4 = (bf16[48,1536]{1,0:T(8,128)(2,1)}, bf16[48,1536]{1,0:T(8,128)(2,1)S(1)}, u32[]{:S(2)}, u32[]{:S(2)}) collective-permute-start(bf16[48,1536]{1,0:T(8,128)(2,1)} %param.21), channel_id=1, source_target_pairs={{0,1},{1,2},{2,3},{3,0},{4,5},{5,6},{6,7},{7,4},{8,9},{9,10},{10,1... | collective-permute-start | bytes 442376 | tf_op jit(solution)/shard_map/ppermute | solution.py:140
  10.3 16.8 %collective-permute-start.5 = (bf16[48,1536]{1,0:T(8,128)(2,1)}, bf16[48,1536]{1,0:T(8,128)(2,1)S(1)}, u32[]{:S(2)}, u32[]{:S(2)}) collective-permute-start(bf16[48,1536]{1,0:T(8,128)(2,1)} %param.21), channel_id=1, source_target_pairs={{0,3},{1,0},{2,1},{3,2},{4,7},{5,4},{6,5},{7,6},{8,11},{9,8},{10,9... | collective-permute-start | bytes 442376 | tf_op jit(solution)/shard_map/ppermute | solution.py:140
  14.3 7.2 %collective-permute-start.6 = (f32[40,128]{1,0:T(8,128)S(1)}, f32[40,128]{1,0:T(8,128)S(1)}, u32[]{:S(2)}, u32[]{:S(2)}) collective-permute-start(f32[40,128]{1,0:T(8,128)S(1)} %maximum_bitcast_fusion.23), channel_id=1, source_target_pairs={{0,4},{4,0},{1,5},{5,1},{2,6},{6,2},{3,7},{7,3},{8,12},{12,8},{9,1... | collective-permute-start | bytes 61448 | tf_op jit(solution)/shard_map/ppermute | solution.py:87
  27.2 13.0 %collective-permute-start.9 = (bf16[128,1536]{1,0:T(8,128)(2,1)S(1)}, bf16[128,1536]{1,0:T(8,128)(2,1)S(1)}, u32[]{:S(2)}, u32[]{:S(2)}) collective-permute-start(bf16[128,1536]{1,0:T(8,128)(2,1)S(1)} %get-tuple-element.181), channel_id=1, source_target_pairs={{0,24},{8,16},{16,8},{24,0},{1,25},{9,17},{17,9},{25,1},{2,26},{10... | collective-permute-start | bytes 1179656 | tf_op jit(solution)/shard_map/ppermute | solution.py:90
  28.9 17.8 %collective-permute-start.8 = (bf16[128,1536]{1,0:T(8,128)(2,1)S(1)}, bf16[128,1536]{1,0:T(8,128)(2,1)S(1)}, u32[]{:S(2)}, u32[]{:S(2)}) collective-permute-start(bf16[128,1536]{1,0:T(8,128)(2,1)S(1)} %get-tuple-element.181), channel_id=1, source_target_pairs={{0,16},{8,24},{16,0},{24,8},{1,17},{9,25},{17,1},{25,9},{2,18},{10... | collective-permute-start | bytes 1179656 | tf_op jit(solution)/shard_map/ppermute | solution.py:90
  29.8 17.7 %collective-permute-start.7 = (bf16[128,1536]{1,0:T(8,128)(2,1)S(1)}, bf16[128,1536]{1,0:T(8,128)(2,1)}, u32[]{:S(2)}, u32[]{:S(2)}) collective-permute-start(bf16[128,1536]{1,0:T(8,128)(2,1)S(1)} %get-tuple-element.181), channel_id=1, source_target_pairs={{0,8},{8,0},{16,24},{24,16},{1,9},{9,1},{17,25},{25,17},{2,10},{10... | collective-permute-start | bytes 1179656 | tf_op jit(solution)/shard_map/ppermute | solution.py:90
  30.8 18.2 %collective-permute-start.11 = (bf16[192,768]{1,0:T(8,128)(2,1)S(1)}, bf16[192,768]{1,0:T(8,128)(2,1)}, u32[]{:S(2)}, u32[]{:S(2)}) collective-permute-start(bf16[192,768]{1,0:T(8,128)(2,1)S(1)} %bitcast.394), channel_id=1, source_target_pairs={{0,3},{1,0},{2,1},{3,2},{4,7},{5,4},{6,5},{7,6},{8,11},{9,8},{10,9... | collective-permute-start | bytes 884744 | tf_op jit(solution)/shard_map/ppermute | solution.py:140
  32.7 16.3 %collective-permute-start.10 = (bf16[192,768]{1,0:T(8,128)(2,1)S(1)}, bf16[192,768]{1,0:T(8,128)(2,1)}, u32[]{:S(2)}, u32[]{:S(2)}) collective-permute-start(bf16[192,768]{1,0:T(8,128)(2,1)S(1)} %bitcast.395), channel_id=1, source_target_pairs={{0,1},{1,2},{2,3},{3,0},{4,5},{5,6},{6,7},{7,4},{8,9},{9,10},{10,1... | collective-permute-start | bytes 884744 | tf_op jit(solution)/shard_map/ppermute | solution.py:140
  32.8 173.8 %all-gather.5.cloned.1.call-start = ((), (), s32[]{:S(2)}) async-start(), calls=%async_computation.4 | async-start | bytes 3932160 | tf_op jit(solution)/shard_map/all_gather | solution.py:221
  51.0 11.8 %collective-permute-start.15 = (bf16[192,384]{1,0:T(8,128)(2,1)S(1)}, bf16[192,384]{1,0:T(8,128)(2,1)}, u32[]{:S(2)}, u32[]{:S(2)}) collective-permute-start(bf16[192,384]{1,0:T(8,128)(2,1)S(1)} %slice.322), channel_id=1, source_target_pairs={{0,1},{1,2},{2,3},{3,0},{4,5},{5,6},{6,7},{7,4},{8,9},{9,10},{10,1... | collective-permute-start | bytes 442376 | tf_op jit(solution)/shard_map/ppermute | solution.py:140
  53.3 15.4 %collective-permute-start.16 = (bf16[192,384]{1,0:T(8,128)(2,1)S(1)}, bf16[192,384]{1,0:T(8,128)(2,1)}, u32[]{:S(2)}, u32[]{:S(2)}) collective-permute-start(bf16[192,384]{1,0:T(8,128)(2,1)S(1)} %slice.323), channel_id=1, source_target_pairs={{0,3},{1,0},{2,1},{3,2},{4,7},{5,4},{6,5},{7,6},{8,11},{9,8},{10,9... | collective-permute-start | bytes 442376 | tf_op jit(solution)/shard_map/ppermute | solution.py:140
  57.7 13.2 %collective-permute-start.14 = (bf16[2,48,1024]{2,1,0:T(8,128)(2,1)S(1)}, bf16[2,48,1024]{2,1,0:T(8,128)(2,1)S(1)}, u32[]{:S(2)}, u32[]{:S(2)}) collective-permute-start(bf16[2,48,1024]{2,1,0:T(8,128)(2,1)S(1)} %get-tuple-element.183), channel_id=1, source_target_pairs={{0,24},{8,16},{16,8},{24,0},{1,25},{9,17},{17,9},{25,1},{2,26},{10... | collective-permute-start | bytes 589832 | tf_op jit(solution)/shard_map/ppermute | solution.py:90
  59.8 11.1 %collective-permute-start.13 = (bf16[2,48,1024]{2,1,0:T(8,128)(2,1)S(1)}, bf16[2,48,1024]{2,1,0:T(8,128)(2,1)S(1)}, u32[]{:S(2)}, u32[]{:S(2)}) collective-permute-start(bf16[2,48,1024]{2,1,0:T(8,128)(2,1)S(1)} %get-tuple-element.184), channel_id=1, source_target_pairs={{0,16},{8,24},{16,0},{24,8},{1,17},{9,25},{17,1},{25,9},{2,18},{10... | collective-permute-start | bytes 589832 | tf_op jit(solution)/shard_map/ppermute | solution.py:90
  61.2 9.7 %collective-permute-start.12 = (bf16[2,48,1024]{2,1,0:T(8,128)(2,1)S(1)}, bf16[2,48,1024]{2,1,0:T(8,128)(2,1)S(1)}, u32[]{:S(2)}, u32[]{:S(2)}) collective-permute-start(bf16[2,48,1024]{2,1,0:T(8,128)(2,1)S(1)} %get-tuple-element.185), channel_id=1, source_target_pairs={{0,8},{8,0},{16,24},{24,16},{1,9},{9,1},{17,25},{25,17},{2,10},{10... | collective-permute-start | bytes 589832 | tf_op jit(solution)/shard_map/ppermute | solution.py:90
  73.8 9.0 %collective-permute-start.17 = (bf16[4,4,48,768]{3,2,1,0:T(8,128)(2,1)}, bf16[4,4,48,768]{3,2,1,0:T(8,128)(2,1)}, u32[]{:S(2)}, u32[]{:S(2)}) collective-permute-start(bf16[4,4,48,768]{3,2,1,0:T(8,128)(2,1)} %bitcast.43), channel_id=1, source_target_pairs={{0,4},{4,0},{1,5},{5,1},{2,6},{6,2},{3,7},{7,3},{8,12},{12,8},{9,1... | collective-permute-start | bytes 3538952 | tf_op jit(solution)/shard_map/ppermute | solution.py:87
  87.0 45.9 %collective-permute-start.25 = (bf16[128,1536]{1,0:T(8,128)(2,1)S(1)}, bf16[128,1536]{1,0:T(8,128)(2,1)}, u32[]{:S(2)}, u32[]{:S(2)}) collective-permute-start(bf16[128,1536]{1,0:T(8,128)(2,1)S(1)} %get-tuple-element.72), channel_id=1, source_target_pairs={{0,24},{8,16},{16,8},{24,0},{1,25},{9,17},{17,9},{25,1},{2,26},{10... | collective-permute-start | bytes 1179656 | tf_op jit(solution)/shard_map/ppermute | solution.py:90
  88.4 44.6 %collective-permute-start.24 = (bf16[128,1536]{1,0:T(8,128)(2,1)S(1)}, bf16[128,1536]{1,0:T(8,128)(2,1)}, u32[]{:S(2)}, u32[]{:S(2)}) collective-permute-start(bf16[128,1536]{1,0:T(8,128)(2,1)S(1)} %get-tuple-element.72), channel_id=1, source_target_pairs={{0,16},{8,24},{16,0},{24,8},{1,17},{9,25},{17,1},{25,9},{2,18},{10... | collective-permute-start | bytes 1179656 | tf_op jit(solution)/shard_map/ppermute | solution.py:90
  89.9 43.0 %collective-permute-start.23 = (bf16[128,1536]{1,0:T(8,128)(2,1)S(1)}, bf16[128,1536]{1,0:T(8,128)(2,1)}, u32[]{:S(2)}, u32[]{:S(2)}) collective-permute-start(bf16[128,1536]{1,0:T(8,128)(2,1)S(1)} %get-tuple-element.72), channel_id=1, source_target_pairs={{0,8},{8,0},{16,24},{24,16},{1,9},{9,1},{17,25},{25,17},{2,10},{10... | collective-permute-start | bytes 1179656 | tf_op jit(solution)/shard_map/ppermute | solution.py:90
  98.6 24.6 %collective-permute-start.26 = (bf16[48,768]{1,0:T(8,128)(2,1)}, bf16[48,768]{1,0:T(8,128)(2,1)}, u32[]{:S(2)}, u32[]{:S(2)}) collective-permute-start(bf16[48,768]{1,0:T(8,128)(2,1)} %slice.340), channel_id=1, source_target_pairs={{0,1},{1,2},{2,3},{3,0},{4,5},{5,6},{6,7},{7,4},{8,9},{9,10},{10,1... | collective-permute-start | bytes 221192 | tf_op jit(solution)/shard_map/ppermute | solution.py:140
  106.6 16.5 %collective-permute-start.27 = (bf16[48,768]{1,0:T(8,128)(2,1)}, bf16[48,768]{1,0:T(8,128)(2,1)}, u32[]{:S(2)}, u32[]{:S(2)}) collective-permute-start(bf16[48,768]{1,0:T(8,128)(2,1)} %slice.341), channel_id=1, source_target_pairs={{0,3},{1,0},{2,1},{3,2},{4,7},{5,4},{6,5},{7,6},{8,11},{9,8},{10,9... | collective-permute-start | bytes 221192 | tf_op jit(solution)/shard_map/ppermute | solution.py:140
  135.6 30.3 %collective-permute-start.32 = (bf16[512,1536]{1,0:T(8,128)(2,1)}, bf16[512,1536]{1,0:T(8,128)(2,1)S(1)}, u32[]{:S(2)}, u32[]{:S(2)}) collective-permute-start(bf16[512,1536]{1,0:T(8,128)(2,1)} %pad_maximum_fusion.3), channel_id=1, source_target_pairs={{0,4},{4,0},{1,5},{5,1},{2,6},{6,2},{3,7},{7,3},{8,12},{12,8},{9,1... | collective-permute-start | bytes 4718600 | tf_op jit(solution)/shard_map/ppermute | solution.py:87
  141.1 12.3 %collective-permute-start.29 = (bf16[128,1536]{1,0:T(8,128)(2,1)}, bf16[128,1536]{1,0:T(8,128)(2,1)}, u32[]{:S(2)}, u32[]{:S(2)}) collective-permute-start(bf16[128,1536]{1,0:T(8,128)(2,1)} %get-tuple-element.159), channel_id=1, source_target_pairs={{0,8},{8,0},{16,24},{24,16},{1,9},{9,1},{17,25},{25,17},{2,10},{10... | collective-permute-start | bytes 1179656 | tf_op jit(solution)/shard_map/ppermute | solution.py:90
  142.7 19.5 %collective-permute-start.31 = (bf16[128,1536]{1,0:T(8,128)(2,1)}, bf16[128,1536]{1,0:T(8,128)(2,1)}, u32[]{:S(2)}, u32[]{:S(2)}) collective-permute-start(bf16[128,1536]{1,0:T(8,128)(2,1)} %get-tuple-element.160), channel_id=1, source_target_pairs={{0,24},{8,16},{16,8},{24,0},{1,25},{9,17},{17,9},{25,1},{2,26},{10... | collective-permute-start | bytes 1179656 | tf_op jit(solution)/shard_map/ppermute | solution.py:90
  144.3 19.2 %collective-permute-start.30 = (bf16[128,1536]{1,0:T(8,128)(2,1)}, bf16[128,1536]{1,0:T(8,128)(2,1)}, u32[]{:S(2)}, u32[]{:S(2)}) collective-permute-start(bf16[128,1536]{1,0:T(8,128)(2,1)} %get-tuple-element.161), channel_id=1, source_target_pairs={{0,16},{8,24},{16,0},{24,8},{1,17},{9,25},{17,1},{25,9},{2,18},{10... | collective-permute-start | bytes 1179656 | tf_op jit(solution)/shard_map/ppermute | solution.py:90
  145.5 201.4 %reduce-scatter.8.cloned.1.call-start = ((), (), s32[]{:S(2)}) async-start(), calls=%async_computation.7 | async-start | bytes 1966080 | tf_op jit(solution)/shard_map/reduce_scatter | solution.py:283
  173.7 12.9 %collective-permute-start.35 = (bf16[128,1536]{1,0:T(8,128)(2,1)S(1)}, bf16[128,1536]{1,0:T(8,128)(2,1)S(1)}, u32[]{:S(2)}, u32[]{:S(2)}) collective-permute-start(bf16[128,1536]{1,0:T(8,128)(2,1)S(1)} %get-tuple-element.142), channel_id=1, source_target_pairs={{0,24},{8,16},{16,8},{24,0},{1,25},{9,17},{17,9},{25,1},{2,26},{10... | collective-permute-start | bytes 1179656 | tf_op jit(solution)/shard_map/ppermute | solution.py:90
  175.0 16.8 %collective-permute-start.34 = (bf16[128,1536]{1,0:T(8,128)(2,1)S(1)}, bf16[128,1536]{1,0:T(8,128)(2,1)S(1)}, u32[]{:S(2)}, u32[]{:S(2)}) collective-permute-start(bf16[128,1536]{1,0:T(8,128)(2,1)S(1)} %get-tuple-element.142), channel_id=1, source_target_pairs={{0,16},{8,24},{16,0},{24,8},{1,17},{9,25},{17,1},{25,9},{2,18},{10... | collective-permute-start | bytes 1179656 | tf_op jit(solution)/shard_map/ppermute | solution.py:90
  175.5 16.3 %collective-permute-start.33 = (bf16[128,1536]{1,0:T(8,128)(2,1)S(1)}, bf16[128,1536]{1,0:T(8,128)(2,1)S(1)}, u32[]{:S(2)}, u32[]{:S(2)}) collective-permute-start(bf16[128,1536]{1,0:T(8,128)(2,1)S(1)} %get-tuple-element.142), channel_id=1, source_target_pairs={{0,8},{8,0},{16,24},{24,16},{1,9},{9,1},{17,25},{25,17},{2,10},{10... | collective-permute-start | bytes 1179656 | tf_op jit(solution)/shard_map/ppermute | solution.py:90
  229.7 139.7 %reduce-scatter.6.cloned.1.call-start = ((), (), s32[]{:S(2)}) async-start(), calls=%async_computation.6 | async-start | bytes 3932160 | tf_op jit(solution)/shard_map/reduce_scatter | solution.py:293
  234.0 31.2 %collective-permute-start.44 = (bf16[512,1536]{1,0:T(8,128)(2,1)}, bf16[512,1536]{1,0:T(8,128)(2,1)}, u32[]{:S(2)}, u32[]{:S(2)}) collective-permute-start(bf16[512,1536]{1,0:T(8,128)(2,1)} %convolution_convert_fusion.2), channel_id=1, source_target_pairs={{0,4},{4,0},{1,5},{5,1},{2,6},{6,2},{3,7},{7,3},{8,12},{12,8},{9,1... | collective-permute-start | bytes 4718600 | tf_op jit(solution)/shard_map/ppermute | solution.py:87
  237.9 12.1 %collective-permute-start.38 = (bf16[128,1536]{1,0:T(8,128)(2,1)S(1)}, bf16[128,1536]{1,0:T(8,128)(2,1)S(1)}, u32[]{:S(2)}, u32[]{:S(2)}) collective-permute-start(bf16[128,1536]{1,0:T(8,128)(2,1)S(1)} %get-tuple-element.156), channel_id=1, source_target_pairs={{0,8},{8,0},{16,24},{24,16},{1,9},{9,1},{17,25},{25,17},{2,10},{10... | collective-permute-start | bytes 1179656 | tf_op jit(solution)/shard_map/ppermute | solution.py:90
  239.5 19.0 %collective-permute-start.40 = (bf16[128,1536]{1,0:T(8,128)(2,1)S(1)}, bf16[128,1536]{1,0:T(8,128)(2,1)S(1)}, u32[]{:S(2)}, u32[]{:S(2)}) collective-permute-start(bf16[128,1536]{1,0:T(8,128)(2,1)S(1)} %get-tuple-element.157), channel_id=1, source_target_pairs={{0,24},{8,16},{16,8},{24,0},{1,25},{9,17},{17,9},{25,1},{2,26},{10... | collective-permute-start | bytes 1179656 | tf_op jit(solution)/shard_map/ppermute | solution.py:90
  241.0 18.9 %collective-permute-start.39 = (bf16[128,1536]{1,0:T(8,128)(2,1)S(1)}, bf16[128,1536]{1,0:T(8,128)(2,1)S(1)}, u32[]{:S(2)}, u32[]{:S(2)}) collective-permute-start(bf16[128,1536]{1,0:T(8,128)(2,1)S(1)} %get-tuple-element.158), channel_id=1, source_target_pairs={{0,16},{8,24},{16,0},{24,8},{1,17},{9,25},{17,1},{25,9},{2,18},{10... | collective-permute-start | bytes 1179656 | tf_op jit(solution)/shard_map/ppermute | solution.py:90
  261.7 13.0 %collective-permute-start.43 = (bf16[128,1536]{1,0:T(8,128)(2,1)S(1)}, bf16[128,1536]{1,0:T(8,128)(2,1)S(1)}, u32[]{:S(2)}, u32[]{:S(2)}) collective-permute-start(bf16[128,1536]{1,0:T(8,128)(2,1)S(1)} %fusion.87), channel_id=1, source_target_pairs={{0,24},{8,16},{16,8},{24,0},{1,25},{9,17},{17,9},{25,1},{2,26},{10... | collective-permute-start | bytes 1179656 | tf_op jit(solution)/shard_map/ppermute | solution.py:90
  263.2 16.8 %collective-permute-start.42 = (bf16[128,1536]{1,0:T(8,128)(2,1)S(1)}, bf16[128,1536]{1,0:T(8,128)(2,1)}, u32[]{:S(2)}, u32[]{:S(2)}) collective-permute-start(bf16[128,1536]{1,0:T(8,128)(2,1)S(1)} %fusion.87), channel_id=1, source_target_pairs={{0,16},{8,24},{16,0},{24,8},{1,17},{9,25},{17,1},{25,9},{2,18},{10... | collective-permute-start | bytes 1179656 | tf_op jit(solution)/shard_map/ppermute | solution.py:90
  264.7 15.3 %collective-permute-start.41 = (bf16[128,1536]{1,0:T(8,128)(2,1)S(1)}, bf16[128,1536]{1,0:T(8,128)(2,1)}, u32[]{:S(2)}, u32[]{:S(2)}) collective-permute-start(bf16[128,1536]{1,0:T(8,128)(2,1)S(1)} %fusion.87), channel_id=1, source_target_pairs={{0,8},{8,0},{16,24},{24,16},{1,9},{9,1},{17,25},{25,17},{2,10},{10... | collective-permute-start | bytes 1179656 | tf_op jit(solution)/shard_map/ppermute | solution.py:90
  269.3 120.4 %reduce-scatter.4.cloned.1.call-start = ((), (), s32[]{:S(2)}) async-start(), calls=%async_computation.5 | async-start | bytes 2211840 | tf_op jit(solution)/shard_map/reduce_scatter | solution.py:333
  288.8 23.7 %collective-permute-start.48 = (bf16[192,1536]{1,0:T(8,128)(2,1)S(1)}, bf16[192,1536]{1,0:T(8,128)(2,1)S(1)}, u32[]{:S(2)}, u32[]{:S(2)}) collective-permute-start(bf16[192,1536]{1,0:T(8,128)(2,1)S(1)} %dynamic-slice_bitcast_fusion), channel_id=1, source_target_pairs={{0,4},{4,0},{1,5},{5,1},{2,6},{6,2},{3,7},{7,3},{8,12},{12,8},{9,1... | collective-permute-start | bytes 1769480 | tf_op jit(solution)/shard_map/ppermute | solution.py:87
  290.5 12.1 %collective-permute-start.45 = (bf16[128,1536]{1,0:T(8,128)(2,1)S(1)}, bf16[128,1536]{1,0:T(8,128)(2,1)S(1)}, u32[]{:S(2)}, u32[]{:S(2)}) collective-permute-start(bf16[128,1536]{1,0:T(8,128)(2,1)S(1)} %get-tuple-element.153), channel_id=1, source_target_pairs={{0,8},{8,0},{16,24},{24,16},{1,9},{9,1},{17,25},{25,17},{2,10},{10... | collective-permute-start | bytes 1179656 | tf_op jit(solution)/shard_map/ppermute | solution.py:90
  291.4 18.8 %collective-permute-start.47 = (bf16[128,1536]{1,0:T(8,128)(2,1)S(1)}, bf16[128,1536]{1,0:T(8,128)(2,1)S(1)}, u32[]{:S(2)}, u32[]{:S(2)}) collective-permute-start(bf16[128,1536]{1,0:T(8,128)(2,1)S(1)} %get-tuple-element.154), channel_id=1, source_target_pairs={{0,24},{8,16},{16,8},{24,0},{1,25},{9,17},{17,9},{25,1},{2,26},{10... | collective-permute-start | bytes 1179656 | tf_op jit(solution)/shard_map/ppermute | solution.py:90
  292.6 18.9 %collective-permute-start.46 = (bf16[128,1536]{1,0:T(8,128)(2,1)S(1)}, bf16[128,1536]{1,0:T(8,128)(2,1)S(1)}, u32[]{:S(2)}, u32[]{:S(2)}) collective-permute-start(bf16[128,1536]{1,0:T(8,128)(2,1)S(1)} %get-tuple-element.155), channel_id=1, source_target_pairs={{0,16},{8,24},{16,0},{24,8},{1,17},{9,25},{17,1},{25,9},{2,18},{10... | collective-permute-start | bytes 1179656 | tf_op jit(solution)/shard_map/ppermute | solution.py:90
  322.1 12.1 %collective-permute-start.54 = (bf16[128,1536]{1,0:T(8,128)(2,1)S(1)}, bf16[128,1536]{1,0:T(8,128)(2,1)S(1)}, u32[]{:S(2)}, u32[]{:S(2)}) collective-permute-start(bf16[128,1536]{1,0:T(8,128)(2,1)S(1)} %get-tuple-element.150), channel_id=1, source_target_pairs={{0,8},{8,0},{16,24},{24,16},{1,9},{9,1},{17,25},{25,17},{2,10},{10... | collective-permute-start | bytes 1179656 | tf_op jit(solution)/shard_map/ppermute | solution.py:90
  323.8 19.0 %collective-permute-start.56 = (bf16[128,1536]{1,0:T(8,128)(2,1)S(1)}, bf16[128,1536]{1,0:T(8,128)(2,1)S(1)}, u32[]{:S(2)}, u32[]{:S(2)}) collective-permute-start(bf16[128,1536]{1,0:T(8,128)(2,1)S(1)} %get-tuple-element.151), channel_id=1, source_target_pairs={{0,24},{8,16},{16,8},{24,0},{1,25},{9,17},{17,9},{25,1},{2,26},{10... | collective-permute-start | bytes 1179656 | tf_op jit(solution)/shard_map/ppermute | solution.py:90
  325.1 19.0 %collective-permute-start.55 = (bf16[128,1536]{1,0:T(8,128)(2,1)S(1)}, bf16[128,1536]{1,0:T(8,128)(2,1)S(1)}, u32[]{:S(2)}, u32[]{:S(2)}) collective-permute-start(bf16[128,1536]{1,0:T(8,128)(2,1)S(1)} %get-tuple-element.152), channel_id=1, source_target_pairs={{0,16},{8,24},{16,0},{24,8},{1,17},{9,25},{17,1},{25,9},{2,18},{10... | collective-permute-start | bytes 1179656 | tf_op jit(solution)/shard_map/ppermute | solution.py:90
  373.4 7.8 %collective-permute-start.51 = (bf16[2,48,1024]{2,1,0:T(8,128)(2,1)S(1)}, bf16[2,48,1024]{2,1,0:T(8,128)(2,1)S(1)}, u32[]{:S(2)}, u32[]{:S(2)}) collective-permute-start(bf16[2,48,1024]{2,1,0:T(8,128)(2,1)S(1)} %get-tuple-element.177), channel_id=1, source_target_pairs={{0,8},{8,0},{16,24},{24,16},{1,9},{9,1},{17,25},{25,17},{2,10},{10... | collective-permute-start | bytes 589832 | tf_op jit(solution)/shard_map/ppermute | solution.py:90
  373.4 11.2 %collective-permute-start.52 = (bf16[2,48,1024]{2,1,0:T(8,128)(2,1)S(1)}, bf16[2,48,1024]{2,1,0:T(8,128)(2,1)S(1)}, u32[]{:S(2)}, u32[]{:S(2)}) collective-permute-start(bf16[2,48,1024]{2,1,0:T(8,128)(2,1)S(1)} %get-tuple-element.178), channel_id=1, source_target_pairs={{0,16},{8,24},{16,0},{24,8},{1,17},{9,25},{17,1},{25,9},{2,18},{10... | collective-permute-start | bytes 589832 | tf_op jit(solution)/shard_map/ppermute | solution.py:90
  374.3 10.4 %collective-permute-start.53 = (bf16[2,48,1024]{2,1,0:T(8,128)(2,1)S(1)}, bf16[2,48,1024]{2,1,0:T(8,128)(2,1)S(1)}, u32[]{:S(2)}, u32[]{:S(2)}) collective-permute-start(bf16[2,48,1024]{2,1,0:T(8,128)(2,1)S(1)} %get-tuple-element.179), channel_id=1, source_target_pairs={{0,24},{8,16},{16,8},{24,0},{1,25},{9,17},{17,9},{25,1},{2,26},{10... | collective-permute-start | bytes 589832 | tf_op jit(solution)/shard_map/ppermute | solution.py:90
  (83 other events, 823.2 us)
Sparse Core Ops, SparseCore 0:
  32.9 43.9 all-gather.2
  145.7 60.9 all-gather.4
  229.8 34.2 reduce-scatter.7
  269.5 57.9 reduce-scatter.5
  352.6 36.5 reduce-scatter.3

commit v4 on v3

--- a/solution.py
+++ b/solution.py
@@ -143,40 +143,32 @@
         return along_z(a, 1), along_z(a, -1)
 
     def ring_rest(a, right, left):
-        found = {0: a, rows_z - 1: right, 1: left}
+        found = [(a, 0, 0), (right, -1, 0), (left, 1, 0)]
         for step in range(2, rows_z // 2 + 1):
             if 2 * step == rows_z:
                 half = a.shape[-1] // 2
-                low = along_z(right[..., :half], 1)
-                high = along_z(left[..., half:], -1)
-                found[step] = jnp.concatenate([low, high], axis=-1)
+                found.append((along_z(right[..., :half], 1), -step, 0))
+                found.append((along_z(left[..., half:], -1), step, half))
             else:
                 right, left = along_z(right, 1), along_z(left, -1)
-                found[rows_z - step], found[step] = right, left
-        return jnp.stack([found[step] for step in range(rows_z)])
-
-    def by_place(a):
-        doubled = jnp.concatenate([a, a])
-        return lax.dynamic_slice_in_dim(doubled, rows_z - place, rows_z, 0)
-
-    def order_columns(along):
-        cols = along.shape[-1]
-        full = both_cores(along.reshape(rows_z, chips, d_rows, cols))
-        return jnp.transpose(full, (2, 0, 1, 3, 4)).reshape(chips * 2 * rows_z * d_rows, cols)
+                found += [(right, -step, 0), (left, step, 0)]
+        return found
+
+    def assemble(found, groups):
+        rows, cols = found[0][0].shape
+        whole = jnp.zeros((groups, rows_z, rows // groups, cols), bf16)
+        for piece, offset, column in found:
+            piece = piece.reshape(groups, 1, rows // groups, piece.shape[-1])
+            index = lax.rem(place + offset + rows_z, rows_z)
+            whole = lax.dynamic_update_slice(whole, piece, (0, index, 0, column))
+        return whole
 
     owner = (chip * 2 + core) * rows_z + place
-    spot = chip * 2 + core
-    gains = lax.dynamic_update_slice(
-        jnp.zeros((2, width), f32),
-        jnp.stack([attn_gain, mlp_gain]).astype(f32),
-        (0, owner * d_rows),
-    )
-    marks = lax.dynamic_update_slice(
-        jnp.zeros((4, chips * 2 * tok), f32),
-        jnp.concatenate([positions[:, 0], segments[:, 0]]).astype(f32),
-        (0, spot * tok),
-    )
-    table = jnp.concatenate([gains.reshape(-1), marks.reshape(-1)]).reshape(-1, 128)
+    gains = lax.all_gather(
+        jnp.stack([attn_gain, mlp_gain]), ("chip", "core", "fsdp"), axis=1, tiled=True
+    )
+    marks = jnp.stack([positions[:, 0], segments[:, 0]])
+    marks = lax.all_gather(marks, ("chip", "core"), axis=0)
 
     def sum_chips(a):
         bit = 1
@@ -192,48 +184,41 @@
             bit *= 2
         return a
 
-    along_down = lax.all_gather(w_down, "fsdp", axis=0, tiled=True)
+    down_right, down_left = ring_first(w_down)
     pair = jnp.stack([block_input[:, 0], out_cotangent[:, 0]], axis=1)
     pair = jnp.concatenate([pick(pair, core), core_swap(pick(pair, 1 - core))], axis=1)
     pack_qkv = chip_slices((w_query, w_key, w_value), (q_cols, kv_cols, kv_cols))
     piece_qkv = exchange_chips(pack_qkv).reshape(-1, pack_qkv.shape[-1])
-    out_right, out_left = ring_first(w_out)
-    table = table + core_swap(table)
     pack_gu = jnp.stack(
         [
             jnp.concatenate([w[:, n * ff_cols : (n + 1) * ff_cols] for w in (w_gate, w_up)], axis=1)
             for n in range(2 * chips)
         ]
     ).reshape(chips, 2, d_rows, 2 * ff_cols)
-    pair, piece_qkv, out_right, out_left, table, pack_gu = tie(
-        pair, piece_qkv, out_right, out_left, table, pack_gu
-    )
+    pair, piece_qkv, pack_gu = tie(pair, piece_qkv, pack_gu)
 
     x_low, dy_low = pair[0], pair[1]
     x_all = gather_chips(x_low)
+    piece_qkv, down_right, down_left = tie(piece_qkv, down_right, down_left)
     qkv_right, qkv_left = ring_first(piece_qkv)
-    x_all, qkv_right, qkv_left, pack_gu, table = tie(x_all, qkv_right, qkv_left, pack_gu, table)
+    x_all, qkv_right, qkv_left, pack_gu = tie(x_all, qkv_right, qkv_left, pack_gu)
 
     piece_gu = exchange_chips(pack_gu)
-    qkv_rel = ring_rest(piece_qkv, qkv_right, qkv_left)
-    piece_gu, qkv_rel, table = tie(piece_gu, qkv_rel, table)
+    found_qkv = ring_rest(piece_qkv, qkv_right, qkv_left)
+    *late, piece_gu, w_out = tie(*[f[0] for f in found_qkv], piece_gu, w_out)
+    found_qkv = [(piece,) + f[1:] for piece, f in zip(late, found_qkv)]
+    out_right, out_left = ring_first(w_out)
     piece_gu = core_pair(pick(piece_gu, core, 1), core_swap(pick(piece_gu, 1 - core, 1)), 1)
-    along_gu = lax.all_gather(
-        piece_gu.reshape(2 * chips * d_rows, 2 * ff_cols), "fsdp", axis=0, tiled=True
-    )
-    table = sum_chips(table).reshape(-1)
-    w_qkv = order_columns(by_place(qkv_rel))
-    w_qkv, table, piece_gu, out_right, out_left, dy_low = tie(
-        w_qkv, table, piece_gu, out_right, out_left, dy_low
-    )
-    out_rel = ring_rest(w_out, out_right, out_left)
-    out_w = both_cores(by_place(out_rel)).reshape(-1, width)
-    gain_one, gain_two = sum_z(table[: 2 * width].reshape(2, width))
-    marks = table[2 * width :].reshape(2, 2, chips, 2, tok)
-    marks = pick(marks, core, 1)
-    marks = jnp.where(core == 0, marks, jnp.flip(marks, axis=2)).reshape(2, chips, 2 * tok)
-    marks_all = by_chip([marks[:, k] for k in range(chips)])
-    marks_all = jnp.transpose(marks_all, (1, 0, 2)).reshape(2, chips * 2 * tok)
+    piece_gu = piece_gu.reshape(2 * chips * d_rows, 2 * ff_cols)
+    w_qkv = assemble(found_qkv, chips)
+    w_qkv = core_pair(w_qkv, core_swap(w_qkv), 1).reshape(width, -1)
+    w_qkv, piece_gu, out_right, out_left, dy_low = tie(w_qkv, piece_gu, out_right, out_left, dy_low)
+    gu_right, gu_left = ring_first(piece_gu)
+    gain_one, gain_two = gains.astype(f32)
+    marks = pick(marks.reshape(chips, 2, 2, 2, tok), core, 3).astype(f32)
+    marks = jnp.where(core == 0, marks, jnp.flip(marks, axis=1))
+    marks_all = by_chip([marks[k] for k in range(chips)])
+    marks_all = jnp.transpose(marks_all, (2, 0, 1, 3)).reshape(2, chips * 2 * tok)
     own = x_low.shape[0]
     seq = x_all.shape[0]
 
@@ -250,27 +235,35 @@
         qkv[:, q_cols : q_cols + kv_cols].reshape(seq, kv_heads, HEAD), cosine, sine
     ).astype(bf16)
     value = qkv[:, q_cols + kv_cols :].astype(bf16).reshape(seq, kv_heads, HEAD)
+    q_rot, dy_all, out_right, out_left = tie(q_rot, dy_all, out_right, out_left)
+    out_w = assemble(ring_rest(w_out, out_right, out_left), 1).reshape(rows_z * d_rows, width)
+    out_w = both_cores(out_w).reshape(-1, width)
     scores = jnp.einsum("sgrh,tgh->grst", q_rot, k_rot, preferred_element_type=f32) * factor
     scores = jnp.where(allowed, scores, -1e30)
     raised = jnp.exp(scores - jnp.max(scores, axis=-1, keepdims=True))
     soft = raised / jnp.sum(raised, axis=-1, keepdims=True)
-    soft_low = soft.astype(bf16)
+    soft_low, out_w, down_right, down_left = tie(
+        soft.astype(bf16), out_w, down_right, down_left
+    )
+    found_down = ring_rest(w_down, down_right, down_left)
     mixed = jnp.einsum("grst,tgh->sgrh", soft_low, value, preferred_element_type=f32)
     mixed = mixed.astype(bf16).reshape(seq, q_cols)
-    mixed, dy_all = tie(mixed, dy_all)
+    mixed, gu_right, gu_left, *late = tie(mixed, gu_right, gu_left, *[f[0] for f in found_down])
+    found_down = [(piece,) + f[1:] for piece, f in zip(late, found_down)]
+    found_gu = ring_rest(piece_gu, gu_right, gu_left)
     x_own = x_low.astype(f32)
     middle = x_own + scatter_chips(mm(mixed, out_w))
 
     dy_both = jnp.concatenate([dy_all, core_swap(dy_all)])
-    d_act = mm_nt(dy_both, along_down)
-    middle, dy_both, d_act = tie(middle, dy_both, d_act)
+    down_w = assemble(found_down, 1).reshape(-1, width)
+    d_act = mm_nt(dy_both, down_w)
+    middle, dy_both, d_act, *late = tie(middle, dy_both, d_act, *[f[0] for f in found_gu])
+    found_gu = [(piece,) + f[1:] for piece, f in zip(late, found_gu)]
     scale_two = rms_scale(middle)
     n_two = middle * scale_two
     h_two = gather_chips((n_two * gain_two).astype(bf16))
     h_both = jnp.concatenate([h_two, core_swap(h_two)])
-    h_both, along_gu = tie(h_both, along_gu)
-    w_gu = along_gu.reshape(rows_z, 2 * chips, d_rows, 2 * ff_cols)
-    w_gu = jnp.transpose(w_gu, (1, 0, 2, 3)).reshape(width, 2 * ff_cols)
+    w_gu = assemble(found_gu, 2 * chips).reshape(width, 2 * ff_cols)
     gu = mm(h_both, w_gu)
     gate, up = gu[:, :ff_cols], gu[:, ff_cols:]
     sigma = jax.nn.sigmoid(gate)
@@ -296,7 +289,7 @@
     gain_two_part = jnp.sum(d_h_two * n_two, axis=0)
     d_middle = dy_own + norm_back(d_h_two * gain_two, n_two, scale_two)
     branch = gather_chips(d_middle.astype(bf16))
-    partial = give_partial(act, along_down, mm)
+    partial = give_partial(act, down_w, mm)
     branch, partial = tie(branch, partial)
     result = (middle + scatter_chips(partial)).astype(bf16)
 

time: 417 us -> 471 us (1.13)
  blocking collectives: 0 us -> 77.8 us
  waiting for transfers between devices: 151 us -> 169 us
  matrix products: 57.9 us -> 41.4 us
  local copies, waits for them, and re-layouts: 60.9 us -> 47.8 us
  other arithmetic: 56.3 us -> 43.7 us
    all_gather x0 -> x2, blocking collectives: none -> 77.8 us  [the longest x1 68.7 us: on_device(): lax.all_gather(jnp.stack([attn_gain, mlp_gain]), ('chip', 'core', 'fsdp')...]
    ppermute x8 -> x16, waiting for transfers between devices: 7.42 us -> 28.3 us  [along_z(): lax.ppermute(a, 'fsdp', [(i, (i + step) % rows_z) for i in range(rows_z)])]
    all_gather x2 -> x0, waiting for transfers between devices: 9.98 us -> none  [the longest x1 9.98 us: on_device(): lax.all_gather(piece_gu.reshape(2 * chips * d_rows, 2 * ff_cols), 'fsdp',...]
    ppermute x40 -> x38, waiting for transfers between devices: 119 us -> 129 us  [chip_xor(): return lax.ppermute(a, 'chip', [(i, i ^ j) for i in range(chips)])]
    unnamed x135 -> x145, local copies, waits for them, and re-layouts: 21.4 us -> 14.1 us
    dynamic_update_slice x2 -> x20, local copies, waits for them, and re-layouts: 0.33 us -> 7.09 us  [assemble(): whole = lax.dynamic_update_slice(whole, piece, (0, index, 0, column))]
    dot_general x5, matrix products: 19 us -> 13.8 us  [mm(): return jnp.dot(a, b, preferred_element_type=f32)]
    ppermute x8 -> x16, starting transfers between devices: 15 us -> 20 us  [along_z(): lax.ppermute(a, 'fsdp', [(i, (i + step) % rows_z) for i in range(rows_z)])]
  transfers between devices with their start and end apart: 72 -> 73, of which waited for: 39 -> 40; matrix products, arithmetic and copies ran while one was open for 34% -> 22% of each run, Pallas kernels for 0% -> 0%
where the time goes in v4:
time: 471 us; the launch traced here: 463 us
  waiting for transfers between devices  169 us (36%)
  blocking collectives  77.8 us (17%)
  starting transfers between devices  67.7 us (14%)
  local copies, waits for them, and re-layouts  47.8 us (10%)
  other arithmetic  43.7 us (9%)
  matrix products  41.4 us (9%)
  between operations  15.9 us (3%)
    ppermute x38, waiting for transfers between devices, chip_xor(): return lax.ppermute(a, 'chip', [(i, i ^ j) for i in range(chips)])  129 us
    all_gather x1, blocking collectives, on_device(): lax.all_gather(jnp.stack([attn_gain, mlp_gain]), ('chip', 'core', 'fsdp')...  68.7 us
    ppermute x38, starting transfers between devices, chip_xor(): return lax.ppermute(a, 'chip', [(i, i ^ j) for i in range(chips)])  44.9 us
    ppermute x16, waiting for transfers between devices, along_z(): lax.ppermute(a, 'fsdp', [(i, (i + step) % rows_z) for i in range(rows_z)])  28.3 us
    ppermute x16, starting transfers between devices, along_z(): lax.ppermute(a, 'fsdp', [(i, (i + step) % rows_z) for i in range(rows_z)])  20 us
    unnamed x145, local copies, waits for them, and re-layouts  14.1 us
    dot_general x5, matrix products, mm(): return jnp.dot(a, b, preferred_element_type=f32)  13.8 us
    dot_general x5, matrix products, mm_nt(): return jnp.einsum('te,de->td', a, b, preferred_element_type=f32)  11.5 us
  transfers between devices with their start and end apart: 73, of which 40 were waited for; matrix products, arithmetic and copies ran while one was open for 22% of the time, Pallas kernels for 0%

profile of v4, /device:TPU:0, one launch (start us, length us, event | category | flops | bytes accessed | tf_op | source)
XLA Modules:
  0.0 463.0 jit_solution(3349553648108523324)
XLA Ops:
  7.3 3.1 collective-permute-start.7
  10.4 2.1 collective-permute-start.8
  16.1 2.6 collective-permute-start.3
  19.6 9.1 %all-gather = s32[16,2,64]{2,1,0:T(2,128)S(1)} all-gather(s32[2,2,64]{2,1,0:T(2,128)S(1)} %pad_add_fusion), channel_id=2, replica_groups=mesh['chip'=4,'core'=2,'fsdp'=4] {'chip','core'}, dimensions={0}, use_global_device_ids=true | all-gather | bytes 9216 | tf_op jit(solution)/shard_map/all_gather | solution.py:171
  28.9 68.7 %all-gather.1 = bf16[32,48,2]{1,2,0:T(2,128)(2,1)} all-gather(bf16[1,48,2]{1,2,0:T(2,128)(2,1)S(1)} %maximum_bitcast_fusion.22), channel_id=1, replica_groups=mesh['chip'=4,'core'=2,'fsdp'=4] {'chip','core','fsdp'}, dimensions={0}, use_global_device_ids=true | all-gather | bytes 6336 | tf_op jit(solution)/shard_map/all_gather | solution.py:167
  107.1 2.0 collective-permute-start.9
  109.2 6.2 %collective-permute-done.6 = bf16[128,1536]{1,0:T(8,128)(2,1)} collective-permute-done((bf16[128,1536]{1,0:T(8,128)(2,1)S(1)}, bf16[128,1536]{1,0:T(8,128)(2,1)}, u32[]{:S(2)}, u32[]{:S(2)}) %collective-permute-start.6) | collective-permute-done | bytes 393248 | tf_op jit(solution)/shard_map/ppermute | solution.py:90
  115.4 6.8 %collective-permute-done.5 = bf16[128,1536]{1,0:T(8,128)(2,1)} collective-permute-done((bf16[128,1536]{1,0:T(8,128)(2,1)S(1)}, bf16[128,1536]{1,0:T(8,128)(2,1)}, u32[]{:S(2)}, u32[]{:S(2)}) %collective-permute-start.5) | collective-permute-done | bytes 393248 | tf_op jit(solution)/shard_map/ppermute | solution.py:90
  126.1 2.0 collective-permute-start.11
  131.9 4.7 %collective-permute-done.15 = bf16[2,48,1024]{2,1,0:T(8,128)(2,1)S(1)} collective-permute-done((bf16[2,48,1024]{2,1,0:T(8,128)(2,1)S(1)}, bf16[2,48,1024]{2,1,0:T(8,128)(2,1)S(1)}, u32[]{:S(2)}, u32[]{:S(2)}) %collective-permute-start.15) | collective-permute-done | bytes 196640 | tf_op jit(solution)/shard_map/ppermute | solution.py:90
  140.2 2.2 collective-permute-start.19
  146.6 3.4 collective-permute-done.18
  163.1 6.7 %collective-permute-done.21 = bf16[128,1536]{1,0:T(8,128)(2,1)} collective-permute-done((bf16[128,1536]{1,0:T(8,128)(2,1)S(1)}, bf16[128,1536]{1,0:T(8,128)(2,1)}, u32[]{:S(2)}, u32[]{:S(2)}) %collective-permute-start.21) | collective-permute-done | bytes 393248 | tf_op jit(solution)/shard_map/ppermute | solution.py:90
  169.8 2.5 pad_maximum_fusion.4
  176.0 3.7 fusion.93
  179.7 12.3 %collective-permute-done.23 = bf16[48,768]{1,0:T(8,128)(2,1)S(1)} collective-permute-done((bf16[48,768]{1,0:T(8,128)(2,1)S(1)}, bf16[48,768]{1,0:T(8,128)(2,1)S(1)}, u32[]{:S(2)}, u32[]{:S(2)}) %collective-permute-start.23) | collective-permute-done | bytes 73760 | tf_op jit(solution)/shard_map/ppermute | solution.py:140
  194.8 2.8 fusion.81
  201.7 4.8 %collective-permute-done.29 = bf16[128,768]{1,0:T(8,128)(2,1)S(1)} collective-permute-done((bf16[128,768]{1,0:T(8,128)(2,1)S(1)}, bf16[128,768]{1,0:T(8,128)(2,1)S(1)}, u32[]{:S(2)}, u32[]{:S(2)}) %collective-permute-start.29) | collective-permute-done | bytes 196640 | tf_op jit(solution)/shard_map/ppermute | solution.py:140
  206.5 5.9 %collective-permute-done.28 = bf16[128,768]{1,0:T(8,128)(2,1)S(1)} collective-permute-done((bf16[128,768]{1,0:T(8,128)(2,1)S(1)}, bf16[128,768]{1,0:T(8,128)(2,1)S(1)}, u32[]{:S(2)}, u32[]{:S(2)}) %collective-permute-start.28) | collective-permute-done | bytes 196640 | tf_op jit(solution)/shard_map/ppermute | solution.py:140
  221.2 8.2 %collective-permute-done.30 = bf16[128,1536]{1,0:T(8,128)(2,1)S(1)} collective-permute-done((bf16[128,1536]{1,0:T(8,128)(2,1)S(1)}, bf16[128,1536]{1,0:T(8,128)(2,1)S(1)}, u32[]{:S(2)}, u32[]{:S(2)}) %collective-permute-start.30) | collective-permute-done | bytes 393248 | tf_op jit(solution)/shard_map/ppermute | solution.py:90
  229.7 7.3 %collective-permute-done.32 = bf16[128,1536]{1,0:T(8,128)(2,1)S(1)} collective-permute-done((bf16[128,1536]{1,0:T(8,128)(2,1)S(1)}, bf16[128,1536]{1,0:T(8,128)(2,1)S(1)}, u32[]{:S(2)}, u32[]{:S(2)}) %collective-permute-start.32) | collective-permute-done | bytes 393248 | tf_op jit(solution)/shard_map/ppermute | solution.py:90
  246.0 9.4 %collective-permute-done.38 = bf16[128,1536]{1,0:T(8,128)(2,1)S(1)} collective-permute-done((bf16[128,1536]{1,0:T(8,128)(2,1)S(1)}, bf16[128,1536]{1,0:T(8,128)(2,1)S(1)}, u32[]{:S(2)}, u32[]{:S(2)}) %collective-permute-start.38) | collective-permute-done | bytes 393248 | tf_op jit(solution)/shard_map/ppermute | solution.py:90
  255.4 4.7 %collective-permute-done.37 = bf16[128,1536]{1,0:T(8,128)(2,1)S(1)} collective-permute-done((bf16[128,1536]{1,0:T(8,128)(2,1)S(1)}, bf16[128,1536]{1,0:T(8,128)(2,1)S(1)}, u32[]{:S(2)}, u32[]{:S(2)}) %collective-permute-start.37) | collective-permute-done | bytes 393248 | tf_op jit(solution)/shard_map/ppermute | solution.py:90
  265.5 3.4 fusion.98
  269.0 2.7 multiply_convert_fusion.1
  272.7 3.0 convolution_convert_fusion.4
  278.2 3.0 convolution_convert_fusion.3
  281.9 3.9 convolution_convert_fusion.2
  286.2 3.4 fusion.95
  293.3 3.7 convolution_convert_fusion
  297.0 2.2 copy.143
  299.2 2.6 collective-permute-done.41
  301.8 8.0 %collective-permute-done.43 = bf16[128,1536]{1,0:T(8,128)(2,1)S(1)} collective-permute-done((bf16[128,1536]{1,0:T(8,128)(2,1)S(1)}, bf16[128,1536]{1,0:T(8,128)(2,1)S(1)}, u32[]{:S(2)}, u32[]{:S(2)}) %collective-permute-start.43) | collective-permute-done | bytes 393248 | tf_op jit(solution)/shard_map/ppermute | solution.py:90
  312.2 2.2 multiply_reduce_fusion
  318.8 4.1 convert_add_fusion
  323.2 5.4 %collective-permute-done.46 = bf16[128,1536]{1,0:T(8,128)(2,1)} collective-permute-done((bf16[128,1536]{1,0:T(8,128)(2,1)}, bf16[128,1536]{1,0:T(8,128)(2,1)}, u32[]{:S(2)}, u32[]{:S(2)}) %collective-permute-start.46) | collective-permute-done | bytes 393248 | tf_op jit(solution)/shard_map/ppermute | solution.py:90
  328.6 5.3 %collective-permute-done.45 = bf16[128,1536]{1,0:T(8,128)(2,1)} collective-permute-done((bf16[128,1536]{1,0:T(8,128)(2,1)}, bf16[128,1536]{1,0:T(8,128)(2,1)}, u32[]{:S(2)}, u32[]{:S(2)}) %collective-permute-start.45) | collective-permute-done | bytes 393248 | tf_op jit(solution)/shard_map/ppermute | solution.py:90
  347.8 8.2 %collective-permute-done.48 = bf16[128,1536]{1,0:T(8,128)(2,1)S(1)} collective-permute-done((bf16[128,1536]{1,0:T(8,128)(2,1)S(1)}, bf16[128,1536]{1,0:T(8,128)(2,1)S(1)}, u32[]{:S(2)}, u32[]{:S(2)}) %collective-permute-start.48) | collective-permute-done | bytes 393248 | tf_op jit(solution)/shard_map/ppermute | solution.py:90
  355.9 8.1 %collective-permute-done.50 = bf16[128,1536]{1,0:T(8,128)(2,1)S(1)} collective-permute-done((bf16[128,1536]{1,0:T(8,128)(2,1)S(1)}, bf16[128,1536]{1,0:T(8,128)(2,1)S(1)}, u32[]{:S(2)}, u32[]{:S(2)}) %collective-permute-start.50) | collective-permute-done | bytes 393248 | tf_op jit(solution)/shard_map/ppermute | solution.py:90
  368.5 2.8 collective-permute-done.52
  373.7 2.6 fusion.96
  380.0 8.5 %collective-permute-done.57 = bf16[128,1536]{1,0:T(8,128)(2,1)S(1)} collective-permute-done((bf16[128,1536]{1,0:T(8,128)(2,1)S(1)}, bf16[128,1536]{1,0:T(8,128)(2,1)S(1)}, u32[]{:S(2)}, u32[]{:S(2)}) %collective-permute-start.57) | collective-permute-done | bytes 393248 | tf_op jit(solution)/shard_map/ppermute | solution.py:90
  388.5 8.1 %collective-permute-done.59 = bf16[128,1536]{1,0:T(8,128)(2,1)S(1)} collective-permute-done((bf16[128,1536]{1,0:T(8,128)(2,1)S(1)}, bf16[128,1536]{1,0:T(8,128)(2,1)S(1)}, u32[]{:S(2)}, u32[]{:S(2)}) %collective-permute-start.59) | collective-permute-done | bytes 393248 | tf_op jit(solution)/shard_map/ppermute | solution.py:90
  413.3 3.7 collective-permute-done.63
  419.1 4.0 collective-permute-done.64
  428.5 2.2 collective-permute-start.56
  431.5 3.5 collective-permute-done.54
  435.0 4.4 collective-permute-done.55
  (441 shorter events, 157.2 us)
Async XLA Ops:
  7.2 393.5 %reduce-scatter.8.cloned.1.call-start = ((), (), s32[]{:S(2)}) async-start(), calls=%async_computation.5 | async-start | bytes 1966080 | tf_op jit(solution)/shard_map/reduce_scatter | solution.py:276
  7.3 99.8 %collective-permute-start.7 = (bf16[128,1536]{1,0:T(8,128)(2,1)}, bf16[128,1536]{1,0:T(8,128)(2,1)S(1)}, u32[]{:S(2)}, u32[]{:S(2)}) collective-permute-start(bf16[128,1536]{1,0:T(8,128)(2,1)} %param.25), channel_id=1, source_target_pairs={{0,1},{1,2},{2,3},{3,0},{4,5},{5,6},{6,7},{7,4},{8,9},{9,10},{10,1... | collective-permute-start | bytes 1179656 | tf_op jit(solution)/shard_map/ppermute | solution.py:140
  10.4 96.7 %collective-permute-start.8 = (bf16[128,1536]{1,0:T(8,128)(2,1)}, bf16[128,1536]{1,0:T(8,128)(2,1)S(1)}, u32[]{:S(2)}, u32[]{:S(2)}) collective-permute-start(bf16[128,1536]{1,0:T(8,128)(2,1)} %param.25), channel_id=1, source_target_pairs={{0,3},{1,0},{2,1},{3,2},{4,7},{5,4},{6,5},{7,6},{8,11},{9,8},{10,9... | collective-permute-start | bytes 1179656 | tf_op jit(solution)/shard_map/ppermute | solution.py:140
  16.1 83.5 %collective-permute-start.3 = (bf16[48,768]{1,0:T(8,128)(2,1)}, bf16[48,768]{1,0:T(8,128)(2,1)}, u32[]{:S(2)}, u32[]{:S(2)}) collective-permute-start(bf16[48,768]{1,0:T(8,128)(2,1)} %get-tuple-element.285), channel_id=1, source_target_pairs={{0,24},{8,16},{16,8},{24,0},{1,25},{9,17},{17,9},{25,1},{2,26},{10... | collective-permute-start | bytes 221192 | tf_op jit(solution)/shard_map/ppermute | solution.py:90
  18.7 80.9 %collective-permute-start.2 = (bf16[48,768]{1,0:T(8,128)(2,1)}, bf16[48,768]{1,0:T(8,128)(2,1)}, u32[]{:S(2)}, u32[]{:S(2)}) collective-permute-start(bf16[48,768]{1,0:T(8,128)(2,1)} %get-tuple-element.286), channel_id=1, source_target_pairs={{0,16},{8,24},{16,0},{24,8},{1,17},{9,25},{17,1},{25,9},{2,18},{10... | collective-permute-start | bytes 221192 | tf_op jit(solution)/shard_map/ppermute | solution.py:90
  19.2 80.4 %collective-permute-start.1 = (bf16[48,768]{1,0:T(8,128)(2,1)S(1)}, bf16[48,768]{1,0:T(8,128)(2,1)}, u32[]{:S(2)}, u32[]{:S(2)}) collective-permute-start(bf16[48,768]{1,0:T(8,128)(2,1)S(1)} %get-tuple-element.287), channel_id=1, source_target_pairs={{0,8},{8,0},{16,24},{24,16},{1,9},{9,1},{17,25},{25,17},{2,10},{10... | collective-permute-start | bytes 221192 | tf_op jit(solution)/shard_map/ppermute | solution.py:90
  102.3 13.1 %collective-permute-start.6 = (bf16[128,1536]{1,0:T(8,128)(2,1)S(1)}, bf16[128,1536]{1,0:T(8,128)(2,1)}, u32[]{:S(2)}, u32[]{:S(2)}) collective-permute-start(bf16[128,1536]{1,0:T(8,128)(2,1)S(1)} %get-tuple-element.245), channel_id=1, source_target_pairs={{0,24},{8,16},{16,8},{24,0},{1,25},{9,17},{17,9},{25,1},{2,26},{10... | collective-permute-start | bytes 1179656 | tf_op jit(solution)/shard_map/ppermute | solution.py:90
  102.4 19.8 %collective-permute-start.5 = (bf16[128,1536]{1,0:T(8,128)(2,1)S(1)}, bf16[128,1536]{1,0:T(8,128)(2,1)}, u32[]{:S(2)}, u32[]{:S(2)}) collective-permute-start(bf16[128,1536]{1,0:T(8,128)(2,1)S(1)} %get-tuple-element.245), channel_id=1, source_target_pairs={{0,16},{8,24},{16,0},{24,8},{1,17},{9,25},{17,1},{25,9},{2,18},{10... | collective-permute-start | bytes 1179656 | tf_op jit(solution)/shard_map/ppermute | solution.py:90
  104.3 19.1 %collective-permute-start.4 = (bf16[128,1536]{1,0:T(8,128)(2,1)S(1)}, bf16[128,1536]{1,0:T(8,128)(2,1)}, u32[]{:S(2)}, u32[]{:S(2)}) collective-permute-start(bf16[128,1536]{1,0:T(8,128)(2,1)S(1)} %get-tuple-element.245), channel_id=1, source_target_pairs={{0,8},{8,0},{16,24},{24,16},{1,9},{9,1},{17,25},{25,17},{2,10},{10... | collective-permute-start | bytes 1179656 | tf_op jit(solution)/shard_map/ppermute | solution.py:90
  107.1 17.7 %collective-permute-start.10 = (bf16[192,768]{1,0:T(8,128)(2,1)S(1)}, bf16[192,768]{1,0:T(8,128)(2,1)S(1)}, u32[]{:S(2)}, u32[]{:S(2)}) collective-permute-start(bf16[192,768]{1,0:T(8,128)(2,1)S(1)} %bitcast.419), channel_id=1, source_target_pairs={{0,3},{1,0},{2,1},{3,2},{4,7},{5,4},{6,5},{7,6},{8,11},{9,8},{10,9... | collective-permute-start | bytes 884744 | tf_op jit(solution)/shard_map/ppermute | solution.py:140
  107.1 17.6 %collective-permute-start.9 = (bf16[192,768]{1,0:T(8,128)(2,1)S(1)}, bf16[192,768]{1,0:T(8,128)(2,1)}, u32[]{:S(2)}, u32[]{:S(2)}) collective-permute-start(bf16[192,768]{1,0:T(8,128)(2,1)S(1)} %bitcast.420), channel_id=1, source_target_pairs={{0,1},{1,2},{2,3},{3,0},{4,5},{5,6},{6,7},{7,4},{8,9},{9,10},{10,1... | collective-permute-start | bytes 884744 | tf_op jit(solution)/shard_map/ppermute | solution.py:140
  126.0 12.8 %collective-permute-start.12 = (bf16[192,384]{1,0:T(8,128)(2,1)S(1)}, bf16[192,384]{1,0:T(8,128)(2,1)S(1)}, u32[]{:S(2)}, u32[]{:S(2)}) collective-permute-start(bf16[192,384]{1,0:T(8,128)(2,1)S(1)} %slice.314), channel_id=1, source_target_pairs={{0,3},{1,0},{2,1},{3,2},{4,7},{5,4},{6,5},{7,6},{8,11},{9,8},{10,9... | collective-permute-start | bytes 442376 | tf_op jit(solution)/shard_map/ppermute | solution.py:140
  126.1 12.8 %collective-permute-start.11 = (bf16[192,384]{1,0:T(8,128)(2,1)S(1)}, bf16[192,384]{1,0:T(8,128)(2,1)S(1)}, u32[]{:S(2)}, u32[]{:S(2)}) collective-permute-start(bf16[192,384]{1,0:T(8,128)(2,1)S(1)} %slice.313), channel_id=1, source_target_pairs={{0,1},{1,2},{2,3},{3,0},{4,5},{5,6},{6,7},{7,4},{8,9},{9,10},{10,1... | collective-permute-start | bytes 442376 | tf_op jit(solution)/shard_map/ppermute | solution.py:140
  150.1 13.0 %collective-permute-start.22 = (bf16[128,1536]{1,0:T(8,128)(2,1)S(1)}, bf16[128,1536]{1,0:T(8,128)(2,1)}, u32[]{:S(2)}, u32[]{:S(2)}) collective-permute-start(bf16[128,1536]{1,0:T(8,128)(2,1)S(1)} %get-tuple-element.92), channel_id=1, source_target_pairs={{0,24},{8,16},{16,8},{24,0},{1,25},{9,17},{17,9},{25,1},{2,26},{10... | collective-permute-start | bytes 1179656 | tf_op jit(solution)/shard_map/ppermute | solution.py:90
  151.6 18.2 %collective-permute-start.21 = (bf16[128,1536]{1,0:T(8,128)(2,1)S(1)}, bf16[128,1536]{1,0:T(8,128)(2,1)}, u32[]{:S(2)}, u32[]{:S(2)}) collective-permute-start(bf16[128,1536]{1,0:T(8,128)(2,1)S(1)} %get-tuple-element.92), channel_id=1, source_target_pairs={{0,16},{8,24},{16,0},{24,8},{1,17},{9,25},{17,1},{25,9},{2,18},{10... | collective-permute-start | bytes 1179656 | tf_op jit(solution)/shard_map/ppermute | solution.py:90
  152.9 16.9 %collective-permute-start.20 = (bf16[128,1536]{1,0:T(8,128)(2,1)S(1)}, bf16[128,1536]{1,0:T(8,128)(2,1)}, u32[]{:S(2)}, u32[]{:S(2)}) collective-permute-start(bf16[128,1536]{1,0:T(8,128)(2,1)S(1)} %get-tuple-element.92), channel_id=1, source_target_pairs={{0,8},{8,0},{16,24},{24,16},{1,9},{9,1},{17,25},{25,17},{2,10},{10... | collective-permute-start | bytes 1179656 | tf_op jit(solution)/shard_map/ppermute | solution.py:90
  153.5 48.1 %collective-permute-start.27 = (bf16[384,1024]{1,0:T(8,128)(2,1)S(1)}, bf16[384,1024]{1,0:T(8,128)(2,1)}, u32[]{:S(2)}, u32[]{:S(2)}) collective-permute-start(bf16[384,1024]{1,0:T(8,128)(2,1)S(1)} %bitcast.387), channel_id=1, source_target_pairs={{0,3},{1,0},{2,1},{3,2},{4,7},{5,4},{6,5},{7,6},{8,11},{9,8},{10,9... | collective-permute-start | bytes 2359304 | tf_op jit(solution)/shard_map/ppermute | solution.py:140
  155.2 46.4 %collective-permute-start.26 = (bf16[384,1024]{1,0:T(8,128)(2,1)S(1)}, bf16[384,1024]{1,0:T(8,128)(2,1)}, u32[]{:S(2)}, u32[]{:S(2)}) collective-permute-start(bf16[384,1024]{1,0:T(8,128)(2,1)S(1)} %bitcast.388), channel_id=1, source_target_pairs={{0,1},{1,2},{2,3},{3,0},{4,5},{5,6},{6,7},{7,4},{8,9},{9,10},{10,1... | collective-permute-start | bytes 2359304 | tf_op jit(solution)/shard_map/ppermute | solution.py:140
  173.7 19.0 %collective-permute-start.24 = (bf16[48,768]{1,0:T(8,128)(2,1)S(1)}, bf16[48,768]{1,0:T(8,128)(2,1)S(1)}, u32[]{:S(2)}, u32[]{:S(2)}) collective-permute-start(bf16[48,768]{1,0:T(8,128)(2,1)S(1)} %slice.326), channel_id=1, source_target_pairs={{0,3},{1,0},{2,1},{3,2},{4,7},{5,4},{6,5},{7,6},{8,11},{9,8},{10,9... | collective-permute-start | bytes 221192 | tf_op jit(solution)/shard_map/ppermute | solution.py:140
  175.6 16.4 %collective-permute-start.23 = (bf16[48,768]{1,0:T(8,128)(2,1)S(1)}, bf16[48,768]{1,0:T(8,128)(2,1)S(1)}, u32[]{:S(2)}, u32[]{:S(2)}) collective-permute-start(bf16[48,768]{1,0:T(8,128)(2,1)S(1)} %slice.325), channel_id=1, source_target_pairs={{0,1},{1,2},{2,3},{3,0},{4,5},{5,6},{6,7},{7,4},{8,9},{9,10},{10,1... | collective-permute-start | bytes 221192 | tf_op jit(solution)/shard_map/ppermute | solution.py:140
  176.0 62.8 %collective-permute-start.33 = (bf16[512,1536]{1,0:T(8,128)(2,1)}, bf16[512,1536]{1,0:T(8,128)(2,1)}, u32[]{:S(2)}, u32[]{:S(2)}) collective-permute-start(bf16[512,1536]{1,0:T(8,128)(2,1)} %pad_maximum_fusion.4), channel_id=1, source_target_pairs={{0,4},{4,0},{1,5},{5,1},{2,6},{6,2},{3,7},{7,3},{8,12},{12,8},{9,1... | collective-permute-start | bytes 4718600 | tf_op jit(solution)/shard_map/ppermute | solution.py:87
  201.0 11.4 %collective-permute-start.28 = (bf16[128,768]{1,0:T(8,128)(2,1)S(1)}, bf16[128,768]{1,0:T(8,128)(2,1)S(1)}, u32[]{:S(2)}, u32[]{:S(2)}) collective-permute-start(bf16[128,768]{1,0:T(8,128)(2,1)S(1)} %slice.327), channel_id=1, source_target_pairs={{0,1},{1,2},{2,3},{3,0},{4,5},{5,6},{6,7},{7,4},{8,9},{9,10},{10,1... | collective-permute-start | bytes 589832 | tf_op jit(solution)/shard_map/ppermute | solution.py:140
  214.4 27.6 %collective-permute-start.35 = (bf16[384,512]{1,0:T(8,128)(2,1)S(1)}, bf16[384,512]{1,0:T(8,128)(2,1)S(1)}, u32[]{:S(2)}, u32[]{:S(2)}) collective-permute-start(bf16[384,512]{1,0:T(8,128)(2,1)S(1)} %slice.334), channel_id=1, source_target_pairs={{0,3},{1,0},{2,1},{3,2},{4,7},{5,4},{6,5},{7,6},{8,11},{9,8},{10,9... | collective-permute-start | bytes 1179656 | tf_op jit(solution)/shard_map/ppermute | solution.py:140
  217.4 12.1 %collective-permute-start.30 = (bf16[128,1536]{1,0:T(8,128)(2,1)S(1)}, bf16[128,1536]{1,0:T(8,128)(2,1)S(1)}, u32[]{:S(2)}, u32[]{:S(2)}) collective-permute-start(bf16[128,1536]{1,0:T(8,128)(2,1)S(1)} %get-tuple-element.223), channel_id=1, source_target_pairs={{0,8},{8,0},{16,24},{24,16},{1,9},{9,1},{17,25},{25,17},{2,10},{10... | collective-permute-start | bytes 1179656 | tf_op jit(solution)/shard_map/ppermute | solution.py:90
  218.8 18.2 %collective-permute-start.32 = (bf16[128,1536]{1,0:T(8,128)(2,1)S(1)}, bf16[128,1536]{1,0:T(8,128)(2,1)S(1)}, u32[]{:S(2)}, u32[]{:S(2)}) collective-permute-start(bf16[128,1536]{1,0:T(8,128)(2,1)S(1)} %get-tuple-element.224), channel_id=1, source_target_pairs={{0,24},{8,16},{16,8},{24,0},{1,25},{9,17},{17,9},{25,1},{2,26},{10... | collective-permute-start | bytes 1179656 | tf_op jit(solution)/shard_map/ppermute | solution.py:90
  220.0 18.4 %collective-permute-start.31 = (bf16[128,1536]{1,0:T(8,128)(2,1)S(1)}, bf16[128,1536]{1,0:T(8,128)(2,1)S(1)}, u32[]{:S(2)}, u32[]{:S(2)}) collective-permute-start(bf16[128,1536]{1,0:T(8,128)(2,1)S(1)} %get-tuple-element.225), channel_id=1, source_target_pairs={{0,16},{8,24},{16,0},{24,8},{1,17},{9,25},{17,1},{25,9},{2,18},{10... | collective-permute-start | bytes 1179656 | tf_op jit(solution)/shard_map/ppermute | solution.py:90
  229.4 12.7 %collective-permute-start.34 = (bf16[384,512]{1,0:T(8,128)(2,1)S(1)}, bf16[384,512]{1,0:T(8,128)(2,1)S(1)}, u32[]{:S(2)}, u32[]{:S(2)}) collective-permute-start(bf16[384,512]{1,0:T(8,128)(2,1)S(1)} %slice.333), channel_id=1, source_target_pairs={{0,1},{1,2},{2,3},{3,0},{4,5},{5,6},{6,7},{7,4},{8,9},{9,10},{10,1... | collective-permute-start | bytes 1179656 | tf_op jit(solution)/shard_map/ppermute | solution.py:140
  242.4 13.0 %collective-permute-start.38 = (bf16[128,1536]{1,0:T(8,128)(2,1)S(1)}, bf16[128,1536]{1,0:T(8,128)(2,1)S(1)}, u32[]{:S(2)}, u32[]{:S(2)}) collective-permute-start(bf16[128,1536]{1,0:T(8,128)(2,1)S(1)} %get-tuple-element.206), channel_id=1, source_target_pairs={{0,24},{8,16},{16,8},{24,0},{1,25},{9,17},{17,9},{25,1},{2,26},{10... | collective-permute-start | bytes 1179656 | tf_op jit(solution)/shard_map/ppermute | solution.py:90
  244.2 15.8 %collective-permute-start.37 = (bf16[128,1536]{1,0:T(8,128)(2,1)S(1)}, bf16[128,1536]{1,0:T(8,128)(2,1)S(1)}, u32[]{:S(2)}, u32[]{:S(2)}) collective-permute-start(bf16[128,1536]{1,0:T(8,128)(2,1)S(1)} %get-tuple-element.206), channel_id=1, source_target_pairs={{0,16},{8,24},{16,0},{24,8},{1,17},{9,25},{17,1},{25,9},{2,18},{10... | collective-permute-start | bytes 1179656 | tf_op jit(solution)/shard_map/ppermute | solution.py:90
  244.9 15.1 %collective-permute-start.36 = (bf16[128,1536]{1,0:T(8,128)(2,1)S(1)}, bf16[128,1536]{1,0:T(8,128)(2,1)S(1)}, u32[]{:S(2)}, u32[]{:S(2)}) collective-permute-start(bf16[128,1536]{1,0:T(8,128)(2,1)S(1)} %get-tuple-element.206), channel_id=1, source_target_pairs={{0,8},{8,0},{16,24},{24,16},{1,9},{9,1},{17,25},{25,17},{2,10},{10... | collective-permute-start | bytes 1179656 | tf_op jit(solution)/shard_map/ppermute | solution.py:90
  281.3 141.9 %reduce-scatter.6.cloned.1.call-start = ((), (), s32[]{:S(2)}) async-start(), calls=%async_computation.4 | async-start | bytes 3932160 | tf_op jit(solution)/shard_map/reduce_scatter | solution.py:286
  285.7 33.1 %collective-permute-start.47 = (bf16[512,1536]{1,0:T(8,128)(2,1)}, bf16[512,1536]{1,0:T(8,128)(2,1)}, u32[]{:S(2)}, u32[]{:S(2)}) collective-permute-start(bf16[512,1536]{1,0:T(8,128)(2,1)} %convolution_convert_fusion.2), channel_id=1, source_target_pairs={{0,4},{4,0},{1,5},{5,1},{2,6},{6,2},{3,7},{7,3},{8,12},{12,8},{9,1... | collective-permute-start | bytes 4718600 | tf_op jit(solution)/shard_map/ppermute | solution.py:87
  289.7 12.1 %collective-permute-start.41 = (bf16[128,1536]{1,0:T(8,128)(2,1)S(1)}, bf16[128,1536]{1,0:T(8,128)(2,1)S(1)}, u32[]{:S(2)}, u32[]{:S(2)}) collective-permute-start(bf16[128,1536]{1,0:T(8,128)(2,1)S(1)} %get-tuple-element.220), channel_id=1, source_target_pairs={{0,8},{8,0},{16,24},{24,16},{1,9},{9,1},{17,25},{25,17},{2,10},{10... | collective-permute-start | bytes 1179656 | tf_op jit(solution)/shard_map/ppermute | solution.py:90
  290.8 19.0 %collective-permute-start.43 = (bf16[128,1536]{1,0:T(8,128)(2,1)S(1)}, bf16[128,1536]{1,0:T(8,128)(2,1)S(1)}, u32[]{:S(2)}, u32[]{:S(2)}) collective-permute-start(bf16[128,1536]{1,0:T(8,128)(2,1)S(1)} %get-tuple-element.221), channel_id=1, source_target_pairs={{0,24},{8,16},{16,8},{24,0},{1,25},{9,17},{17,9},{25,1},{2,26},{10... | collective-permute-start | bytes 1179656 | tf_op jit(solution)/shard_map/ppermute | solution.py:90
  292.2 18.9 %collective-permute-start.42 = (bf16[128,1536]{1,0:T(8,128)(2,1)S(1)}, bf16[128,1536]{1,0:T(8,128)(2,1)S(1)}, u32[]{:S(2)}, u32[]{:S(2)}) collective-permute-start(bf16[128,1536]{1,0:T(8,128)(2,1)S(1)} %get-tuple-element.222), channel_id=1, source_target_pairs={{0,16},{8,24},{16,0},{24,8},{1,17},{9,25},{17,1},{25,9},{2,18},{10... | collective-permute-start | bytes 1179656 | tf_op jit(solution)/shard_map/ppermute | solution.py:90
  315.3 13.2 %collective-permute-start.46 = (bf16[128,1536]{1,0:T(8,128)(2,1)}, bf16[128,1536]{1,0:T(8,128)(2,1)}, u32[]{:S(2)}, u32[]{:S(2)}) collective-permute-start(bf16[128,1536]{1,0:T(8,128)(2,1)} %fusion.80), channel_id=1, source_target_pairs={{0,24},{8,16},{16,8},{24,0},{1,25},{9,17},{17,9},{25,1},{2,26},{10... | collective-permute-start | bytes 1179656 | tf_op jit(solution)/shard_map/ppermute | solution.py:90
  316.8 17.0 %collective-permute-start.45 = (bf16[128,1536]{1,0:T(8,128)(2,1)}, bf16[128,1536]{1,0:T(8,128)(2,1)}, u32[]{:S(2)}, u32[]{:S(2)}) collective-permute-start(bf16[128,1536]{1,0:T(8,128)(2,1)} %fusion.80), channel_id=1, source_target_pairs={{0,16},{8,24},{16,0},{24,8},{1,17},{9,25},{17,1},{25,9},{2,18},{10... | collective-permute-start | bytes 1179656 | tf_op jit(solution)/shard_map/ppermute | solution.py:90
  318.2 15.7 %collective-permute-start.44 = (bf16[128,1536]{1,0:T(8,128)(2,1)}, bf16[128,1536]{1,0:T(8,128)(2,1)}, u32[]{:S(2)}, u32[]{:S(2)}) collective-permute-start(bf16[128,1536]{1,0:T(8,128)(2,1)} %fusion.80), channel_id=1, source_target_pairs={{0,8},{8,0},{16,24},{24,16},{1,9},{9,1},{17,25},{25,17},{2,10},{10... | collective-permute-start | bytes 1179656 | tf_op jit(solution)/shard_map/ppermute | solution.py:90
  322.9 121.7 %reduce-scatter.4.cloned.1.call-start = ((), (), s32[]{:S(2)}) async-start(), calls=%async_computation.3 | async-start | bytes 2211840 | tf_op jit(solution)/shard_map/reduce_scatter | solution.py:326
  342.2 24.2 %collective-permute-start.51 = (bf16[192,1536]{1,0:T(8,128)(2,1)S(1)}, bf16[192,1536]{1,0:T(8,128)(2,1)S(1)}, u32[]{:S(2)}, u32[]{:S(2)}) collective-permute-start(bf16[192,1536]{1,0:T(8,128)(2,1)S(1)} %dynamic-slice_bitcast_fusion), channel_id=1, source_target_pairs={{0,4},{4,0},{1,5},{5,1},{2,6},{6,2},{3,7},{7,3},{8,12},{12,8},{9,1... | collective-permute-start | bytes 1769480 | tf_op jit(solution)/shard_map/ppermute | solution.py:87
  343.9 12.1 %collective-permute-start.48 = (bf16[128,1536]{1,0:T(8,128)(2,1)S(1)}, bf16[128,1536]{1,0:T(8,128)(2,1)S(1)}, u32[]{:S(2)}, u32[]{:S(2)}) collective-permute-start(bf16[128,1536]{1,0:T(8,128)(2,1)S(1)} %get-tuple-element.217), channel_id=1, source_target_pairs={{0,8},{8,0},{16,24},{24,16},{1,9},{9,1},{17,25},{25,17},{2,10},{10... | collective-permute-start | bytes 1179656 | tf_op jit(solution)/shard_map/ppermute | solution.py:90
  345.3 18.7 %collective-permute-start.50 = (bf16[128,1536]{1,0:T(8,128)(2,1)S(1)}, bf16[128,1536]{1,0:T(8,128)(2,1)S(1)}, u32[]{:S(2)}, u32[]{:S(2)}) collective-permute-start(bf16[128,1536]{1,0:T(8,128)(2,1)S(1)} %get-tuple-element.218), channel_id=1, source_target_pairs={{0,24},{8,16},{16,8},{24,0},{1,25},{9,17},{17,9},{25,1},{2,26},{10... | collective-permute-start | bytes 1179656 | tf_op jit(solution)/shard_map/ppermute | solution.py:90
  346.4 19.0 %collective-permute-start.49 = (bf16[128,1536]{1,0:T(8,128)(2,1)S(1)}, bf16[128,1536]{1,0:T(8,128)(2,1)S(1)}, u32[]{:S(2)}, u32[]{:S(2)}) collective-permute-start(bf16[128,1536]{1,0:T(8,128)(2,1)S(1)} %get-tuple-element.219), channel_id=1, source_target_pairs={{0,16},{8,24},{16,0},{24,8},{1,17},{9,25},{17,1},{25,9},{2,18},{10... | collective-permute-start | bytes 1179656 | tf_op jit(solution)/shard_map/ppermute | solution.py:90
  376.5 12.1 %collective-permute-start.57 = (bf16[128,1536]{1,0:T(8,128)(2,1)S(1)}, bf16[128,1536]{1,0:T(8,128)(2,1)S(1)}, u32[]{:S(2)}, u32[]{:S(2)}) collective-permute-start(bf16[128,1536]{1,0:T(8,128)(2,1)S(1)} %get-tuple-element.214), channel_id=1, source_target_pairs={{0,8},{8,0},{16,24},{24,16},{1,9},{9,1},{17,25},{25,17},{2,10},{10... | collective-permute-start | bytes 1179656 | tf_op jit(solution)/shard_map/ppermute | solution.py:90
  377.4 19.1 %collective-permute-start.59 = (bf16[128,1536]{1,0:T(8,128)(2,1)S(1)}, bf16[128,1536]{1,0:T(8,128)(2,1)S(1)}, u32[]{:S(2)}, u32[]{:S(2)}) collective-permute-start(bf16[128,1536]{1,0:T(8,128)(2,1)S(1)} %get-tuple-element.215), channel_id=1, source_target_pairs={{0,24},{8,16},{16,8},{24,0},{1,25},{9,17},{17,9},{25,1},{2,26},{10... | collective-permute-start | bytes 1179656 | tf_op jit(solution)/shard_map/ppermute | solution.py:90
  378.9 19.0 %collective-permute-start.58 = (bf16[128,1536]{1,0:T(8,128)(2,1)S(1)}, bf16[128,1536]{1,0:T(8,128)(2,1)S(1)}, u32[]{:S(2)}, u32[]{:S(2)}) collective-permute-start(bf16[128,1536]{1,0:T(8,128)(2,1)S(1)} %get-tuple-element.216), channel_id=1, source_target_pairs={{0,16},{8,24},{16,0},{24,8},{1,17},{9,25},{17,1},{25,9},{2,18},{10... | collective-permute-start | bytes 1179656 | tf_op jit(solution)/shard_map/ppermute | solution.py:90
  428.5 10.9 %collective-permute-start.55 = (bf16[2,48,1024]{2,1,0:T(8,128)(2,1)S(1)}, bf16[2,48,1024]{2,1,0:T(8,128)(2,1)S(1)}, u32[]{:S(2)}, u32[]{:S(2)}) collective-permute-start(bf16[2,48,1024]{2,1,0:T(8,128)(2,1)S(1)} %get-tuple-element.242), channel_id=1, source_target_pairs={{0,16},{8,24},{16,0},{24,8},{1,17},{9,25},{17,1},{25,9},{2,18},{10... | collective-permute-start | bytes 589832 | tf_op jit(solution)/shard_map/ppermute | solution.py:90
  428.5 10.9 %collective-permute-start.56 = (bf16[2,48,1024]{2,1,0:T(8,128)(2,1)S(1)}, bf16[2,48,1024]{2,1,0:T(8,128)(2,1)S(1)}, u32[]{:S(2)}, u32[]{:S(2)}) collective-permute-start(bf16[2,48,1024]{2,1,0:T(8,128)(2,1)S(1)} %get-tuple-element.243), channel_id=1, source_target_pairs={{0,24},{8,16},{16,8},{24,0},{1,25},{9,17},{17,9},{25,1},{2,26},{10... | collective-permute-start | bytes 589832 | tf_op jit(solution)/shard_map/ppermute | solution.py:90
  (93 other events, 1218.8 us)
Sparse Core Ops, SparseCore 0:
  281.4 33.2 reduce-scatter.7
  323.1 57.7 reduce-scatter.5
  407.3 35.8 reduce-scatter.3

commit v5 on v4

--- a/solution.py
+++ b/solution.py
@@ -142,17 +142,40 @@
     def ring_first(a):
         return along_z(a, 1), along_z(a, -1)
 
-    def ring_rest(a, right, left):
+    def second_right(right):
+        return along_z(right[..., : right.shape[-1] // 2] if rows_z == 4 else right, 1)
+
+    def ring_rest(a, right, left, following=None):
         found = [(a, 0, 0), (right, -1, 0), (left, 1, 0)]
         for step in range(2, rows_z // 2 + 1):
             if 2 * step == rows_z:
                 half = a.shape[-1] // 2
-                found.append((along_z(right[..., :half], 1), -step, 0))
+                low = along_z(right[..., :half], 1) if following is None else following
+                found.append((low, -step, 0))
                 found.append((along_z(left[..., half:], -1), step, half))
             else:
-                right, left = along_z(right, 1), along_z(left, -1)
+                right = along_z(right, 1) if following is None else following
+                left = along_z(left, -1)
                 found += [(right, -step, 0), (left, step, 0)]
+            following = None
         return found
+
+    windows = [2 + (rows_z - 1) * w // 3 for w in range(4)]
+
+    def part(a, index, start):
+        index = lax.rem(index + 2 * rows_z, rows_z)
+        size = (a.shape[0], 1, a.shape[2], a.shape[3] // 2)
+        return lax.dynamic_slice(a, (0, index, 0, start), size)
+
+    def scatter_begin(a):
+        return part(a, place - 1, 0), part(a, place + 1, a.shape[3] // 2)
+
+    def scatter_window(a, sums, window):
+        low, high = sums
+        for step in range(windows[window], windows[window + 1]):
+            low = along_z(low, 1) + part(a, place - step, 0)
+            high = along_z(high, -1) + part(a, place + step, a.shape[3] // 2)
+        return low, high
 
     def assemble(found, groups):
         rows, cols = found[0][0].shape
@@ -164,11 +187,19 @@
         return whole
 
     owner = (chip * 2 + core) * rows_z + place
-    gains = lax.all_gather(
-        jnp.stack([attn_gain, mlp_gain]), ("chip", "core", "fsdp"), axis=1, tiled=True
-    )
-    marks = jnp.stack([positions[:, 0], segments[:, 0]])
-    marks = lax.all_gather(marks, ("chip", "core"), axis=0)
+    spot = chip * 2 + core
+    spots = chips * 2
+    gains = lax.dynamic_update_slice(
+        jnp.zeros((2, width), f32),
+        jnp.stack([attn_gain, mlp_gain]).astype(f32),
+        (0, owner * d_rows),
+    )
+    marks = lax.dynamic_update_slice(
+        jnp.zeros((4, spots * tok), f32),
+        jnp.concatenate([positions[:, 0], segments[:, 0]]).astype(f32),
+        (0, spot * tok),
+    )
+    table = jnp.concatenate([gains.reshape(-1), marks.reshape(-1)]).reshape(-1, 128)
 
     def sum_chips(a):
         bit = 1
@@ -184,48 +215,59 @@
             bit *= 2
         return a
 
-    down_right, down_left = ring_first(w_down)
+    out_right, out_left = ring_first(w_out)
+    along_down = lax.all_gather(w_down, "fsdp", axis=0, tiled=True)
+    pack_qkv = chip_slices((w_query, w_key, w_value), (q_cols, kv_cols, kv_cols))
+    piece_qkv = exchange_chips(pack_qkv).reshape(-1, pack_qkv.shape[-1])
     pair = jnp.stack([block_input[:, 0], out_cotangent[:, 0]], axis=1)
     pair = jnp.concatenate([pick(pair, core), core_swap(pick(pair, 1 - core))], axis=1)
-    pack_qkv = chip_slices((w_query, w_key, w_value), (q_cols, kv_cols, kv_cols))
-    piece_qkv = exchange_chips(pack_qkv).reshape(-1, pack_qkv.shape[-1])
+    table = table + core_swap(table)
+    pair, piece_qkv, table = tie(pair, piece_qkv, table)
+    x_low, dy_low = pair[0], pair[1]
+
+    x_all = gather_chips(x_low)
+    qkv_right, qkv_left = ring_first(piece_qkv)
     pack_gu = jnp.stack(
         [
             jnp.concatenate([w[:, n * ff_cols : (n + 1) * ff_cols] for w in (w_gate, w_up)], axis=1)
             for n in range(2 * chips)
         ]
     ).reshape(chips, 2, d_rows, 2 * ff_cols)
-    pair, piece_qkv, pack_gu = tie(pair, piece_qkv, pack_gu)
-
-    x_low, dy_low = pair[0], pair[1]
-    x_all = gather_chips(x_low)
-    piece_qkv, down_right, down_left = tie(piece_qkv, down_right, down_left)
-    qkv_right, qkv_left = ring_first(piece_qkv)
-    x_all, qkv_right, qkv_left, pack_gu = tie(x_all, qkv_right, qkv_left, pack_gu)
+    table = sum_chips(table)
+    qkv_right, qkv_left, pack_gu, out_right, out_left, table = tie(
+        qkv_right, qkv_left, pack_gu, out_right, out_left, table
+    )
+    gains = sum_z(table.reshape(-1)[: 2 * width].reshape(2, width))
+    marks = pick(table.reshape(-1)[2 * width :].reshape(2, 2, spots, tok), core, 1)
+    marks = jnp.concatenate(
+        [pick(marks, (chip ^ k) * 2 + (core ^ c), 1) for k in range(chips) for c in range(2)],
+        axis=1,
+    )
+    found_qkv = ring_rest(piece_qkv, qkv_right, qkv_left)
+    x_all, pack_gu, out_right, out_left, gains, marks, *late = tie(
+        x_all, pack_gu, out_right, out_left, gains, marks, *[f[0] for f in found_qkv]
+    )
+    found_qkv = [(piece,) + f[1:] for piece, f in zip(late, found_qkv)]
 
     piece_gu = exchange_chips(pack_gu)
-    found_qkv = ring_rest(piece_qkv, qkv_right, qkv_left)
-    *late, piece_gu, w_out = tie(*[f[0] for f in found_qkv], piece_gu, w_out)
-    found_qkv = [(piece,) + f[1:] for piece, f in zip(late, found_qkv)]
-    out_right, out_left = ring_first(w_out)
+    found_out = ring_rest(w_out, out_right, out_left)
+    w_qkv = assemble(found_qkv, chips)
+    w_qkv = core_pair(w_qkv, core_swap(w_qkv), 1).reshape(width, -1)
     piece_gu = core_pair(pick(piece_gu, core, 1), core_swap(pick(piece_gu, 1 - core, 1)), 1)
     piece_gu = piece_gu.reshape(2 * chips * d_rows, 2 * ff_cols)
-    w_qkv = assemble(found_qkv, chips)
-    w_qkv = core_pair(w_qkv, core_swap(w_qkv), 1).reshape(width, -1)
-    w_qkv, piece_gu, out_right, out_left, dy_low = tie(w_qkv, piece_gu, out_right, out_left, dy_low)
-    gu_right, gu_left = ring_first(piece_gu)
-    gain_one, gain_two = gains.astype(f32)
-    marks = pick(marks.reshape(chips, 2, 2, 2, tok), core, 3).astype(f32)
-    marks = jnp.where(core == 0, marks, jnp.flip(marks, axis=1))
-    marks_all = by_chip([marks[k] for k in range(chips)])
-    marks_all = jnp.transpose(marks_all, (2, 0, 1, 3)).reshape(2, chips * 2 * tok)
+    gain_one, gain_two = gains
+    pos_all, seg_all = marks
+    allowed = (seg_all[:, None] == seg_all[None, :]) & (pos_all[None, :] <= pos_all[:, None])
+    cosine, sine = rope_tables(pos_all)
+    w_qkv, piece_gu, dy_low, cosine, sine, allowed, *late = tie(
+        w_qkv, piece_gu, dy_low, cosine, sine, allowed, *[f[0] for f in found_out]
+    )
+    found_out = [(piece,) + f[1:] for piece, f in zip(late, found_out)]
+    gu_right = along_z(piece_gu, 1)
     own = x_low.shape[0]
     seq = x_all.shape[0]
 
     dy_all = gather_chips(dy_low)
-    pos_all, seg_all = marks_all[0], marks_all[1]
-    allowed = (seg_all[:, None] == seg_all[None, :]) & (pos_all[None, :] <= pos_all[:, None])
-    cosine, sine = rope_tables(pos_all)
     x_full = x_all.astype(f32)
     h_one = (x_full * rms_scale(x_full) * gain_one).astype(bf16)
     qkv = mm(h_one, w_qkv)
@@ -235,30 +277,25 @@
         qkv[:, q_cols : q_cols + kv_cols].reshape(seq, kv_heads, HEAD), cosine, sine
     ).astype(bf16)
     value = qkv[:, q_cols + kv_cols :].astype(bf16).reshape(seq, kv_heads, HEAD)
-    q_rot, dy_all, out_right, out_left = tie(q_rot, dy_all, out_right, out_left)
-    out_w = assemble(ring_rest(w_out, out_right, out_left), 1).reshape(rows_z * d_rows, width)
+    out_w = assemble(found_out, 1).reshape(rows_z * d_rows, width)
     out_w = both_cores(out_w).reshape(-1, width)
     scores = jnp.einsum("sgrh,tgh->grst", q_rot, k_rot, preferred_element_type=f32) * factor
     scores = jnp.where(allowed, scores, -1e30)
     raised = jnp.exp(scores - jnp.max(scores, axis=-1, keepdims=True))
     soft = raised / jnp.sum(raised, axis=-1, keepdims=True)
-    soft_low, out_w, down_right, down_left = tie(
-        soft.astype(bf16), out_w, down_right, down_left
-    )
-    found_down = ring_rest(w_down, down_right, down_left)
+    soft_low = soft.astype(bf16)
     mixed = jnp.einsum("grst,tgh->sgrh", soft_low, value, preferred_element_type=f32)
     mixed = mixed.astype(bf16).reshape(seq, q_cols)
-    mixed, gu_right, gu_left, *late = tie(mixed, gu_right, gu_left, *[f[0] for f in found_down])
-    found_down = [(piece,) + f[1:] for piece, f in zip(late, found_down)]
-    found_gu = ring_rest(piece_gu, gu_right, gu_left)
+    mixed, dy_all, out_w, gu_right, piece_gu = tie(mixed, dy_all, out_w, gu_right, piece_gu)
+    gu_left = along_z(piece_gu, -1)
+    gu_next = second_right(gu_right)
     x_own = x_low.astype(f32)
     middle = x_own + scatter_chips(mm(mixed, out_w))
 
     dy_both = jnp.concatenate([dy_all, core_swap(dy_all)])
-    down_w = assemble(found_down, 1).reshape(-1, width)
-    d_act = mm_nt(dy_both, down_w)
-    middle, dy_both, d_act, *late = tie(middle, dy_both, d_act, *[f[0] for f in found_gu])
-    found_gu = [(piece,) + f[1:] for piece, f in zip(late, found_gu)]
+    d_act = mm_nt(dy_both, along_down)
+    middle, dy_both, d_act, gu_left, gu_next = tie(middle, dy_both, d_act, gu_left, gu_next)
+    found_gu = ring_rest(piece_gu, gu_right, gu_left, gu_next)
     scale_two = rms_scale(middle)
     n_two = middle * scale_two
     h_two = gather_chips((n_two * gain_two).astype(bf16))
@@ -279,19 +316,21 @@
         other = core_swap(product(rows[seq:], weights).astype(bf16)).astype(f32)
         return product(rows[:seq], weights) + other
 
-    d_h_two = scatter_chips(give_partial(d_gu, w_gu, mm_nt))
+    d_h_two = give_partial(d_gu, w_gu, mm_nt)
     g_gu = mm_tn(h_both, d_gu).astype(bf16).reshape(2 * chips, rows_z, d_rows, 2 * ff_cols)
-    g_gu = jnp.transpose(g_gu, (1, 0, 2, 3)).reshape(width, 2 * ff_cols)
     d_h_two, g_gu = tie(d_h_two, g_gu)
-    g_gu = lax.psum_scatter(g_gu, "fsdp", scatter_dimension=0, tiled=True)
+    sums = scatter_window(g_gu, scatter_begin(g_gu), 0)
+    d_h_two, *sums = tie(scatter_chips(d_h_two), *sums)
 
     dy_own = dy_low.astype(f32)
     gain_two_part = jnp.sum(d_h_two * n_two, axis=0)
     d_middle = dy_own + norm_back(d_h_two * gain_two, n_two, scale_two)
     branch = gather_chips(d_middle.astype(bf16))
-    partial = give_partial(act, down_w, mm)
-    branch, partial = tie(branch, partial)
-    result = (middle + scatter_chips(partial)).astype(bf16)
+    partial = give_partial(act, along_down, mm)
+    sums = scatter_window(g_gu, sums, 1)
+    branch, partial, g_down, *sums = tie(branch, partial, g_down, *sums)
+    sums = scatter_window(g_gu, sums, 2)
+    result = partial
 
     g_out = mm_tn(mixed, branch).astype(bf16)
     g_out = g_out.reshape(2, g_out.shape[0] // 2, g_out.shape[1])
@@ -313,18 +352,25 @@
         ],
         axis=1,
     )
-    d_qkv, result, g_out = tie(d_qkv, result, g_out)
+    d_qkv, g_out, *sums = tie(d_qkv, g_out, *sums)
+    g_gu = jnp.concatenate(sums, axis=-1)
     cols_qkv = d_qkv.shape[1]
     g_qkv = mm_tn(h_one, d_qkv).astype(bf16).reshape(chips, 2, rows_z, d_rows, cols_qkv)
     g_qkv = pick(g_qkv, core, 1) + core_swap(pick(g_qkv, 1 - core, 1))
-    g_qkv = jnp.transpose(g_qkv, (1, 0, 2, 3)).reshape(rows_z, chips * d_rows, cols_qkv)
+    g_qkv = jnp.transpose(g_qkv, (1, 0, 2, 3)).reshape(1, rows_z, chips * d_rows, cols_qkv)
     folds = width // cols_qkv
-    g_out = g_out.reshape(rows_z, d_rows, width)
-    g_rest = [g_out[:, :, k * cols_qkv : (k + 1) * cols_qkv] for k in range(folds)]
-    g_rest = jnp.concatenate([g_qkv] + g_rest, axis=1)
-    g_rest, d_qkv = tie(g_rest.reshape(-1, cols_qkv), d_qkv)
-    g_rest = lax.psum_scatter(g_rest, "fsdp", scatter_dimension=0, tiled=True)
-    d_h_one = scatter_chips(mm_nt(d_qkv, w_qkv))
+    g_out = g_out.reshape(1, rows_z, d_rows, width)
+    g_rest = [g_out[..., k * cols_qkv : (k + 1) * cols_qkv] for k in range(folds)]
+    g_rest = jnp.concatenate([g_qkv] + g_rest, axis=2)
+    d_h_one = mm_nt(d_qkv, w_qkv)
+    g_rest, d_h_one = tie(g_rest, d_h_one)
+    sums = scatter_window(g_rest, scatter_begin(g_rest), 0)
+    d_h_one, result, *sums = tie(scatter_chips(d_h_one), result, *sums)
+    sums = scatter_window(g_rest, sums, 1)
+    result, *sums = tie(scatter_chips(result), *sums)
+    result = (middle + result).astype(bf16)
+    sums = scatter_window(g_rest, sums, 2)
+    g_rest = jnp.concatenate(sums, axis=-1).reshape(-1, cols_qkv)
     scale_one = rms_scale(x_own)
     n_one = x_own * scale_one
     gain_one_part = jnp.sum(d_h_one * n_one, axis=0)

time: 471 us -> 436 us (0.926)
  blocking collectives: 77.8 us -> 0 us
  starting transfers between devices: 67.7 us -> 102 us
  waiting for transfers between devices: 169 us -> 184 us
  matrix products: 41.4 us -> 51.2 us
  other arithmetic: 43.7 us -> 33.9 us
  local copies, waits for them, and re-layouts: 47.8 us -> 40.4 us
    ppermute x16 -> x24, waiting for transfers between devices: 28.3 us -> 112 us  [along_z(): lax.ppermute(a, 'fsdp', [(i, (i + step) % rows_z) for i in range(rows_z)])]
    all_gather x2 -> x0, blocking collectives: 77.8 us -> none  [the longest x1 68.7 us: on_device(): lax.all_gather(jnp.stack([attn_gain, mlp_gain]), ('chip', 'core', 'fsdp')...]
    ppermute x38 -> x40, waiting for transfers between devices: 129 us -> 62.6 us  [chip_xor(): return lax.ppermute(a, 'chip', [(i, i ^ j) for i in range(chips)])]
    ppermute x16 -> x24, starting transfers between devices: 20 us -> 48.7 us  [along_z(): lax.ppermute(a, 'fsdp', [(i, (i + step) % rows_z) for i in range(rows_z)])]
    dot_general x4, matrix products: 9.12 us -> 15 us  [mm_tn(): return jnp.einsum('td,te->de', a, b, preferred_element_type=f32)]
    ppermute x2 -> x4, starting transfers between devices: 0.14 us -> 5.48 us  [sum_z(): a = a + lax.ppermute(a, 'fsdp', [(i, i ^ bit) for i in range(rows_z)])]
    dot_general x5, matrix products: 11.5 us -> 16.5 us  [mm_nt(): return jnp.einsum('te,de->td', a, b, preferred_element_type=f32)]
    add x0 -> x7, other arithmetic: none -> 4.91 us  [the longest x5 3.06 us: scatter_window(): high = along_z(high, -1) + part(a, place + step, a.shape[3] // 2)]
  transfers between devices with their start and end apart: 73 -> 85, of which waited for: 40 -> 39; matrix products, arithmetic and copies ran while one was open for 22% -> 21% of each run, Pallas kernels for 0% -> 0%
where the time goes in v5:
time: 436 us; the launch traced here: 428 us
  waiting for transfers between devices  184 us (42%)
  starting transfers between devices  102 us (23%)
  matrix products  51.2 us (12%)
  local copies, waits for them, and re-layouts  40.4 us (9%)
  other arithmetic  33.9 us (8%)
  between operations  16.2 us (4%)
    ppermute x24, waiting for transfers between devices, along_z(): lax.ppermute(a, 'fsdp', [(i, (i + step) % rows_z) for i in range(rows_z)])  112 us
    ppermute x40, waiting for transfers between devices, chip_xor(): return lax.ppermute(a, 'chip', [(i, i ^ j) for i in range(chips)])  62.6 us
    ppermute x24, starting transfers between devices, along_z(): lax.ppermute(a, 'fsdp', [(i, (i + step) % rows_z) for i in range(rows_z)])  48.7 us
    ppermute x40, starting transfers between devices, chip_xor(): return lax.ppermute(a, 'chip', [(i, i ^ j) for i in range(chips)])  45.9 us
    dot_general x5, matrix products, mm_nt(): return jnp.einsum('te,de->td', a, b, preferred_element_type=f32)  16.5 us
    dot_general x4, matrix products, mm_tn(): return jnp.einsum('td,te->de', a, b, preferred_element_type=f32)  15 us
    unnamed x130, local copies, waits for them, and re-layouts  10.4 us
    dot_general x5, matrix products, mm(): return jnp.dot(a, b, preferred_element_type=f32)  9.51 us
  transfers between devices with their start and end apart: 85, of which 39 were waited for; matrix products, arithmetic and copies ran while one was open for 21% of the time, Pallas kernels for 0%

profile of v5, /device:TPU:0, one launch (start us, length us, event | category | flops | bytes accessed | tf_op | source)
XLA Modules:
  0.0 427.9 jit_solution(2981456512974882529)
XLA Ops:
  7.3 3.1 collective-permute-start.10
  16.2 2.6 collective-permute-start.3
  23.4 2.9 collective-permute-done.2
  29.1 3.8 collective-permute-start.9
  37.2 9.9 %collective-permute-done.8 = bf16[192,768]{1,0:T(8,128)(2,1)S(1)} collective-permute-done((bf16[192,768]{1,0:T(8,128)(2,1)S(1)}, bf16[192,768]{1,0:T(8,128)(2,1)S(1)}, u32[]{:S(2)}, u32[]{:S(2)}) %collective-permute-start.8) | collective-permute-done | bytes 294944 | tf_op jit(solution)/shard_map/ppermute | solution.py:140
  47.1 10.4 %collective-permute-done.9 = bf16[192,768]{1,0:T(8,128)(2,1)S(1)} collective-permute-done((bf16[192,768]{1,0:T(8,128)(2,1)S(1)}, bf16[192,768]{1,0:T(8,128)(2,1)S(1)}, u32[]{:S(2)}, u32[]{:S(2)}) %collective-permute-start.9) | collective-permute-done | bytes 294944 | tf_op jit(solution)/shard_map/ppermute | solution.py:140
  64.8 4.2 collective-permute-done.15
  69.1 3.8 collective-permute-start.17
  84.5 2.9 collective-permute-start.24
  107.3 4.7 %fusion.87 = (f32[2,2,512]{2,1,0:T(2,128)S(1)}, f32[2,2,512,512]{2,3,1,0:T(8,128)}) fusion(pred[512,512]{0,1:T(8,128)(4,1)} %compare_and_fusion, bf16[512,2,2,48]{0,3,2,1:T(8,128)(2,1)S(1)} %bitcast.424, bf16[512,2,2,48]{0,3,2,1:T(8,128)(2,1)S(1)} %bitcast.422, bf16[512,2,48]{0,2,1:T(8,128)(2,1)} %get-tuple-element.272, ...), kind=kOutput, calls=%fused_computation.291 | convolution fusion | flops 206701056 | bytes 5054464 | tf_op jit(solution)/shard_map/sub | solution.py:284
  112.1 2.7 convolution_convert_fusion.6
  117.8 10.7 %collective-permute-done.29 = bf16[384,1024]{1,0:T(8,128)(2,1)S(1)} collective-permute-done((bf16[384,1024]{1,0:T(8,128)(2,1)S(1)}, bf16[384,1024]{1,0:T(8,128)(2,1)S(1)}, u32[]{:S(2)}, u32[]{:S(2)}) %collective-permute-start.29) | collective-permute-done | bytes 786464 | tf_op jit(solution)/shard_map/ppermute | solution.py:140
  136.7 4.9 %collective-permute-done.30 = bf16[128,1536]{1,0:T(8,128)(2,1)S(1)} collective-permute-done((bf16[128,1536]{1,0:T(8,128)(2,1)S(1)}, bf16[128,1536]{1,0:T(8,128)(2,1)S(1)}, u32[]{:S(2)}, u32[]{:S(2)}) %collective-permute-start.30) | collective-permute-done | bytes 393248 | tf_op jit(solution)/shard_map/ppermute | solution.py:90
  141.6 9.3 %collective-permute-done.31 = bf16[128,1536]{1,0:T(8,128)(2,1)S(1)} collective-permute-done((bf16[128,1536]{1,0:T(8,128)(2,1)S(1)}, bf16[128,1536]{1,0:T(8,128)(2,1)S(1)}, u32[]{:S(2)}, u32[]{:S(2)}) %collective-permute-start.31) | collective-permute-done | bytes 393248 | tf_op jit(solution)/shard_map/ppermute | solution.py:90
  153.0 4.2 fusion.89
  157.2 3.5 collective-permute-done.35
  164.6 8.5 %collective-permute-done.36 = bf16[128,1536]{1,0:T(8,128)(2,1)S(1)} collective-permute-done((bf16[128,1536]{1,0:T(8,128)(2,1)S(1)}, bf16[128,1536]{1,0:T(8,128)(2,1)S(1)}, u32[]{:S(2)}, u32[]{:S(2)}) %collective-permute-start.36) | collective-permute-done | bytes 393248 | tf_op jit(solution)/shard_map/ppermute | solution.py:90
  173.1 7.7 %collective-permute-done.37 = bf16[128,1536]{1,0:T(8,128)(2,1)S(1)} collective-permute-done((bf16[128,1536]{1,0:T(8,128)(2,1)S(1)}, bf16[128,1536]{1,0:T(8,128)(2,1)S(1)}, u32[]{:S(2)}, u32[]{:S(2)}) %collective-permute-start.37) | collective-permute-done | bytes 393248 | tf_op jit(solution)/shard_map/ppermute | solution.py:90
  182.0 4.8 %collective-permute-start.40 = (bf16[384,512]{1,0:T(8,128)(2,1)S(1)}, bf16[384,512]{1,0:T(8,128)(2,1)S(1)}, u32[]{:S(2)}, u32[]{:S(2)}) collective-permute-start(bf16[384,512]{1,0:T(8,128)(2,1)S(1)} %slice.321), channel_id=1, source_target_pairs={{0,3},{1,0},{2,1},{3,2},{4,7},{5,4},{6,5},{7,6},{8,11},{9,8},{10,9... | collective-permute-start | bytes 1179656 | tf_op jit(solution)/shard_map/ppermute | solution.py:140
  189.6 6.3 %collective-permute-done.40 = bf16[384,512]{1,0:T(8,128)(2,1)S(1)} collective-permute-done((bf16[384,512]{1,0:T(8,128)(2,1)S(1)}, bf16[384,512]{1,0:T(8,128)(2,1)S(1)}, u32[]{:S(2)}, u32[]{:S(2)}) %collective-permute-start.40) | collective-permute-done | bytes 393248 | tf_op jit(solution)/shard_map/ppermute | solution.py:140
  198.6 3.4 fusion.90
  205.4 4.9 %convolution_convert_fusion.4 = bf16[512,1536]{1,0:T(8,128)(2,1)} fusion(bf16[1024,512]{1,0:T(8,128)(2,1)S(1)} %get-tuple-element.130, bf16[1024,1536]{1,0:T(8,128)(2,1)} %constant_dynamic-update-slice_fusion.2), kind=kOutput, calls=%fused_computation.20 | convolution fusion | flops 1611399168 | bytes 5767168 | tf_op jit(solution)/shard_map/td,te->de/dot_general | solution.py:50
  210.3 5.2 %convolution_convert_fusion.3 = bf16[512,1536]{1,0:T(8,128)(2,1)} fusion(bf16[1536,1024]{1,0:T(8,128)(2,1)} %bitcast.378, bf16[1024,1024]{1,0:T(8,128)(2,1)} %pad_maximum_fusion.1), kind=kOutput, calls=%fused_computation.19 | convolution fusion | flops 1611399168 | bytes 5767168 | tf_op jit(solution)/shard_map/te,de->td/dot_general | solution.py:54
  215.6 6.2 %convolution_convert_fusion = bf16[1536,1024]{1,0:T(8,128)(2,1)S(1)} fusion(bf16[1024,1536]{1,0:T(8,128)(2,1)} %copy-done.43, bf16[1024,1024]{1,0:T(8,128)(2,1)} %pad_maximum_fusion.1), kind=kOutput, calls=%fused_computation.10 | convolution fusion | flops 3222798336 | bytes 8388608 | tf_op jit(solution)/shard_map/td,te->de/dot_general | solution.py:50
  221.8 4.9 %convolution_add_fusion = f32[512,1536]{1,0:T(8,128)S(1)} fusion(bf16[1536,1024]{1,0:T(8,128)(2,1)S(1)} %bitcast.379, bf16[512,1536]{1,0:T(8,128)(2,1)} %collective-permute-done.41, bf16[1024,1024]{1,0:T(8,128)(2,1)S(1)} %copy-done.16), kind=kOutput, calls=%fused_computation.12 | convolution fusion | flops 1612185600 | bytes 8912896 | tf_op jit(solution)/shard_map/te,de->td/dot_general | solution.py:54
  227.1 4.0 collective-permute-start.46
  236.0 13.5 %collective-permute-done.45 = bf16[8,1,48,512]{3,2,1,0:T(8,128)(2,1)S(1)} collective-permute-done((bf16[8,1,48,512]{3,2,1,0:T(8,128)(2,1)S(1)}, bf16[8,1,48,512]{3,2,1,0:T(8,128)(2,1)S(1)}, u32[]{:S(2)}, u32[]{:S(2)}) %collective-permute-start.45) | collective-permute-done | bytes 393248 | tf_op jit(solution)/shard_map/ppermute | solution.py:140
  249.5 15.6 %collective-permute-done.46 = bf16[8,1,48,512]{3,2,1,0:T(8,128)(2,1)S(1)} collective-permute-done((bf16[8,1,48,512]{3,2,1,0:T(8,128)(2,1)S(1)}, bf16[8,1,48,512]{3,2,1,0:T(8,128)(2,1)S(1)}, u32[]{:S(2)}, u32[]{:S(2)}) %collective-permute-start.46) | collective-permute-done | bytes 393248 | tf_op jit(solution)/shard_map/ppermute | solution.py:140
  273.9 2.7 convert_add_fusion
  276.6 7.3 %collective-permute-done.51 = bf16[8,1,48,512]{3,2,1,0:T(8,128)(2,1)S(1)} collective-permute-done((bf16[8,1,48,512]{3,2,1,0:T(8,128)(2,1)S(1)}, bf16[8,1,48,512]{3,2,1,0:T(8,128)(2,1)S(1)}, u32[]{:S(2)}, u32[]{:S(2)}) %collective-permute-start.51) | collective-permute-done | bytes 393248 | tf_op jit(solution)/shard_map/ppermute | solution.py:140
  283.9 6.3 %collective-permute-done.52 = bf16[8,1,48,512]{3,2,1,0:T(8,128)(2,1)S(1)} collective-permute-done((bf16[8,1,48,512]{3,2,1,0:T(8,128)(2,1)S(1)}, bf16[8,1,48,512]{3,2,1,0:T(8,128)(2,1)S(1)}, u32[]{:S(2)}, u32[]{:S(2)}) %collective-permute-start.52) | collective-permute-done | bytes 393248 | tf_op jit(solution)/shard_map/ppermute | solution.py:140
  292.3 2.3 convolution_convert_fusion.5
  302.2 3.4 collective-permute-start.55
  306.1 9.4 %collective-permute-done.54 = bf16[8,1,48,512]{3,2,1,0:T(8,128)(2,1)S(1)} collective-permute-done((bf16[8,1,48,512]{3,2,1,0:T(8,128)(2,1)S(1)}, bf16[8,1,48,512]{3,2,1,0:T(8,128)(2,1)S(1)}, u32[]{:S(2)}, u32[]{:S(2)}) %collective-permute-start.54) | collective-permute-done | bytes 393248 | tf_op jit(solution)/shard_map/ppermute | solution.py:140
  315.5 6.0 %collective-permute-done.55 = bf16[8,1,48,512]{3,2,1,0:T(8,128)(2,1)S(1)} collective-permute-done((bf16[8,1,48,512]{3,2,1,0:T(8,128)(2,1)S(1)}, bf16[8,1,48,512]{3,2,1,0:T(8,128)(2,1)S(1)}, u32[]{:S(2)}, u32[]{:S(2)}) %collective-permute-start.55) | collective-permute-done | bytes 393248 | tf_op jit(solution)/shard_map/ppermute | solution.py:140
  329.8 3.5 collective-permute-start.61
  337.3 2.3 collective-permute-done.60
  342.8 2.8 collective-permute-done.57
  347.3 6.8 %collective-permute-done.58 = bf16[128,1536]{1,0:T(8,128)(2,1)S(1)} collective-permute-done((bf16[128,1536]{1,0:T(8,128)(2,1)S(1)}, bf16[128,1536]{1,0:T(8,128)(2,1)S(1)}, u32[]{:S(2)}, u32[]{:S(2)}) %collective-permute-start.58) | collective-permute-done | bytes 393248 | tf_op jit(solution)/shard_map/ppermute | solution.py:90
  355.1 3.3 collective-permute-done.70
  358.3 2.9 collective-permute-done.71
  362.9 2.2 collective-permute-done.74
  366.9 3.8 collective-permute-start.66
  373.1 2.8 collective-permute-done.76
  378.1 2.4 collective-permute-start.77
  383.1 4.8 %collective-permute-done.63 = bf16[128,1536]{1,0:T(8,128)(2,1)S(1)} collective-permute-done((bf16[128,1536]{1,0:T(8,128)(2,1)S(1)}, bf16[128,1536]{1,0:T(8,128)(2,1)S(1)}, u32[]{:S(2)}, u32[]{:S(2)}) %collective-permute-start.63) | collective-permute-done | bytes 393248 | tf_op jit(solution)/shard_map/ppermute | solution.py:90
  401.6 3.8 collective-permute-done.67
  405.4 3.8 collective-permute-done.68
  (456 shorter events, 160.8 us)
Async XLA Ops:
  7.2 145.8 %all-gather.2.cloned.1.call-start = ((), (), s32[]{:S(2)}) async-start(), calls=%async_computation.1 | async-start | bytes 1966080 | tf_op jit(solution)/shard_map/all_gather | solution.py:219
  7.3 26.3 %collective-permute-start.10 = (bf16[48,1536]{1,0:T(8,128)(2,1)}, bf16[48,1536]{1,0:T(8,128)(2,1)S(1)}, u32[]{:S(2)}, u32[]{:S(2)}) collective-permute-start(bf16[48,1536]{1,0:T(8,128)(2,1)} %param.21), channel_id=1, source_target_pairs={{0,1},{1,2},{2,3},{3,0},{4,5},{5,6},{6,7},{7,4},{8,9},{9,10},{10,1... | collective-permute-start | bytes 442376 | tf_op jit(solution)/shard_map/ppermute | solution.py:140
  10.4 23.6 %collective-permute-start.11 = (bf16[48,1536]{1,0:T(8,128)(2,1)}, bf16[48,1536]{1,0:T(8,128)(2,1)}, u32[]{:S(2)}, u32[]{:S(2)}) collective-permute-start(bf16[48,1536]{1,0:T(8,128)(2,1)} %param.21), channel_id=1, source_target_pairs={{0,3},{1,0},{2,1},{3,2},{4,7},{5,4},{6,5},{7,6},{8,11},{9,8},{10,9... | collective-permute-start | bytes 442376 | tf_op jit(solution)/shard_map/ppermute | solution.py:140
  19.9 272.5 %reduce-scatter.2.cloned.1.call-start = ((), (), s32[]{:S(2)}) async-start(), calls=%async_computation.2 | async-start | bytes 1966080 | tf_op jit(solution)/shard_map/reduce_scatter | solution.py:313
  29.0 18.1 %collective-permute-start.8 = (bf16[192,768]{1,0:T(8,128)(2,1)S(1)}, bf16[192,768]{1,0:T(8,128)(2,1)S(1)}, u32[]{:S(2)}, u32[]{:S(2)}) collective-permute-start(bf16[192,768]{1,0:T(8,128)(2,1)S(1)} %bitcast.415), channel_id=1, source_target_pairs={{0,1},{1,2},{2,3},{3,0},{4,5},{5,6},{6,7},{7,4},{8,9},{9,10},{10,1... | collective-permute-start | bytes 884744 | tf_op jit(solution)/shard_map/ppermute | solution.py:140
  29.1 28.4 %collective-permute-start.9 = (bf16[192,768]{1,0:T(8,128)(2,1)S(1)}, bf16[192,768]{1,0:T(8,128)(2,1)S(1)}, u32[]{:S(2)}, u32[]{:S(2)}) collective-permute-start(bf16[192,768]{1,0:T(8,128)(2,1)S(1)} %bitcast.416), channel_id=1, source_target_pairs={{0,3},{1,0},{2,1},{3,2},{4,7},{5,4},{6,5},{7,6},{8,11},{9,8},{10,9... | collective-permute-start | bytes 884744 | tf_op jit(solution)/shard_map/ppermute | solution.py:140
  33.5 39.3 %collective-permute-start.5 = (bf16[128,1536]{1,0:T(8,128)(2,1)S(1)}, bf16[128,1536]{1,0:T(8,128)(2,1)}, u32[]{:S(2)}, u32[]{:S(2)}) collective-permute-start(bf16[128,1536]{1,0:T(8,128)(2,1)S(1)} %get-tuple-element.256), channel_id=1, source_target_pairs={{0,8},{8,0},{16,24},{24,16},{1,9},{9,1},{17,25},{25,17},{2,10},{10... | collective-permute-start | bytes 1179656 | tf_op jit(solution)/shard_map/ppermute | solution.py:90
  34.0 38.9 %collective-permute-start.6 = (bf16[128,1536]{1,0:T(8,128)(2,1)S(1)}, bf16[128,1536]{1,0:T(8,128)(2,1)}, u32[]{:S(2)}, u32[]{:S(2)}) collective-permute-start(bf16[128,1536]{1,0:T(8,128)(2,1)S(1)} %get-tuple-element.256), channel_id=1, source_target_pairs={{0,16},{8,24},{16,0},{24,8},{1,17},{9,25},{17,1},{25,9},{2,18},{10... | collective-permute-start | bytes 1179656 | tf_op jit(solution)/shard_map/ppermute | solution.py:90
  37.0 35.9 %collective-permute-start.7 = (bf16[128,1536]{1,0:T(8,128)(2,1)S(1)}, bf16[128,1536]{1,0:T(8,128)(2,1)}, u32[]{:S(2)}, u32[]{:S(2)}) collective-permute-start(bf16[128,1536]{1,0:T(8,128)(2,1)S(1)} %get-tuple-element.256), channel_id=1, source_target_pairs={{0,24},{8,16},{16,8},{24,0},{1,25},{9,17},{17,9},{25,1},{2,26},{10... | collective-permute-start | bytes 1179656 | tf_op jit(solution)/shard_map/ppermute | solution.py:90
  59.6 14.6 %collective-permute-start.16 = (bf16[192,384]{1,0:T(8,128)(2,1)}, bf16[192,384]{1,0:T(8,128)(2,1)}, u32[]{:S(2)}, u32[]{:S(2)}) collective-permute-start(bf16[192,384]{1,0:T(8,128)(2,1)} %slice.304), channel_id=1, source_target_pairs={{0,1},{1,2},{2,3},{3,0},{4,5},{5,6},{6,7},{7,4},{8,9},{9,10},{10,1... | collective-permute-start | bytes 442376 | tf_op jit(solution)/shard_map/ppermute | solution.py:140
  90.4 24.4 %collective-permute-start.25 = (bf16[128,1536]{1,0:T(8,128)(2,1)S(1)}, bf16[128,1536]{1,0:T(8,128)(2,1)}, u32[]{:S(2)}, u32[]{:S(2)}) collective-permute-start(bf16[128,1536]{1,0:T(8,128)(2,1)S(1)} %get-tuple-element.109), channel_id=1, source_target_pairs={{0,8},{8,0},{16,24},{24,16},{1,9},{9,1},{17,25},{25,17},{2,10},{10... | collective-permute-start | bytes 1179656 | tf_op jit(solution)/shard_map/ppermute | solution.py:90
  92.0 22.8 %collective-permute-start.26 = (bf16[128,1536]{1,0:T(8,128)(2,1)S(1)}, bf16[128,1536]{1,0:T(8,128)(2,1)}, u32[]{:S(2)}, u32[]{:S(2)}) collective-permute-start(bf16[128,1536]{1,0:T(8,128)(2,1)S(1)} %get-tuple-element.109), channel_id=1, source_target_pairs={{0,16},{8,24},{16,0},{24,8},{1,17},{9,25},{17,1},{25,9},{2,18},{10... | collective-permute-start | bytes 1179656 | tf_op jit(solution)/shard_map/ppermute | solution.py:90
  93.1 21.7 %collective-permute-start.27 = (bf16[128,1536]{1,0:T(8,128)(2,1)S(1)}, bf16[128,1536]{1,0:T(8,128)(2,1)}, u32[]{:S(2)}, u32[]{:S(2)}) collective-permute-start(bf16[128,1536]{1,0:T(8,128)(2,1)S(1)} %get-tuple-element.109), channel_id=1, source_target_pairs={{0,24},{8,16},{16,8},{24,0},{1,25},{9,17},{17,9},{25,1},{2,26},{10... | collective-permute-start | bytes 1179656 | tf_op jit(solution)/shard_map/ppermute | solution.py:90
  101.4 14.9 %collective-permute-start.28 = (bf16[192,1536]{1,0:T(8,128)(2,1)}, bf16[192,1536]{1,0:T(8,128)(2,1)}, u32[]{:S(2)}, u32[]{:S(2)}) collective-permute-start(bf16[192,1536]{1,0:T(8,128)(2,1)} %bitcast.87), channel_id=1, source_target_pairs={{0,4},{4,0},{1,5},{5,1},{2,6},{6,2},{3,7},{7,3},{8,12},{12,8},{9,1... | collective-permute-start | bytes 1769480 | tf_op jit(solution)/shard_map/ppermute | solution.py:87
  106.5 21.9 %collective-permute-start.29 = (bf16[384,1024]{1,0:T(8,128)(2,1)S(1)}, bf16[384,1024]{1,0:T(8,128)(2,1)S(1)}, u32[]{:S(2)}, u32[]{:S(2)}) collective-permute-start(bf16[384,1024]{1,0:T(8,128)(2,1)S(1)} %bitcast.370), channel_id=1, source_target_pairs={{0,1},{1,2},{2,3},{3,0},{4,5},{5,6},{6,7},{7,4},{8,9},{9,10},{10,1... | collective-permute-start | bytes 2359304 | tf_op jit(solution)/shard_map/ppermute | solution.py:140
  128.4 23.3 %collective-permute-start.33 = (bf16[512,1536]{1,0:T(8,128)(2,1)S(1)}, bf16[512,1536]{1,0:T(8,128)(2,1)S(1)}, u32[]{:S(2)}, u32[]{:S(2)}) collective-permute-start(bf16[512,1536]{1,0:T(8,128)(2,1)S(1)} %pad_maximum_fusion.4), channel_id=1, source_target_pairs={{0,4},{4,0},{1,5},{5,1},{2,6},{6,2},{3,7},{7,3},{8,12},{12,8},{9,1... | collective-permute-start | bytes 4718600 | tf_op jit(solution)/shard_map/ppermute | solution.py:87
  131.2 19.7 %collective-permute-start.31 = (bf16[128,1536]{1,0:T(8,128)(2,1)S(1)}, bf16[128,1536]{1,0:T(8,128)(2,1)S(1)}, u32[]{:S(2)}, u32[]{:S(2)}) collective-permute-start(bf16[128,1536]{1,0:T(8,128)(2,1)S(1)} %get-tuple-element.234), channel_id=1, source_target_pairs={{0,16},{8,24},{16,0},{24,8},{1,17},{9,25},{17,1},{25,9},{2,18},{10... | collective-permute-start | bytes 1179656 | tf_op jit(solution)/shard_map/ppermute | solution.py:90
  132.3 18.6 %collective-permute-start.32 = (bf16[128,1536]{1,0:T(8,128)(2,1)S(1)}, bf16[128,1536]{1,0:T(8,128)(2,1)S(1)}, u32[]{:S(2)}, u32[]{:S(2)}) collective-permute-start(bf16[128,1536]{1,0:T(8,128)(2,1)S(1)} %get-tuple-element.233), channel_id=1, source_target_pairs={{0,24},{8,16},{16,8},{24,0},{1,25},{9,17},{17,9},{25,1},{2,26},{10... | collective-permute-start | bytes 1179656 | tf_op jit(solution)/shard_map/ppermute | solution.py:90
  133.1 27.6 %collective-permute-start.34 = (bf16[384,1024]{1,0:T(8,128)(2,1)S(1)}, bf16[384,1024]{1,0:T(8,128)(2,1)}, u32[]{:S(2)}, u32[]{:S(2)}) collective-permute-start(bf16[384,1024]{1,0:T(8,128)(2,1)S(1)} %bitcast.371), channel_id=1, source_target_pairs={{0,3},{1,0},{2,1},{3,2},{4,7},{5,4},{6,5},{7,6},{8,11},{9,8},{10,9... | collective-permute-start | bytes 2359304 | tf_op jit(solution)/shard_map/ppermute | solution.py:140
  141.6 19.1 %collective-permute-start.35 = (bf16[384,512]{1,0:T(8,128)(2,1)}, bf16[384,512]{1,0:T(8,128)(2,1)}, u32[]{:S(2)}, u32[]{:S(2)}) collective-permute-start(bf16[384,512]{1,0:T(8,128)(2,1)} %slice.320), channel_id=1, source_target_pairs={{0,1},{1,2},{2,3},{3,0},{4,5},{5,6},{6,7},{7,4},{8,9},{9,10},{10,1... | collective-permute-start | bytes 1179656 | tf_op jit(solution)/shard_map/ppermute | solution.py:140
  162.7 18.1 %collective-permute-start.37 = (bf16[128,1536]{1,0:T(8,128)(2,1)S(1)}, bf16[128,1536]{1,0:T(8,128)(2,1)S(1)}, u32[]{:S(2)}, u32[]{:S(2)}) collective-permute-start(bf16[128,1536]{1,0:T(8,128)(2,1)S(1)} %get-tuple-element.199), channel_id=1, source_target_pairs={{0,16},{8,24},{16,0},{24,8},{1,17},{9,25},{17,1},{25,9},{2,18},{10... | collective-permute-start | bytes 1179656 | tf_op jit(solution)/shard_map/ppermute | solution.py:90
  163.8 17.0 %collective-permute-start.38 = (bf16[128,1536]{1,0:T(8,128)(2,1)S(1)}, bf16[128,1536]{1,0:T(8,128)(2,1)S(1)}, u32[]{:S(2)}, u32[]{:S(2)}) collective-permute-start(bf16[128,1536]{1,0:T(8,128)(2,1)S(1)} %get-tuple-element.199), channel_id=1, source_target_pairs={{0,24},{8,16},{16,8},{24,0},{1,25},{9,17},{17,9},{25,1},{2,26},{10... | collective-permute-start | bytes 1179656 | tf_op jit(solution)/shard_map/ppermute | solution.py:90
  180.9 15.1 %collective-permute-start.39 = (bf16[512,1536]{1,0:T(8,128)(2,1)S(1)}, bf16[512,1536]{1,0:T(8,128)(2,1)S(1)}, u32[]{:S(2)}, u32[]{:S(2)}) collective-permute-start(bf16[512,1536]{1,0:T(8,128)(2,1)S(1)} %pad_maximum_fusion.5), channel_id=1, source_target_pairs={{0,4},{4,0},{1,5},{5,1},{2,6},{6,2},{3,7},{7,3},{8,12},{12,8},{9,1... | collective-permute-start | bytes 4718600 | tf_op jit(solution)/shard_map/ppermute | solution.py:87
  182.0 13.9 %collective-permute-start.40 = (bf16[384,512]{1,0:T(8,128)(2,1)S(1)}, bf16[384,512]{1,0:T(8,128)(2,1)S(1)}, u32[]{:S(2)}, u32[]{:S(2)}) collective-permute-start(bf16[384,512]{1,0:T(8,128)(2,1)S(1)} %slice.321), channel_id=1, source_target_pairs={{0,3},{1,0},{2,1},{3,2},{4,7},{5,4},{6,5},{7,6},{8,11},{9,8},{10,9... | collective-permute-start | bytes 1179656 | tf_op jit(solution)/shard_map/ppermute | solution.py:140
  226.8 22.7 %collective-permute-start.45 = (bf16[8,1,48,512]{3,2,1,0:T(8,128)(2,1)S(1)}, bf16[8,1,48,512]{3,2,1,0:T(8,128)(2,1)S(1)}, u32[]{:S(2)}, u32[]{:S(2)}) collective-permute-start(bf16[8,1,48,512]{3,2,1,0:T(8,128)(2,1)S(1)} %get-tuple-element.210), channel_id=1, source_target_pairs={{0,1},{1,2},{2,3},{3,0},{4,5},{5,6},{6,7},{7,4},{8,9},{9,10},{10,1... | collective-permute-start | bytes 1179656 | tf_op jit(solution)/shard_map/ppermute | solution.py:140
  227.1 38.0 %collective-permute-start.46 = (bf16[8,1,48,512]{3,2,1,0:T(8,128)(2,1)S(1)}, bf16[8,1,48,512]{3,2,1,0:T(8,128)(2,1)S(1)}, u32[]{:S(2)}, u32[]{:S(2)}) collective-permute-start(bf16[8,1,48,512]{3,2,1,0:T(8,128)(2,1)S(1)} %get-tuple-element.209), channel_id=1, source_target_pairs={{0,3},{1,0},{2,1},{3,2},{4,7},{5,4},{6,5},{7,6},{8,11},{9,8},{10,9... | collective-permute-start | bytes 1179656 | tf_op jit(solution)/shard_map/ppermute | solution.py:140
  231.4 33.8 %collective-permute-start.42 = (bf16[128,1536]{1,0:T(8,128)(2,1)S(1)}, bf16[128,1536]{1,0:T(8,128)(2,1)S(1)}, u32[]{:S(2)}, u32[]{:S(2)}) collective-permute-start(bf16[128,1536]{1,0:T(8,128)(2,1)S(1)} %get-tuple-element.229), channel_id=1, source_target_pairs={{0,8},{8,0},{16,24},{24,16},{1,9},{9,1},{17,25},{25,17},{2,10},{10... | collective-permute-start | bytes 1179656 | tf_op jit(solution)/shard_map/ppermute | solution.py:90
  232.3 33.0 %collective-permute-start.43 = (bf16[128,1536]{1,0:T(8,128)(2,1)S(1)}, bf16[128,1536]{1,0:T(8,128)(2,1)S(1)}, u32[]{:S(2)}, u32[]{:S(2)}) collective-permute-start(bf16[128,1536]{1,0:T(8,128)(2,1)S(1)} %get-tuple-element.231), channel_id=1, source_target_pairs={{0,16},{8,24},{16,0},{24,8},{1,17},{9,25},{17,1},{25,9},{2,18},{10... | collective-permute-start | bytes 1179656 | tf_op jit(solution)/shard_map/ppermute | solution.py:90
  233.5 31.7 %collective-permute-start.44 = (bf16[128,1536]{1,0:T(8,128)(2,1)S(1)}, bf16[128,1536]{1,0:T(8,128)(2,1)S(1)}, u32[]{:S(2)}, u32[]{:S(2)}) collective-permute-start(bf16[128,1536]{1,0:T(8,128)(2,1)S(1)} %get-tuple-element.230), channel_id=1, source_target_pairs={{0,24},{8,16},{16,8},{24,0},{1,25},{9,17},{17,9},{25,1},{2,26},{10... | collective-permute-start | bytes 1179656 | tf_op jit(solution)/shard_map/ppermute | solution.py:90
  249.5 22.7 %collective-permute-start.50 = (bf16[512,1536]{1,0:T(8,128)(2,1)S(1)}, bf16[512,1536]{1,0:T(8,128)(2,1)S(1)}, u32[]{:S(2)}, u32[]{:S(2)}) collective-permute-start(bf16[512,1536]{1,0:T(8,128)(2,1)S(1)} %convolution_convert_fusion.2), channel_id=1, source_target_pairs={{0,4},{4,0},{1,5},{5,1},{2,6},{6,2},{3,7},{7,3},{8,12},{12,8},{9,1... | collective-permute-start | bytes 4718600 | tf_op jit(solution)/shard_map/ppermute | solution.py:87
  266.6 24.5 %collective-permute-start.47 = (bf16[128,1536]{1,0:T(8,128)(2,1)S(1)}, bf16[128,1536]{1,0:T(8,128)(2,1)S(1)}, u32[]{:S(2)}, u32[]{:S(2)}) collective-permute-start(bf16[128,1536]{1,0:T(8,128)(2,1)S(1)} %fusion.75), channel_id=1, source_target_pairs={{0,8},{8,0},{16,24},{24,16},{1,9},{9,1},{17,25},{25,17},{2,10},{10... | collective-permute-start | bytes 1179656 | tf_op jit(solution)/shard_map/ppermute | solution.py:90
  267.0 24.0 %collective-permute-start.48 = (bf16[128,1536]{1,0:T(8,128)(2,1)S(1)}, bf16[128,1536]{1,0:T(8,128)(2,1)S(1)}, u32[]{:S(2)}, u32[]{:S(2)}) collective-permute-start(bf16[128,1536]{1,0:T(8,128)(2,1)S(1)} %fusion.75), channel_id=1, source_target_pairs={{0,16},{8,24},{16,0},{24,8},{1,17},{9,25},{17,1},{25,9},{2,18},{10... | collective-permute-start | bytes 1179656 | tf_op jit(solution)/shard_map/ppermute | solution.py:90
  268.3 22.7 %collective-permute-start.49 = (bf16[128,1536]{1,0:T(8,128)(2,1)S(1)}, bf16[128,1536]{1,0:T(8,128)(2,1)S(1)}, u32[]{:S(2)}, u32[]{:S(2)}) collective-permute-start(bf16[128,1536]{1,0:T(8,128)(2,1)S(1)} %fusion.75), channel_id=1, source_target_pairs={{0,24},{8,16},{16,8},{24,0},{1,25},{9,17},{17,9},{25,1},{2,26},{10... | collective-permute-start | bytes 1179656 | tf_op jit(solution)/shard_map/ppermute | solution.py:90
  270.1 13.8 %collective-permute-start.51 = (bf16[8,1,48,512]{3,2,1,0:T(8,128)(2,1)S(1)}, bf16[8,1,48,512]{3,2,1,0:T(8,128)(2,1)S(1)}, u32[]{:S(2)}, u32[]{:S(2)}) collective-permute-start(bf16[8,1,48,512]{3,2,1,0:T(8,128)(2,1)S(1)} %get-tuple-element.132), channel_id=1, source_target_pairs={{0,1},{1,2},{2,3},{3,0},{4,5},{5,6},{6,7},{7,4},{8,9},{9,10},{10,1... | collective-permute-start | bytes 1179656 | tf_op jit(solution)/shard_map/ppermute | solution.py:140
  272.1 18.0 %collective-permute-start.52 = (bf16[8,1,48,512]{3,2,1,0:T(8,128)(2,1)S(1)}, bf16[8,1,48,512]{3,2,1,0:T(8,128)(2,1)S(1)}, u32[]{:S(2)}, u32[]{:S(2)}) collective-permute-start(bf16[8,1,48,512]{3,2,1,0:T(8,128)(2,1)S(1)} %get-tuple-element.133), channel_id=1, source_target_pairs={{0,3},{1,0},{2,1},{3,2},{4,7},{5,4},{6,5},{7,6},{8,11},{9,8},{10,9... | collective-permute-start | bytes 1179656 | tf_op jit(solution)/shard_map/ppermute | solution.py:140
  301.7 13.8 %collective-permute-start.54 = (bf16[8,1,48,512]{3,2,1,0:T(8,128)(2,1)S(1)}, bf16[8,1,48,512]{3,2,1,0:T(8,128)(2,1)S(1)}, u32[]{:S(2)}, u32[]{:S(2)}) collective-permute-start(bf16[8,1,48,512]{3,2,1,0:T(8,128)(2,1)S(1)} %copy-done.34), channel_id=1, source_target_pairs={{0,1},{1,2},{2,3},{3,0},{4,5},{5,6},{6,7},{7,4},{8,9},{9,10},{10,1... | collective-permute-start | bytes 1179656 | tf_op jit(solution)/shard_map/ppermute | solution.py:140
  302.2 19.3 %collective-permute-start.55 = (bf16[8,1,48,512]{3,2,1,0:T(8,128)(2,1)S(1)}, bf16[8,1,48,512]{3,2,1,0:T(8,128)(2,1)S(1)}, u32[]{:S(2)}, u32[]{:S(2)}) collective-permute-start(bf16[8,1,48,512]{3,2,1,0:T(8,128)(2,1)S(1)} %get-tuple-element.136), channel_id=1, source_target_pairs={{0,3},{1,0},{2,1},{3,2},{4,7},{5,4},{6,5},{7,6},{8,11},{9,8},{10,9... | collective-permute-start | bytes 1179656 | tf_op jit(solution)/shard_map/ppermute | solution.py:140
  305.7 17.1 %collective-permute-start.53 = (bf16[192,1536]{1,0:T(8,128)(2,1)S(1)}, bf16[192,1536]{1,0:T(8,128)(2,1)S(1)}, u32[]{:S(2)}, u32[]{:S(2)}) collective-permute-start(bf16[192,1536]{1,0:T(8,128)(2,1)S(1)} %dynamic-slice_bitcast_fusion), channel_id=1, source_target_pairs={{0,4},{4,0},{1,5},{5,1},{2,6},{6,2},{3,7},{7,3},{8,12},{12,8},{9,1... | collective-permute-start | bytes 1769480 | tf_op jit(solution)/shard_map/ppermute | solution.py:87
  329.8 12.1 %collective-permute-start.61 = (bf16[1,1,288,384]{3,2,1,0:T(8,128)(2,1)S(1)}, bf16[1,1,288,384]{3,2,1,0:T(8,128)(2,1)S(1)}, u32[]{:S(2)}, u32[]{:S(2)}) collective-permute-start(bf16[1,1,288,384]{3,2,1,0:T(8,128)(2,1)S(1)} %get-tuple-element.221), channel_id=1, source_target_pairs={{0,3},{1,0},{2,1},{3,2},{4,7},{5,4},{6,5},{7,6},{8,11},{9,8},{10,9... | collective-permute-start | bytes 663560 | tf_op jit(solution)/shard_map/ppermute | solution.py:140
  333.6 12.1 %collective-permute-start.57 = (bf16[128,1536]{1,0:T(8,128)(2,1)S(1)}, bf16[128,1536]{1,0:T(8,128)(2,1)S(1)}, u32[]{:S(2)}, u32[]{:S(2)}) collective-permute-start(bf16[128,1536]{1,0:T(8,128)(2,1)S(1)} %get-tuple-element.226), channel_id=1, source_target_pairs={{0,8},{8,0},{16,24},{24,16},{1,9},{9,1},{17,25},{25,17},{2,10},{10... | collective-permute-start | bytes 1179656 | tf_op jit(solution)/shard_map/ppermute | solution.py:90
  334.4 19.6 %collective-permute-start.58 = (bf16[128,1536]{1,0:T(8,128)(2,1)S(1)}, bf16[128,1536]{1,0:T(8,128)(2,1)S(1)}, u32[]{:S(2)}, u32[]{:S(2)}) collective-permute-start(bf16[128,1536]{1,0:T(8,128)(2,1)S(1)} %get-tuple-element.228), channel_id=1, source_target_pairs={{0,16},{8,24},{16,0},{24,8},{1,17},{9,25},{17,1},{25,9},{2,18},{10... | collective-permute-start | bytes 1179656 | tf_op jit(solution)/shard_map/ppermute | solution.py:90
  335.9 18.6 %collective-permute-start.59 = (bf16[128,1536]{1,0:T(8,128)(2,1)S(1)}, bf16[128,1536]{1,0:T(8,128)(2,1)S(1)}, u32[]{:S(2)}, u32[]{:S(2)}) collective-permute-start(bf16[128,1536]{1,0:T(8,128)(2,1)S(1)} %get-tuple-element.227), channel_id=1, source_target_pairs={{0,24},{8,16},{16,8},{24,0},{1,25},{9,17},{17,9},{25,1},{2,26},{10... | collective-permute-start | bytes 1179656 | tf_op jit(solution)/shard_map/ppermute | solution.py:90
  339.6 18.7 %collective-permute-start.70 = (bf16[2,48,1024]{2,1,0:T(8,128)(2,1)S(1)}, bf16[2,48,1024]{2,1,0:T(8,128)(2,1)S(1)}, u32[]{:S(2)}, u32[]{:S(2)}) collective-permute-start(bf16[2,48,1024]{2,1,0:T(8,128)(2,1)S(1)} %get-tuple-element.252), channel_id=1, source_target_pairs={{0,8},{8,0},{16,24},{24,16},{1,9},{9,1},{17,25},{25,17},{2,10},{10... | collective-permute-start | bytes 589832 | tf_op jit(solution)/shard_map/ppermute | solution.py:90
  341.9 19.3 %collective-permute-start.71 = (bf16[2,48,1024]{2,1,0:T(8,128)(2,1)S(1)}, bf16[2,48,1024]{2,1,0:T(8,128)(2,1)S(1)}, u32[]{:S(2)}, u32[]{:S(2)}) collective-permute-start(bf16[2,48,1024]{2,1,0:T(8,128)(2,1)S(1)} %get-tuple-element.253), channel_id=1, source_target_pairs={{0,16},{8,24},{16,0},{24,8},{1,17},{9,25},{17,1},{25,9},{2,18},{10... | collective-permute-start | bytes 589832 | tf_op jit(solution)/shard_map/ppermute | solution.py:90
  345.7 15.6 %collective-permute-start.72 = (bf16[2,48,1024]{2,1,0:T(8,128)(2,1)S(1)}, bf16[2,48,1024]{2,1,0:T(8,128)(2,1)S(1)}, u32[]{:S(2)}, u32[]{:S(2)}) collective-permute-start(bf16[2,48,1024]{2,1,0:T(8,128)(2,1)S(1)} %get-tuple-element.254), channel_id=1, source_target_pairs={{0,24},{8,16},{16,8},{24,0},{1,25},{9,17},{17,9},{25,1},{2,26},{10... | collective-permute-start | bytes 589832 | tf_op jit(solution)/shard_map/ppermute | solution.py:90
  366.9 13.5 %collective-permute-start.66 = (bf16[1,1,288,384]{3,2,1,0:T(8,128)(2,1)S(1)}, bf16[1,1,288,384]{3,2,1,0:T(8,128)(2,1)S(1)}, u32[]{:S(2)}, u32[]{:S(2)}) collective-permute-start(bf16[1,1,288,384]{3,2,1,0:T(8,128)(2,1)S(1)} %get-tuple-element.144), channel_id=1, source_target_pairs={{0,3},{1,0},{2,1},{3,2},{4,7},{5,4},{6,5},{7,6},{8,11},{9,8},{10,9... | collective-permute-start | bytes 663560 | tf_op jit(solution)/shard_map/ppermute | solution.py:140
  371.9 15.9 %collective-permute-start.63 = (bf16[128,1536]{1,0:T(8,128)(2,1)S(1)}, bf16[128,1536]{1,0:T(8,128)(2,1)S(1)}, u32[]{:S(2)}, u32[]{:S(2)}) collective-permute-start(bf16[128,1536]{1,0:T(8,128)(2,1)S(1)} %get-tuple-element.225), channel_id=1, source_target_pairs={{0,16},{8,24},{16,0},{24,8},{1,17},{9,25},{17,1},{25,9},{2,18},{10... | collective-permute-start | bytes 1179656 | tf_op jit(solution)/shard_map/ppermute | solution.py:90
  378.1 15.7 %collective-permute-start.77 = (f32[2,1536]{1,0:T(2,128)}, f32[2,1536]{1,0:T(2,128)}, u32[]{:S(2)}, u32[]{:S(2)}) collective-permute-start(f32[2,1536]{1,0:T(2,128)} %add.556), channel_id=1, source_target_pairs={{0,2},{1,3},{2,0},{3,1},{4,6},{5,7},{6,4},{7,5},{8,10},{9,11},{10,... | collective-permute-start | bytes 36872 | tf_op jit(solution)/shard_map/ppermute | solution.py:214
  (96 other events, 809.4 us)
Sparse Core Ops, SparseCore 0:
  20.0 52.0 all-gather.1
  215.7 53.3 reduce-scatter.1
